TPU v7x, 32 devices: a whole 2x2x4 slice. The times are simulated.
32 devices in a mesh: layer: 8 (over z, x), row: 4 (over y, core).
Axes of the slice: x: 2, y: 2, z: 4, core: 2. Of those that a mesh axis runs over, the one named last changes fastest.
Arguments:
- right_side: float32 [8, 1024, 256], P('layer', 'row'), may hold values from -6 to 6
- reduce_factors: float32 [3, 8, 2, 1024, 1024], P(None, 'layer', None, 'row'), may hold values from -0.1875 to 0.1875
- solve_factors: float32 [8, 3, 1024, 1024], P('layer', None, 'row'), may hold values from -0.1875 to 0.1875
Outputs:
- solution: float32 [8, 1024, 256], P('layer', 'row')
All inputs are finite; a program needn't handle non-finite values.
Results may differ from a plain program's by a relative error of at most 0.00016.
Values sent between devices are 32-bit elements; how exact they have to be, the bound alone decides.
No kernel may reach another device: no remote copies, remote signals or barrier semaphores. Data moves between devices by JAX's collectives and lax.ppermute only.
A program may use at most 64 MiB of HBM per device.

v0:
```python
import jax
import jax.numpy as jnp
from jax import lax
from jax.sharding import PartitionSpec as P


def from_behind(shard, axis, by):
    devices = lax.axis_size(axis)
    pairs = [(i, i + by) for i in range(devices) if 0 <= i + by < devices]
    return lax.ppermute(shard, axis, pairs)


def product_of(left, right):
    return jnp.dot(left, right, precision=lax.Precision.HIGHEST, preferred_element_type=jnp.float32)


def neighbour_terms(vectors, left_mats, right_mats, stride):
    whole = lax.all_gather(vectors, "row", axis=1, tiled=True)
    lower = from_behind(whole, "layer", stride)
    upper = from_behind(whole, "layer", -stride)
    return (product_of(left_mats[0], lower[0]) + product_of(right_mats[0], upper[0]))[None]


def on_device(right_side, reduce_factors, solve_factors):
    layer_index = lax.axis_index("layer")
    level_count = reduce_factors.shape[0]
    current = right_side
    saved = right_side
    for level_index in range(level_count):
        stride = 1 << level_index
        terms = neighbour_terms(
            current, reduce_factors[level_index, :, 0], reduce_factors[level_index, :, 1], stride
        )
        saved = jnp.where(layer_index % (2 * stride) == stride, current, saved)
        current = jnp.where(layer_index % (2 * stride) == 0, current - terms, current)
    saved = jnp.where(layer_index == 0, current, saved)
    own_inverse = solve_factors[0, 0]
    base = product_of(own_inverse, lax.all_gather(saved, "row", axis=1, tiled=True)[0])[None]
    solution = jnp.where(layer_index == 0, base, jnp.zeros_like(base))
    for level_index in reversed(range(level_count)):
        stride = 1 << level_index
        terms = neighbour_terms(solution, solve_factors[:, 1], solve_factors[:, 2], stride)
        solution = jnp.where(layer_index % (2 * stride) == stride, base - terms, solution)
    return solution


def solution(mesh):
    placed = (
        P("layer", "row", None),
        P(None, "layer", None, "row", None),
        P("layer", None, "row", None),
    )
    return jax.shard_map(
        on_device, mesh=mesh, in_specs=placed, out_specs=P("layer", "row", None), check_vma=False
    )
```

profile of v0, /device:TPU:8, one launch (start us, length us, event | category | flops | bytes accessed | tf_op | source)
XLA Modules:
  0.0 427.2 jit_solution(3660228800837578581)
XLA Ops:
  6.5 0.7 all-gather.11.cloned.1.call-update
  7.3 19.5 %all-gather.11.cloned.1.call-done = f32[1,1024,256]{2,1,0:T(8,128)} async-done(((f32[1,256,256]{2,1,0:T(8,128)}), f32[1,1024,256]{2,1,0:T(8,128)}) %all-gather.11.cloned.1.call-update) | async-done | bytes 1048592 | tf_op jit(solution)/shard_map/all_gather | solution.py:18
  26.8 3.3 collective-permute-start.1
  30.2 2.5 collective-permute-start
  32.7 44.0 %collective-permute-done.1 = f32[1,1024,256]{2,1,0:T(8,128)S(1)} collective-permute-done((f32[1,1024,256]{2,1,0:T(8,128)}, f32[1,1024,256]{2,1,0:T(8,128)S(1)}, u32[]{:S(2)}, u32[]{:S(2)}) %collective-permute-start.1) | collective-permute-done | bytes 1048608 | tf_op jit(solution)/shard_map/ppermute | solution.py:10
  76.7 2.2 fusion.48
  79.0 3.0 fusion.14
  82.0 0.0 all-gather.15.cloned.1.call-start
  82.0 15.9 %all-gather.13.cloned.1.call-done = f32[1,1024,256]{2,1,0:T(8,128)} async-done(((f32[1,256,256]{2,1,0:T(8,128)}), f32[1,1024,256]{2,1,0:T(8,128)}) %all-gather.13.cloned.1.call-update) | async-done | bytes 1048592 | tf_op jit(solution)/shard_map/all_gather | solution.py:18
  98.0 2.4 collective-permute-start.3
  100.4 3.4 collective-permute-start.2
  103.8 21.5 %collective-permute-done.3 = f32[1,1024,256]{2,1,0:T(8,128)S(1)} collective-permute-done((f32[1,1024,256]{2,1,0:T(8,128)}, f32[1,1024,256]{2,1,0:T(8,128)S(1)}, u32[]{:S(2)}, u32[]{:S(2)}) %collective-permute-start.3) | collective-permute-done | bytes 1048608 | tf_op jit(solution)/shard_map/ppermute | solution.py:10
  125.4 2.3 fusion.43
  127.7 3.1 fusion.16
  130.8 0.0 all-gather.17.cloned.1.call-start
  130.8 16.7 %all-gather.15.cloned.1.call-done = f32[1,1024,256]{2,1,0:T(8,128)} async-done(((f32[1,256,256]{2,1,0:T(8,128)}), f32[1,1024,256]{2,1,0:T(8,128)}) %all-gather.15.cloned.1.call-update) | async-done | bytes 1048592 | tf_op jit(solution)/shard_map/all_gather | solution.py:18
  147.5 1.3 collective-permute-start.5
  148.8 7.4 %collective-permute-start.4 = (f32[1,1024,256]{2,1,0:T(8,128)}, f32[1,1024,256]{2,1,0:T(8,128)}, u32[]{:S(2)}, u32[]{:S(2)}) collective-permute-start(f32[1,1024,256]{2,1,0:T(8,128)} %all-gather.15.cloned.1.call-done), channel_id=1, source_target_pairs={{0,16},{4,20},{8,24},{12,28},{1,17},{5,21},{9,25},{13,29},{2,18},{... | collective-permute-start | bytes 3145736 | tf_op jit(solution)/shard_map/ppermute | solution.py:10
  156.2 19.8 %collective-permute-done.5 = f32[1,1024,256]{2,1,0:T(8,128)} collective-permute-done((f32[1,1024,256]{2,1,0:T(8,128)}, f32[1,1024,256]{2,1,0:T(8,128)}, u32[]{:S(2)}, u32[]{:S(2)}) %collective-permute-start.5) | collective-permute-done | bytes 1048608 | tf_op jit(solution)/shard_map/ppermute | solution.py:10
  176.0 2.6 fusion.38
  178.6 21.9 %collective-permute-done.4 = f32[1,1024,256]{2,1,0:T(8,128)} collective-permute-done((f32[1,1024,256]{2,1,0:T(8,128)}, f32[1,1024,256]{2,1,0:T(8,128)}, u32[]{:S(2)}, u32[]{:S(2)}) %collective-permute-start.4) | collective-permute-done | bytes 1048608 | tf_op jit(solution)/shard_map/ppermute | solution.py:10
  200.5 3.4 fusion.19
  203.9 0.0 all-gather.19.cloned.1.call-start
  204.0 17.9 %all-gather.17.cloned.1.call-done = f32[1,1024,256]{2,1,0:T(8,128)} async-done(((f32[1,256,256]{2,1,0:T(8,128)}), f32[1,1024,256]{2,1,0:T(8,128)}) %all-gather.17.cloned.1.call-update) | async-done | bytes 1048592 | tf_op jit(solution)/shard_map/all_gather | solution.py:38
  221.9 3.0 fusion.35
  224.9 0.7 select_bitcast_fusion
  225.7 16.8 %all-gather.19.cloned.1.call-done = f32[1024,256]{0,1:T(8,128)} async-done(((f32[256,256]{0,1:T(8,128)}), f32[1024,256]{0,1:T(8,128)}) %all-gather.19.cloned.1.call-update) | async-done | bytes 1048592 | tf_op jit(solution)/shard_map/all_gather | solution.py:18
  242.5 1.3 collective-permute-start.7
  243.8 5.6 %collective-permute-start.6 = (f32[1,1024,256]{1,2,0:T(8,128)}, f32[1,1024,256]{1,2,0:T(8,128)S(1)}, u32[]{:S(2)}, u32[]{:S(2)}) collective-permute-start(f32[1,1024,256]{1,2,0:T(8,128)} %bitcast.122), channel_id=1, source_target_pairs={{0,16},{4,20},{8,24},{12,28},{1,17},{5,21},{9,25},{13,29},{2,18},{... | collective-permute-start | bytes 3145736 | tf_op jit(solution)/shard_map/ppermute | solution.py:10
  249.4 21.5 %collective-permute-done.7 = f32[1,1024,256]{1,2,0:T(8,128)S(1)} collective-permute-done((f32[1,1024,256]{1,2,0:T(8,128)}, f32[1,1024,256]{1,2,0:T(8,128)S(1)}, u32[]{:S(2)}, u32[]{:S(2)}) %collective-permute-start.7) | collective-permute-done | bytes 1048608 | tf_op jit(solution)/shard_map/ppermute | solution.py:10
  270.9 1.0 fusion.28
  272.0 22.7 %collective-permute-done.6 = f32[1,1024,256]{1,2,0:T(8,128)S(1)} collective-permute-done((f32[1,1024,256]{1,2,0:T(8,128)}, f32[1,1024,256]{1,2,0:T(8,128)S(1)}, u32[]{:S(2)}, u32[]{:S(2)}) %collective-permute-start.6) | collective-permute-done | bytes 1048608 | tf_op jit(solution)/shard_map/ppermute | solution.py:10
  294.6 1.7 fusion.9
  296.4 0.2 all-gather.23.cloned.1.call-start
  296.6 17.5 %all-gather.21.cloned.1.call-done = f32[1024,256]{0,1:T(8,128)} async-done(((f32[256,256]{0,1:T(8,128)}), f32[1024,256]{0,1:T(8,128)}) %all-gather.21.cloned.1.call-update) | async-done | bytes 1048592 | tf_op jit(solution)/shard_map/all_gather | solution.py:18
  314.1 2.4 collective-permute-start.9
  316.6 3.4 collective-permute-start.8
  320.0 21.5 %collective-permute-done.9 = f32[1,1024,256]{1,2,0:T(8,128)S(1)} collective-permute-done((f32[1,1024,256]{1,2,0:T(8,128)}, f32[1,1024,256]{1,2,0:T(8,128)S(1)}, u32[]{:S(2)}, u32[]{:S(2)}) %collective-permute-start.9) | collective-permute-done | bytes 1048608 | tf_op jit(solution)/shard_map/ppermute | solution.py:10
  341.5 1.0 fusion.23
  342.6 1.1 collective-permute-done.8
  343.7 1.7 fusion.6
  345.5 17.9 %all-gather.23.cloned.1.call-done = f32[1024,256]{0,1:T(8,128)} async-done(((f32[256,256]{0,1:T(8,128)}), f32[1024,256]{0,1:T(8,128)}) %all-gather.23.cloned.1.call-update) | async-done | bytes 1048592 | tf_op jit(solution)/shard_map/all_gather | solution.py:18
  363.4 3.3 collective-permute-start.11
  366.7 2.5 collective-permute-start.10
  369.2 44.1 %collective-permute-done.11 = f32[1,1024,256]{1,2,0:T(8,128)} collective-permute-done((f32[1,1024,256]{1,2,0:T(8,128)}, f32[1,1024,256]{1,2,0:T(8,128)}, u32[]{:S(2)}, u32[]{:S(2)}) %collective-permute-start.11) | collective-permute-done | bytes 1048608 | tf_op jit(solution)/shard_map/ppermute | solution.py:10
  413.3 2.3 fusion.20
  415.6 3.0 fusion.3
  418.6 1.8 copy.8
  (16 shorter events, 0.2 us)
Async XLA Ops:
  6.5 20.3 %all-gather.11.cloned.1.call-start = ((), (), s32[]{:S(2)}) async-start(), calls=%async_computation | async-start | bytes 1310720 | tf_op jit(solution)/shard_map/all_gather | solution.py:18
  7.3 90.7 %all-gather.13.cloned.1.call-start = ((), (), s32[]{:S(2)}) async-start(), calls=%async_computation.1 | async-start | bytes 1310720 | tf_op jit(solution)/shard_map/all_gather | solution.py:18
  26.8 49.9 %collective-permute-start.1 = (f32[1,1024,256]{2,1,0:T(8,128)}, f32[1,1024,256]{2,1,0:T(8,128)S(1)}, u32[]{:S(2)}, u32[]{:S(2)}) collective-permute-start(f32[1,1024,256]{2,1,0:T(8,128)} %all-gather.11.cloned.1.call-done), channel_id=1, source_target_pairs={{4,0},{8,4},{12,8},{16,12},{20,16},{24,20},{28,24},{5,1},{9,5},{13... | collective-permute-start | bytes 3145736 | tf_op jit(solution)/shard_map/ppermute | solution.py:10
  30.2 48.8 %collective-permute-start = (f32[1,1024,256]{2,1,0:T(8,128)}, f32[1,1024,256]{2,1,0:T(8,128)S(1)}, u32[]{:S(2)}, u32[]{:S(2)}) collective-permute-start(f32[1,1024,256]{2,1,0:T(8,128)} %all-gather.11.cloned.1.call-done), channel_id=1, source_target_pairs={{0,4},{4,8},{8,12},{12,16},{16,20},{20,24},{24,28},{1,5},{5,9},{9,... | collective-permute-start | bytes 3145736 | tf_op jit(solution)/shard_map/ppermute | solution.py:10
  82.0 65.5 %all-gather.15.cloned.1.call-start = ((), (), s32[]{:S(2)}) async-start(), calls=%async_computation.2 | async-start | bytes 1310720 | tf_op jit(solution)/shard_map/all_gather | solution.py:18
  98.0 27.4 %collective-permute-start.3 = (f32[1,1024,256]{2,1,0:T(8,128)}, f32[1,1024,256]{2,1,0:T(8,128)S(1)}, u32[]{:S(2)}, u32[]{:S(2)}) collective-permute-start(f32[1,1024,256]{2,1,0:T(8,128)} %all-gather.13.cloned.1.call-done), channel_id=1, source_target_pairs={{8,0},{12,4},{16,8},{20,12},{24,16},{28,20},{9,1},{13,5},{17,9},{2... | collective-permute-start | bytes 3145736 | tf_op jit(solution)/shard_map/ppermute | solution.py:10
  100.4 27.3 %collective-permute-start.2 = (f32[1,1024,256]{2,1,0:T(8,128)}, f32[1,1024,256]{2,1,0:T(8,128)S(1)}, u32[]{:S(2)}, u32[]{:S(2)}) collective-permute-start(f32[1,1024,256]{2,1,0:T(8,128)} %all-gather.13.cloned.1.call-done), channel_id=1, source_target_pairs={{0,8},{4,12},{8,16},{12,20},{16,24},{20,28},{1,9},{5,13},{9,17},{1... | collective-permute-start | bytes 3145736 | tf_op jit(solution)/shard_map/ppermute | solution.py:10
  127.6 72.9 %copy-start.1 = (f32[1,256,256]{2,1,0:T(8,128)S(1)}, f32[1,256,256]{2,1,0:T(8,128)}, u32[]{:S(2)}) copy-start(f32[1,256,256]{2,1,0:T(8,128)} %fusion.14) | copy-start | bytes 786436
  130.7 91.1 %copy-start = (f32[1,3,256,1024]{3,2,1,0:T(8,128)S(1)}, f32[1,3,256,1024]{3,2,1,0:T(8,128)}, u32[]{:S(2)}) copy-start(f32[1,3,256,1024]{3,2,1,0:T(8,128)} %param.5) | copy-start | bytes 9437188
  130.8 91.1 %all-gather.17.cloned.1.call-start = ((), (), s32[]{:S(2)}) async-start(), calls=%async_computation.3 | async-start | bytes 1310720 | tf_op jit(solution)/shard_map/all_gather | solution.py:38
  147.5 28.5 %collective-permute-start.5 = (f32[1,1024,256]{2,1,0:T(8,128)}, f32[1,1024,256]{2,1,0:T(8,128)}, u32[]{:S(2)}, u32[]{:S(2)}) collective-permute-start(f32[1,1024,256]{2,1,0:T(8,128)} %all-gather.15.cloned.1.call-done), channel_id=1, source_target_pairs={{16,0},{20,4},{24,8},{28,12},{17,1},{21,5},{25,9},{29,13},{18,2},{... | collective-permute-start | bytes 3145736 | tf_op jit(solution)/shard_map/ppermute | solution.py:10
  148.8 51.7 %collective-permute-start.4 = (f32[1,1024,256]{2,1,0:T(8,128)}, f32[1,1024,256]{2,1,0:T(8,128)}, u32[]{:S(2)}, u32[]{:S(2)}) collective-permute-start(f32[1,1024,256]{2,1,0:T(8,128)} %all-gather.15.cloned.1.call-done), channel_id=1, source_target_pairs={{0,16},{4,20},{8,24},{12,28},{1,17},{5,21},{9,25},{13,29},{2,18},{... | collective-permute-start | bytes 3145736 | tf_op jit(solution)/shard_map/ppermute | solution.py:10
  203.9 38.6 %all-gather.19.cloned.1.call-start = ((), (), s32[]{:S(2)}) async-start(), calls=%async_computation.4 | async-start | bytes 1310720 | tf_op jit(solution)/shard_map/all_gather | solution.py:18
  225.7 88.5 %all-gather.21.cloned.1.call-start = ((), (), s32[]{:S(2)}) async-start(), calls=%async_computation.5 | async-start | bytes 1310720 | tf_op jit(solution)/shard_map/all_gather | solution.py:18
  242.5 28.4 %collective-permute-start.7 = (f32[1,1024,256]{1,2,0:T(8,128)}, f32[1,1024,256]{1,2,0:T(8,128)S(1)}, u32[]{:S(2)}, u32[]{:S(2)}) collective-permute-start(f32[1,1024,256]{1,2,0:T(8,128)} %bitcast.121), channel_id=1, source_target_pairs={{16,0},{20,4},{24,8},{28,12},{17,1},{21,5},{25,9},{29,13},{18,2},{... | collective-permute-start | bytes 3145736 | tf_op jit(solution)/shard_map/ppermute | solution.py:10
  243.8 50.8 %collective-permute-start.6 = (f32[1,1024,256]{1,2,0:T(8,128)}, f32[1,1024,256]{1,2,0:T(8,128)S(1)}, u32[]{:S(2)}, u32[]{:S(2)}) collective-permute-start(f32[1,1024,256]{1,2,0:T(8,128)} %bitcast.122), channel_id=1, source_target_pairs={{0,16},{4,20},{8,24},{12,28},{1,17},{5,21},{9,25},{13,29},{2,18},{... | collective-permute-start | bytes 3145736 | tf_op jit(solution)/shard_map/ppermute | solution.py:10
  296.4 67.0 %all-gather.23.cloned.1.call-start = ((), (), s32[]{:S(2)}) async-start(), calls=%async_computation.6 | async-start | bytes 1310720 | tf_op jit(solution)/shard_map/all_gather | solution.py:18
  314.1 27.4 %collective-permute-start.9 = (f32[1,1024,256]{1,2,0:T(8,128)}, f32[1,1024,256]{1,2,0:T(8,128)S(1)}, u32[]{:S(2)}, u32[]{:S(2)}) collective-permute-start(f32[1,1024,256]{1,2,0:T(8,128)} %bitcast.125), channel_id=1, source_target_pairs={{8,0},{12,4},{16,8},{20,12},{24,16},{28,20},{9,1},{13,5},{17,9},{2... | collective-permute-start | bytes 3145736 | tf_op jit(solution)/shard_map/ppermute | solution.py:10
  316.6 27.1 %collective-permute-start.8 = (f32[1,1024,256]{1,2,0:T(8,128)}, f32[1,1024,256]{1,2,0:T(8,128)S(1)}, u32[]{:S(2)}, u32[]{:S(2)}) collective-permute-start(f32[1,1024,256]{1,2,0:T(8,128)} %bitcast.126), channel_id=1, source_target_pairs={{0,8},{4,12},{8,16},{12,20},{16,24},{20,28},{1,9},{5,13},{9,17},{1... | collective-permute-start | bytes 3145736 | tf_op jit(solution)/shard_map/ppermute | solution.py:10
  363.4 50.0 %collective-permute-start.11 = (f32[1,1024,256]{1,2,0:T(8,128)}, f32[1,1024,256]{1,2,0:T(8,128)}, u32[]{:S(2)}, u32[]{:S(2)}) collective-permute-start(f32[1,1024,256]{1,2,0:T(8,128)} %bitcast.123), channel_id=1, source_target_pairs={{4,0},{8,4},{12,8},{16,12},{20,16},{24,20},{28,24},{5,1},{9,5},{13... | collective-permute-start | bytes 3145736 | tf_op jit(solution)/shard_map/ppermute | solution.py:10
  366.7 48.9 %collective-permute-start.10 = (f32[1,1024,256]{1,2,0:T(8,128)}, f32[1,1024,256]{1,2,0:T(8,128)}, u32[]{:S(2)}, u32[]{:S(2)}) collective-permute-start(f32[1,1024,256]{1,2,0:T(8,128)} %bitcast.124), channel_id=1, source_target_pairs={{0,4},{4,8},{8,12},{12,16},{16,20},{20,24},{24,28},{1,5},{5,9},{9,... | collective-permute-start | bytes 3145736 | tf_op jit(solution)/shard_map/ppermute | solution.py:10
Sparse Core Ops, SparseCore 0:
  8.9 17.8 all-gather.10
  82.1 15.8 all-gather.12
  130.9 16.5 all-gather.14
  204.0 17.7 all-gather.16
  225.8 16.7 all-gather.18
  296.5 17.5 all-gather.20
  345.6 17.7 all-gather.22
where the time goes:
time: 428 us; the launch traced here: 427 us
  waiting for transfers between devices  341 us (80%)
  starting transfers between devices  39.3 us (9%)
  matrix products  30.4 us (7%)
  between operations  13.7 us (3%)
    ppermute x12, waiting for transfers between devices, from_behind(): return lax.ppermute(shard, axis, pairs)  218 us
    all_gather x6, waiting for transfers between devices, neighbour_terms(): whole = lax.all_gather(vectors, 'row', axis=1, tiled=True)  104 us
    ppermute x12, starting transfers between devices, from_behind(): return lax.ppermute(shard, axis, pairs)  38.9 us
    dot_general x13, matrix products, product_of(): jnp.dot(left, right, precision=lax.Precision.HIGHEST, preferred_element_t...  30.4 us
    all_gather x1, waiting for transfers between devices, on_device(): lax.all_gather(saved, 'row', axis=1, tiled=True)[0]  17.9 us
  transfers between devices with their start and end apart: 19, of which 16 were waited for; matrix products, arithmetic and copies ran while one was open for 3% of the time, Pallas kernels for 0%

commit v1 on v0

v1 whole, which is shorter than its diff:
```python
import functools

import jax
import jax.numpy as jnp
from jax import lax
from jax.experimental import pallas as pl
from jax.experimental.pallas import tpu as pltpu
from jax.sharding import PartitionSpec as P

AXES = ("layer", "row")
VMEM = pl.BlockSpec(memory_space=pltpu.VMEM)
SMEM = pl.BlockSpec(memory_space=pltpu.SMEM)


def halves(value):
    high = value.astype(jnp.bfloat16)
    return high, (value - high.astype(jnp.float32)).astype(jnp.bfloat16)


def product(left, right):
    left_high, left_low = halves(left)
    right_high, right_low = halves(right)
    dot = functools.partial(jnp.dot, preferred_element_type=jnp.float32)
    return dot(left_high, right_high) + (dot(left_high, right_low) + dot(left_low, right_high))


def combine_kernel(shape, sign, scalar_ref, start_ref, *refs):
    out_ref = refs[-1]
    count = start_ref.shape[0] // 2
    row = scalar_ref[0]
    sums = [start_ref[:count, :], start_ref[count:, :]]
    at = 0
    for pieces in shape:
        mats = refs[at:at + 2]
        at += 2
        for flip, arrivals in pieces:
            piece = refs[at][...]
            for ref in refs[at + 1:at + arrivals]:
                piece = piece + ref[...]
            at += arrivals
            for part in range(2):
                block = row ^ (2 * flip + part)
                columns = pl.ds(pl.multiple_of(block * count, count), count)
                vector = piece[part * count:(part + 1) * count]
                for own in range(2):
                    term = product(mats[own][:, columns], vector)
                    sums[own] = sums[own] + term if sign > 0 else sums[own] - term
    out_ref[:count, :] = sums[0]
    out_ref[count:, :] = sums[1]


def combine(row, start, terms, sign):
    shape, operands = [], []
    for own, sibling, pieces in terms:
        shape.append([(flip, len(arrivals)) for flip, arrivals in pieces])
        operands += [own, sibling]
        for _, arrivals in pieces:
            operands += arrivals
    macs = sum(2 * t[0].size * start.shape[1] for t in terms)
    return pl.pallas_call(
        functools.partial(combine_kernel, shape, sign),
        out_shape=jax.ShapeDtypeStruct(start.shape, start.dtype),
        in_specs=[SMEM] + [VMEM] * (1 + len(operands)),
        out_specs=VMEM,
        cost_estimate=pl.CostEstimate(flops=6 * macs, bytes_accessed=4 * sum(o.size for o in operands), transcendentals=0),
        compiler_params=pltpu.CompilerParams(vmem_limit_bytes=24 << 20),
    )(row, start, *operands)


def on_device(layers, rows, right_side, reduce_factors, solve_factors):
    levels = reduce_factors.shape[0]
    root = layers // 2
    chips = rows // 2
    count, columns = right_side.shape[1], right_side.shape[2] // 2
    layer, row = lax.axis_index("layer"), lax.axis_index("row")
    scalars = row.astype(jnp.int32).reshape(1)
    core = row % 2

    def move(block, pairs, flip=0, swap=0):
        pairs = [(a, b) for a, b in pairs if 0 <= a < layers and 0 <= b < layers]
        if not pairs:
            return None
        hops = [(a * rows + r, b * rows + (r ^ (2 * flip + swap))) for a, b in pairs for r in range(rows)]
        return lax.ppermute(block, AXES, hops)

    def moved(block, pairs, own=True):
        out = []
        for flip in range(0 if own else 1, chips):
            arrived = move(block, pairs, flip)
            if arrived is not None:
                out.append((flip, [arrived]))
        return out

    def both(first, second):
        if not first or not second:
            return first or second
        return [(flip, a + b) for (flip, a), (_, b) in zip(first, second)]

    every = [(i, i) for i in range(layers)]

    mine = lax.dynamic_slice_in_dim(right_side[0], core * columns, columns, 1)
    other = lax.dynamic_slice_in_dim(right_side[0], (1 - core) * columns, columns, 1)
    current = jnp.concatenate([mine, move(other, every, 0, 1)], axis=0)

    sibling_reduce = [move(reduce_factors[k, 0], every, 0, 1) for k in range(levels - 1)]
    sibling_solve = move(solve_factors[0], every, 0, 1)
    own_reduce = [reduce_factors[k, 0] for k in range(levels - 1)]
    own_solve = solve_factors[0]
    root_fold = move(reduce_factors[levels - 1, 0, 1], [(0, root)])
    root_inverse = move(solve_factors[0, 0], [(0, root)])
    root_fold_sibling = move(root_fold, [(root, root)], 0, 1)
    root_inverse_sibling = move(root_inverse, [(root, root)], 0, 1)

    odd = range(1, layers, 2)
    upper = move(current, [(i, i - 1) for i in odd])
    passed = [(flip, move(current, [(i, i + 2) for i in odd], flip)) for flip in range(1, chips)]
    upper_pieces = [(0, [upper])] + moved(upper, [(i - 1, i - 1) for i in odd], own=False)
    lower_pieces = [(0, [move(upper, [(i - 1, i + 1) for i in odd])])]
    lower_pieces += [(flip, [move(block, [(i, i - 1) for i in odd])]) for flip, block in passed]
    current = combine(scalars, current, [
        (own_reduce[0][0], sibling_reduce[0][0], lower_pieces),
        (own_reduce[0][1], sibling_reduce[0][1], upper_pieces),
    ], -1)

    for k in range(1, levels - 1):
        stride = 1 << k
        senders = range(stride, layers, 2 * stride)
        current = combine(scalars, current, [
            (own_reduce[k][0], sibling_reduce[k][0], moved(current, [(i, i + stride) for i in senders])),
            (own_reduce[k][1], sibling_reduce[k][1], moved(current, [(i, i - stride) for i in senders])),
        ], -1)

    first = move(current, [(0, root)])
    saved = [(0, [current])] + moved(current, every, own=False)
    folded = combine(scalars, first, [(root_fold, root_fold_sibling, saved)], -1)
    zero = jnp.zeros_like(current)
    base = combine(scalars, zero, [(own_solve[0], sibling_solve[0], saved)], 1)
    stay = [(root, root)]
    top = combine(scalars, zero, [
        (root_inverse, root_inverse_sibling, [(0, [folded])] + moved(folded, stay, own=False)),
    ], 1)
    middle = combine(scalars, base, [
        (own_solve[1], sibling_solve[1], [(0, [top])] + moved(top, stay, own=False)),
    ], -1)
    top_home = move(top, [(root, 0)])
    result = jnp.where(layer == root, middle, top_home)
    older = top_home

    for k in reversed(range(levels - 1)):
        stride = 1 << k
        late = range(2 * stride, layers, 4 * stride)
        early = range(0, layers, 4 * stride)
        from_early = both(moved(older, [(i, i + stride) for i in early]), moved(older, [(i, i - stride) for i in early]))
        from_late = both(moved(result, [(i, i + stride) for i in late]), moved(result, [(i, i - stride) for i in late]))
        west_late = layer % (4 * stride) == 3 * stride
        target = layer % (2 * stride) == stride
        pick = lambda a, b: jnp.where(west_late, a, b)
        early_own, early_sibling = pick(own_solve[2], own_solve[1]), pick(sibling_solve[2], sibling_solve[1])
        late_own, late_sibling = pick(own_solve[1], own_solve[2]), pick(sibling_solve[1], sibling_solve[2])
        start = combine(scalars, jnp.where(target, base, result), [(early_own, early_sibling, from_early)], -1)
        older = result
        result = combine(scalars, start, [(late_own, late_sibling, from_late)], -1)

    back = move(result[count:], every, 0, 1)
    kept = result[:count]
    return jnp.where(core == 0, jnp.concatenate([kept, back], 1), jnp.concatenate([back, kept], 1))[None]


def solution(mesh):
    placed = (
        P("layer", "row", None),
        P(None, "layer", None, "row", None),
        P("layer", None, "row", None),
    )
    return jax.shard_map(
        functools.partial(on_device, mesh.shape["layer"], mesh.shape["row"]),
        mesh=mesh, in_specs=placed, out_specs=P("layer", "row", None), check_vma=False,
    )
```

time: 428 us -> 167 us (0.39)
  waiting for transfers between devices: 341 us -> 61.4 us
  starting transfers between devices: 39.3 us -> 72 us
  matrix products: 30.4 us -> 0 us
  between operations: 13.7 us -> 0.6 us
  local copies, waits for them, and re-layouts: 1.8 us -> 13.5 us
  Pallas kernels: 0 us -> 11.6 us
  other arithmetic: 0.72 us -> 5.24 us
    ppermute x12 -> x37, waiting for transfers between devices: 218 us -> 61.4 us  [move(): return lax.ppermute(block, AXES, hops)]
    all_gather x7 -> x0, waiting for transfers between devices: 122 us -> none  [the longest x6 104 us: neighbour_terms(): whole = lax.all_gather(vectors, 'row', axis=1, tiled=True)]
    ppermute x12 -> x37, starting transfers between devices: 38.9 us -> 72 us  [move(): return lax.ppermute(block, AXES, hops)]
    dot_general x13 -> x0, matrix products: 30.4 us -> none  [product_of(): jnp.dot(left, right, precision=lax.Precision.HIGHEST, preferred_element_t...]
    squeeze x0 -> x6, local copies, waits for them, and re-layouts: none -> 13.4 us  [the longest x1 4.79 us: on_device(): own_reduce = [reduce_factors[k, 0] for k in range(levels - 1)]]
    pallas_call x0 -> x10, Pallas kernels: none -> 11.6 us  [combine(): pl.pallas_call(functools.partial(combine_kernel, shape, sign), out_shape=...]
    select_n x1 -> x5, other arithmetic: 0.72 us -> 5.22 us  [the longest x2 4.42 us: on_device(): pick = lambda a, b: jnp.where(west_late, a, b)]
  transfers between devices with their start and end apart: 19 -> 37, of which waited for: 16 -> 15; matrix products, arithmetic and copies ran while one was open for 3% -> 8% of each run, Pallas kernels for 0% -> 6%
where the time goes in v1:
time: 167 us; the launch traced here: 164 us
  starting transfers between devices  72 us (43%)
  waiting for transfers between devices  61.4 us (37%)
  local copies, waits for them, and re-layouts  13.5 us (8%)
  Pallas kernels  11.6 us (7%)
  other arithmetic  5.24 us (3%)
    ppermute x37, starting transfers between devices, move(): return lax.ppermute(block, AXES, hops)  72 us
    ppermute x37, waiting for transfers between devices, move(): return lax.ppermute(block, AXES, hops)  61.4 us
    pallas_call x10, Pallas kernels, combine(): pl.pallas_call(functools.partial(combine_kernel, shape, sign), out_shape=...  11.6 us
    squeeze x1, local copies, waits for them, and re-layouts, on_device(): own_reduce = [reduce_factors[k, 0] for k in range(levels - 1)]  4.79 us
    select_n x2, other arithmetic, on_device(): pick = lambda a, b: jnp.where(west_late, a, b)  4.42 us
  transfers between devices with their start and end apart: 37, of which 15 were waited for; matrix products, arithmetic and copies ran while one was open for 8% of the time, Pallas kernels for 6%

profile of v1, /device:TPU:8, one launch (start us, length us, event | category | flops | bytes accessed | tf_op | source)
XLA Modules:
  0.0 164.3 jit_solution(16581884709570007097)
XLA Ops:
  0.0 4.8 %slice_bitcast_fusion = (f32[2,256,1024]{2,1,0:T(8,128)}, f32[2,256,1024]{2,1,0:T(8,128)}) fusion(f32[3,1,2,256,1024]{4,3,2,1,0:T(8,128)} %param.4), kind=kLoop, calls=%fused_computation | loop fusion | bytes 8388608 | tf_op jit(solution)/shard_map/squeeze | solution.py:107
  5.4 3.4 %collective-permute-done.1 = f32[256,128]{1,0:T(8,128)S(1)} collective-permute-done((f32[256,128]{1,0:T(8,128)S(1)}, f32[256,128]{1,0:T(8,128)S(1)}, u32[]{:S(2)}, u32[]{:S(2)}) %collective-permute-start.1) | collective-permute-done | bytes 131104 | tf_op jit(solution)/shard_map/ppermute | solution.py:84
  8.8 1.3 collective-permute-start.3
  11.3 7.9 %collective-permute-done.3.refs_6_ = f32[512,128]{1,0:T(8,128)S(1)} collective-permute-done((f32[512,128]{1,0:T(8,128)S(1)}, f32[512,128]{1,0:T(8,128)S(1)}, u32[]{:S(2)}, u32[]{:S(2)}) %collective-permute-start.3) | collective-permute-done | bytes 262176 | tf_op jit(solution)/shard_map/ppermute | solution.py:84
  19.3 3.5 %collective-permute-start.4 = (f32[512,128]{1,0:T(8,128)S(1)}, f32[512,128]{1,0:T(8,128)S(1)}, u32[]{:S(2)}, u32[]{:S(2)}) collective-permute-start(f32[512,128]{1,0:T(8,128)S(1)} %collective-permute-done.3.refs_6_), channel_id=1, source_target_pairs={{0,8},{1,9},{2,10},{3,11},{8,16},{9,17},{10,18},{11,19},{16,24},{1... | collective-permute-start | bytes 786440 | tf_op jit(solution)/shard_map/ppermute | solution.py:84
  22.8 3.1 %slice_bitcast_fusion.9 = (f32[256,1024]{1,0:T(8,128)S(1)}, f32[256,1024]{1,0:T(8,128)S(1)}, f32[256,1024]{1,0:T(8,128)S(1)}, f32[256,1024]{1,0:T(8,128)S(1)}, f32[256,1024]{1,0:T(8,128)S(1)}) fusion(f32[3,1,2,256,1024]{4,3,2,1,0:T(8,128)} %param.4), kind=kLoop, calls=%fused_computation.13 | loop fusion | bytes 10485760 | tf_op jit(solution)/shard_map/squeeze | solution.py:109
  26.6 2.3 %collective-permute-done.4.refs_2_ = f32[512,128]{1,0:T(8,128)S(1)} collective-permute-done((f32[512,128]{1,0:T(8,128)S(1)}, f32[512,128]{1,0:T(8,128)S(1)}, u32[]{:S(2)}, u32[]{:S(2)}) %collective-permute-start.4) | collective-permute-done | bytes 262176 | tf_op jit(solution)/shard_map/ppermute | solution.py:84
  28.9 1.3 collective-permute-start.6
  30.2 1.7 %slice_bitcast_fusion.10 = (f32[256,1024]{1,0:T(8,128)S(1)}, f32[256,1024]{1,0:T(8,128)S(1)}) fusion(f32[1,3,256,1024]{3,2,1,0:T(8,128)} %param.5), kind=kLoop, calls=%fused_computation.14 | loop fusion | bytes 4194304 | tf_op jit(solution)/shard_map/squeeze | solution.py:143
  31.9 5.8 %collective-permute-done.6.refs_3_ = f32[512,128]{1,0:T(8,128)S(1)} collective-permute-done((f32[512,128]{1,0:T(8,128)S(1)}, f32[512,128]{1,0:T(8,128)S(1)}, u32[]{:S(2)}, u32[]{:S(2)}) %collective-permute-start.6) | collective-permute-done | bytes 262176 | tf_op jit(solution)/shard_map/ppermute | solution.py:84
  38.4 3.4 %collective-permute-start.7 = (f32[512,128]{1,0:T(8,128)S(1)}, f32[512,128]{1,0:T(8,128)S(1)}, u32[]{:S(2)}, u32[]{:S(2)}) collective-permute-start(f32[512,128]{1,0:T(8,128)S(1)} %collective-permute-done.3.refs_6_), channel_id=1, source_target_pairs={{0,2},{1,3},{2,0},{3,1},{8,10},{9,11},{10,8},{11,9},{16,18},{17,19... | collective-permute-start | bytes 786440 | tf_op jit(solution)/shard_map/ppermute | solution.py:84
  42.6 1.8 %slice_bitcast_fusion.6 = (f32[256,1024]{1,0:T(8,128)S(1)}, f32[256,1024]{1,0:T(8,128)S(1)}) fusion(f32[2,256,1024]{2,1,0:T(8,128)} %collective-permute-done.2), kind=kLoop, calls=%fused_computation.6 | loop fusion | bytes 4194304 | tf_op jit(solution)/shard_map/squeeze | solution.py:122
  44.4 2.3 %collective-permute-done.7.refs_7_ = f32[512,128]{1,0:T(8,128)S(1)} collective-permute-done((f32[512,128]{1,0:T(8,128)S(1)}, f32[512,128]{1,0:T(8,128)S(1)}, u32[]{:S(2)}, u32[]{:S(2)}) %collective-permute-start.7) | collective-permute-done | bytes 262176 | tf_op jit(solution)/shard_map/ppermute | solution.py:84
  46.7 1.8 %shard_map.37.start_ref = f32[512,128]{1,0:T(8,128)S(1)} custom-call(s32[1]{0:T(128)} %bitcast.scalar_ref, f32[512,128]{1,0:T(8,128)S(1)} %pad_maximum_fusion.start_ref, f32[256,1024]{1,0:T(8,128)S(1)} %get-tuple-element.10.refs_0_, f32[256,1024]{1,0:T(8,128)S(1)} %get-tuple-element.29.refs_1_, f32[512,128]{1,0:T(8,128)S(1)} %collective-permute-done.4.refs_2_, ...), custom_call_target="tpu_custom_call" | custom-call | flops 805306368 | bytes 5242880 | tf_op jit(solution)/shard_map/pallas_call | solution.py:60
  48.5 20.8 %collective-permute-start.10 = (f32[512,128]{1,0:T(8,128)S(1)}, f32[512,128]{1,0:T(8,128)S(1)}, u32[]{:S(2)}, u32[]{:S(2)}) collective-permute-start(f32[512,128]{1,0:T(8,128)S(1)} %shard_map.37.start_ref), channel_id=1, source_target_pairs={{8,18},{9,19},{10,16},{11,17}} | collective-permute-start | bytes 786440 | tf_op jit(solution)/shard_map/ppermute | solution.py:84
  69.4 7.8 %collective-permute-start.11 = (f32[512,128]{1,0:T(8,128)S(1)}, f32[512,128]{1,0:T(8,128)S(1)}, u32[]{:S(2)}, u32[]{:S(2)}) collective-permute-start(f32[512,128]{1,0:T(8,128)S(1)} %shard_map.37.start_ref), channel_id=1, source_target_pairs={{8,0},{9,1},{10,2},{11,3},{24,16},{25,17},{26,18},{27,19}} | collective-permute-start | bytes 786440 | tf_op jit(solution)/shard_map/ppermute | solution.py:84
  77.9 2.3 %collective-permute-done.10.refs_3_ = f32[512,128]{1,0:T(8,128)S(1)} collective-permute-done((f32[512,128]{1,0:T(8,128)S(1)}, f32[512,128]{1,0:T(8,128)S(1)}, u32[]{:S(2)}, u32[]{:S(2)}) %collective-permute-start.10) | collective-permute-done | bytes 262176 | tf_op jit(solution)/shard_map/ppermute | solution.py:84
  80.2 1.3 collective-permute-start.12
  81.5 5.9 %collective-permute-start.9 = (f32[512,128]{1,0:T(8,128)S(1)}, f32[512,128]{1,0:T(8,128)S(1)}, u32[]{:S(2)}, u32[]{:S(2)}) collective-permute-start(f32[512,128]{1,0:T(8,128)S(1)} %shard_map.37.start_ref), channel_id=1, source_target_pairs={{8,16},{9,17},{10,18},{11,19}} | collective-permute-start | bytes 786440 | tf_op jit(solution)/shard_map/ppermute | solution.py:84
  87.7 4.9 %collective-permute-done.9.refs_2_ = f32[512,128]{1,0:T(8,128)S(1)} collective-permute-done((f32[512,128]{1,0:T(8,128)S(1)}, f32[512,128]{1,0:T(8,128)S(1)}, u32[]{:S(2)}, u32[]{:S(2)}) %collective-permute-start.9) | collective-permute-done | bytes 262176 | tf_op jit(solution)/shard_map/ppermute | solution.py:84
  92.6 1.8 %shard_map.38.refs_2_ = f32[512,128]{1,0:T(8,128)S(1)} custom-call(s32[1]{0:T(128)} %bitcast.scalar_ref, f32[512,128]{1,0:T(8,128)S(1)} %shard_map.37.start_ref, f32[256,1024]{1,0:T(8,128)S(1)} %get-tuple-element.8.refs_0_, f32[256,1024]{1,0:T(8,128)S(1)} %get-tuple-element.27.refs_1_, f32[512,128]{1,0:T(8,128)S(1)} %collective-permute-done.9.refs_2_, ...), custom_call_target="tpu_custom_call" | custom-call | flops 805306368 | bytes 5242880 | tf_op jit(solution)/shard_map/pallas_call | solution.py:60
  95.7 5.5 %collective-permute-done.13.refs_3_ = f32[512,128]{1,0:T(8,128)S(1)} collective-permute-done((f32[512,128]{1,0:T(8,128)S(1)}, f32[512,128]{1,0:T(8,128)S(1)}, u32[]{:S(2)}, u32[]{:S(2)}) %collective-permute-start.13) | collective-permute-done | bytes 262176 | tf_op jit(solution)/shard_map/ppermute | solution.py:84
  101.2 1.0 shard_map.40.refs_2_
  102.9 1.0 shard_map.41.refs_2_
  105.3 1.3 collective-permute-start.22
  106.6 1.5 collective-permute-start.23
  108.1 1.8 %slice_bitcast_fusion.3 = (f32[256,1024]{1,0:T(8,128)S(1)}, f32[256,1024]{1,0:T(8,128)S(1)}) fusion(f32[3,256,1024]{2,1,0:T(8,128)} %collective-permute-done), kind=kLoop, calls=%fused_computation.3 | loop fusion | bytes 4194304 | tf_op jit(solution)/shard_map/squeeze | solution.py:143
  109.9 1.0 shard_map.39.start_ref
  110.9 1.0 shard_map.42
  112.7 1.3 collective-permute-start.25
  114.0 2.2 %bitcast_select_fusion = (f32[256,1024]{1,0:T(8,128)S(1)}, f32[256,1024]{1,0:T(8,128)S(1)}, f32[256,1024]{1,0:T(8,128)S(1)}, f32[256,1024]{1,0:T(8,128)S(1)}) fusion(f32[1,3,256,1024]{3,2,1,0:T(8,128)} %param.5, pred[]{:T(512)S(6)} %eq.29, pred[]{:T(512)S(6)} %eq.28), kind=kLoop, calls=%fused_computation.9 | loop fusion | flops 1048576 | bytes 6291458 | tf_op jit(solution)/shard_map/jit(_where)/select_n | solution.py:157
  116.9 13.5 %collective-permute-done.22.refs_2_ = f32[512,128]{1,0:T(8,128)S(1)} collective-permute-done((f32[512,128]{1,0:T(8,128)S(1)}, f32[512,128]{1,0:T(8,128)S(1)}, u32[]{:S(2)}, u32[]{:S(2)}) %collective-permute-start.22) | collective-permute-done | bytes 262176 | tf_op jit(solution)/shard_map/ppermute | solution.py:84
  130.4 1.3 collective-permute-start.27
  131.7 3.2 %collective-permute-done.23.refs_3_ = f32[512,128]{1,0:T(8,128)S(1)} collective-permute-done((f32[512,128]{1,0:T(8,128)S(1)}, f32[512,128]{1,0:T(8,128)S(1)}, u32[]{:S(2)}, u32[]{:S(2)}) %collective-permute-start.23) | collective-permute-done | bytes 262176 | tf_op jit(solution)/shard_map/ppermute | solution.py:84
  136.3 1.4 collective-permute-done.25.refs_3_
  138.3 2.2 %fusion = (f32[256,1024]{1,0:T(8,128)S(1)}, f32[256,1024]{1,0:T(8,128)S(1)}, f32[256,1024]{1,0:T(8,128)S(1)}, f32[256,1024]{1,0:T(8,128)S(1)}) fusion(f32[3,256,1024]{2,1,0:T(8,128)} %collective-permute-done, pred[]{:T(512)S(6)} %eq.29, pred[]{:T(512)S(6)} %eq.28), kind=kLoop, calls=%fused_computation.20 | loop fusion | flops 1048576 | bytes 6291458 | tf_op jit(solution)/shard_map/jit(_where)/select_n | solution.py:157
  140.6 1.0 shard_map.43.start_ref
  142.2 2.0 %collective-permute-done.27.refs_5_ = f32[512,128]{1,0:T(8,128)S(1)} collective-permute-done((f32[512,128]{1,0:T(8,128)S(1)}, f32[512,128]{1,0:T(8,128)S(1)}, u32[]{:S(2)}, u32[]{:S(2)}) %collective-permute-start.27) | collective-permute-done | bytes 262176 | tf_op jit(solution)/shard_map/ppermute | solution.py:84
  144.2 1.0 shard_map.44
  145.2 1.3 collective-permute-start.32
  146.6 1.3 collective-permute-start.33
  147.9 5.4 %collective-permute-start.34 = (f32[512,128]{1,0:T(8,128)S(1)}, f32[512,128]{1,0:T(8,128)S(1)}, u32[]{:S(2)}, u32[]{:S(2)}) collective-permute-start(f32[512,128]{1,0:T(8,128)S(1)} %shard_map.44), channel_id=1, source_target_pairs={{8,14},{9,15},{10,12},{11,13},{24,30},{25,31},{26,28},{27,29}} | collective-permute-start | bytes 786440 | tf_op jit(solution)/shard_map/ppermute | solution.py:84
  153.3 1.3 collective-permute-start.35
  154.6 1.0 shard_map.45.start_ref
  155.6 0.8 collective-permute-done.32.refs_2_
  156.4 4.8 %collective-permute-done.34.refs_4_ = f32[512,128]{1,0:T(8,128)S(1)} collective-permute-done((f32[512,128]{1,0:T(8,128)S(1)}, f32[512,128]{1,0:T(8,128)S(1)}, u32[]{:S(2)}, u32[]{:S(2)}) %collective-permute-start.34) | collective-permute-done | bytes 262176 | tf_op jit(solution)/shard_map/ppermute | solution.py:84
  161.2 1.0 shard_map.46
  162.3 1.3 collective-permute-done.36
  (53 shorter events, 13.3 us)
Async XLA Ops:
  0.0 4.8 %copy-start = (f32[1,256,256]{2,1,0:T(8,128)S(1)}, f32[1,256,256]{2,1,0:T(8,128)}, u32[]{:S(2)}) copy-start(f32[1,256,256]{2,1,0:T(8,128)} %param.3) | copy-start | bytes 786436
  4.8 37.0 %collective-permute-start.2 = (f32[2,256,1024]{2,1,0:T(8,128)}, f32[2,256,1024]{2,1,0:T(8,128)}, u32[]{:S(2)}, u32[]{:S(2)}) collective-permute-start(f32[2,256,1024]{2,1,0:T(8,128)} %get-tuple-element.13), channel_id=1, source_target_pairs={{0,1},{1,0},{2,3},{3,2},{4,5},{5,4},{6,7},{7,6},{8,9},{9,8},{10,11... | collective-permute-start | bytes 6291464 | tf_op jit(solution)/shard_map/ppermute | solution.py:84
  4.8 3.9 %collective-permute-start.1 = (f32[256,128]{1,0:T(8,128)S(1)}, f32[256,128]{1,0:T(8,128)S(1)}, u32[]{:S(2)}, u32[]{:S(2)}) collective-permute-start(f32[256,128]{1,0:T(8,128)S(1)} %get-tuple-element.33), channel_id=1, source_target_pairs={{0,1},{1,0},{2,3},{3,2},{4,5},{5,4},{6,7},{7,6},{8,9},{9,8},{10,11... | collective-permute-start | bytes 393224 | tf_op jit(solution)/shard_map/ppermute | solution.py:84
  8.8 10.5 %collective-permute-start.3 = (f32[512,128]{1,0:T(8,128)S(1)}, f32[512,128]{1,0:T(8,128)S(1)}, u32[]{:S(2)}, u32[]{:S(2)}) collective-permute-start(f32[512,128]{1,0:T(8,128)S(1)} %pad_maximum_fusion.start_ref), channel_id=1, source_target_pairs={{4,0},{5,1},{6,2},{7,3},{12,8},{13,9},{14,10},{15,11},{20,16},{21,... | collective-permute-start | bytes 786440 | tf_op jit(solution)/shard_map/ppermute | solution.py:84
  10.1 67.0 %collective-permute-start.8 = (f32[2,256,1024]{2,1,0:T(8,128)}, f32[2,256,1024]{2,1,0:T(8,128)S(1)}, u32[]{:S(2)}, u32[]{:S(2)}) collective-permute-start(f32[2,256,1024]{2,1,0:T(8,128)} %get-tuple-element.12), channel_id=1, source_target_pairs={{0,1},{1,0},{2,3},{3,2},{4,5},{5,4},{6,7},{7,6},{8,9},{9,8},{10,11... | collective-permute-start | bytes 6291464 | tf_op jit(solution)/shard_map/ppermute | solution.py:84
  10.5 97.6 %collective-permute-start = (f32[3,256,1024]{2,1,0:T(8,128)}, f32[3,256,1024]{2,1,0:T(8,128)}, u32[]{:S(2)}, u32[]{:S(2)}) collective-permute-start(f32[3,256,1024]{2,1,0:T(8,128)} %bitcast.2), channel_id=1, source_target_pairs={{0,1},{1,0},{2,3},{3,2},{4,5},{5,4},{6,7},{7,6},{8,9},{9,8},{10,11... | collective-permute-start | bytes 9437192 | tf_op jit(solution)/shard_map/ppermute | solution.py:84
  10.7 15.2 %collective-permute-start.5 = (f32[512,128]{1,0:T(8,128)S(1)}, f32[512,128]{1,0:T(8,128)S(1)}, u32[]{:S(2)}, u32[]{:S(2)}) collective-permute-start(f32[512,128]{1,0:T(8,128)S(1)} %pad_maximum_fusion.start_ref), channel_id=1, source_target_pairs={{4,14},{5,15},{6,12},{7,13},{12,22},{13,23},{14,20},{15,21},{20,30... | collective-permute-start | bytes 786440 | tf_op jit(solution)/shard_map/ppermute | solution.py:84
  19.3 9.6 %collective-permute-start.4 = (f32[512,128]{1,0:T(8,128)S(1)}, f32[512,128]{1,0:T(8,128)S(1)}, u32[]{:S(2)}, u32[]{:S(2)}) collective-permute-start(f32[512,128]{1,0:T(8,128)S(1)} %collective-permute-done.3.refs_6_), channel_id=1, source_target_pairs={{0,8},{1,9},{2,10},{3,11},{8,16},{9,17},{10,18},{11,19},{16,24},{1... | collective-permute-start | bytes 786440 | tf_op jit(solution)/shard_map/ppermute | solution.py:84
  25.9 12.5 %collective-permute-start.17 = (f32[256,1024]{1,0:T(8,128)S(1)}, f32[256,1024]{1,0:T(8,128)S(1)}, u32[]{:S(2)}, u32[]{:S(2)}) collective-permute-start(f32[256,1024]{1,0:T(8,128)S(1)} %get-tuple-element.7), channel_id=1, source_target_pairs={{0,16},{1,17},{2,18},{3,19}} | collective-permute-start | bytes 3145736 | tf_op jit(solution)/shard_map/ppermute | solution.py:84
  28.9 8.7 %collective-permute-start.6 = (f32[512,128]{1,0:T(8,128)S(1)}, f32[512,128]{1,0:T(8,128)S(1)}, u32[]{:S(2)}, u32[]{:S(2)}) collective-permute-start(f32[512,128]{1,0:T(8,128)S(1)} %collective-permute-done.5), channel_id=1, source_target_pairs={{4,0},{5,1},{6,2},{7,3},{12,8},{13,9},{14,10},{15,11},{20,16},{21,... | collective-permute-start | bytes 786440 | tf_op jit(solution)/shard_map/ppermute | solution.py:84
  37.7 31.7 %collective-permute-start.14 = (f32[256,1024]{1,0:T(8,128)S(1)}, f32[256,1024]{1,0:T(8,128)S(1)}, u32[]{:S(2)}, u32[]{:S(2)}) collective-permute-start(f32[256,1024]{1,0:T(8,128)S(1)} %get-tuple-element.25.refs_0_), channel_id=1, source_target_pairs={{0,16},{1,17},{2,18},{3,19}} | collective-permute-start | bytes 3145736 | tf_op jit(solution)/shard_map/ppermute | solution.py:84
  38.4 8.3 %collective-permute-start.7 = (f32[512,128]{1,0:T(8,128)S(1)}, f32[512,128]{1,0:T(8,128)S(1)}, u32[]{:S(2)}, u32[]{:S(2)}) collective-permute-start(f32[512,128]{1,0:T(8,128)S(1)} %collective-permute-done.3.refs_6_), channel_id=1, source_target_pairs={{0,2},{1,3},{2,0},{3,1},{8,10},{9,11},{10,8},{11,9},{16,18},{17,19... | collective-permute-start | bytes 786440 | tf_op jit(solution)/shard_map/ppermute | solution.py:84
  41.8 53.8 %collective-permute-start.18 = (f32[256,1024]{1,0:T(8,128)S(1)}, f32[256,1024]{1,0:T(8,128)S(1)}, u32[]{:S(2)}, u32[]{:S(2)}) collective-permute-start(f32[256,1024]{1,0:T(8,128)S(1)} %collective-permute-done.17.refs_0_), channel_id=1, source_target_pairs={{16,17},{17,16},{18,19},{19,18}} | collective-permute-start | bytes 3145736 | tf_op jit(solution)/shard_map/ppermute | solution.py:84
  48.5 31.7 %collective-permute-start.10 = (f32[512,128]{1,0:T(8,128)S(1)}, f32[512,128]{1,0:T(8,128)S(1)}, u32[]{:S(2)}, u32[]{:S(2)}) collective-permute-start(f32[512,128]{1,0:T(8,128)S(1)} %shard_map.37.start_ref), channel_id=1, source_target_pairs={{8,18},{9,19},{10,16},{11,17}} | collective-permute-start | bytes 786440 | tf_op jit(solution)/shard_map/ppermute | solution.py:84
  69.4 12.2 %collective-permute-start.11 = (f32[512,128]{1,0:T(8,128)S(1)}, f32[512,128]{1,0:T(8,128)S(1)}, u32[]{:S(2)}, u32[]{:S(2)}) collective-permute-start(f32[512,128]{1,0:T(8,128)S(1)} %shard_map.37.start_ref), channel_id=1, source_target_pairs={{8,0},{9,1},{10,2},{11,3},{24,16},{25,17},{26,18},{27,19}} | collective-permute-start | bytes 786440 | tf_op jit(solution)/shard_map/ppermute | solution.py:84
  77.1 25.7 %collective-permute-start.15 = (f32[256,1024]{1,0:T(8,128)S(1)}, f32[256,1024]{1,0:T(8,128)S(1)}, u32[]{:S(2)}, u32[]{:S(2)}) collective-permute-start(f32[256,1024]{1,0:T(8,128)S(1)} %collective-permute-done.14.refs_0_), channel_id=1, source_target_pairs={{16,17},{17,16},{18,19},{19,18}} | collective-permute-start | bytes 3145736 | tf_op jit(solution)/shard_map/ppermute | solution.py:84
  80.2 7.5 %collective-permute-start.12 = (f32[512,128]{1,0:T(8,128)S(1)}, f32[512,128]{1,0:T(8,128)S(1)}, u32[]{:S(2)}, u32[]{:S(2)}) collective-permute-start(f32[512,128]{1,0:T(8,128)S(1)} %shard_map.37.start_ref), channel_id=1, source_target_pairs={{8,2},{9,3},{10,0},{11,1},{24,18},{25,19},{26,16},{27,17}} | collective-permute-start | bytes 786440 | tf_op jit(solution)/shard_map/ppermute | solution.py:84
  81.5 11.1 %collective-permute-start.9 = (f32[512,128]{1,0:T(8,128)S(1)}, f32[512,128]{1,0:T(8,128)S(1)}, u32[]{:S(2)}, u32[]{:S(2)}) collective-permute-start(f32[512,128]{1,0:T(8,128)S(1)} %shard_map.37.start_ref), channel_id=1, source_target_pairs={{8,16},{9,17},{10,18},{11,19}} | collective-permute-start | bytes 786440 | tf_op jit(solution)/shard_map/ppermute | solution.py:84
  94.4 6.8 %collective-permute-start.13 = (f32[512,128]{1,0:T(8,128)S(1)}, f32[512,128]{1,0:T(8,128)S(1)}, u32[]{:S(2)}, u32[]{:S(2)}) collective-permute-start(f32[512,128]{1,0:T(8,128)S(1)} %shard_map.38.refs_2_), channel_id=1, source_target_pairs={{0,2},{1,3},{2,0},{3,1},{4,6},{5,7},{6,4},{7,5},{8,10},{9,11},{10,... | collective-permute-start | bytes 786440 | tf_op jit(solution)/shard_map/ppermute | solution.py:84
  95.0 6.2 %collective-permute-start.16 = (f32[512,128]{1,0:T(8,128)S(1)}, f32[512,128]{1,0:T(8,128)S(1)}, u32[]{:S(2)}, u32[]{:S(2)}) collective-permute-start(f32[512,128]{1,0:T(8,128)S(1)} %shard_map.38.refs_2_), channel_id=1, source_target_pairs={{0,16},{1,17},{2,18},{3,19}} | collective-permute-start | bytes 786440 | tf_op jit(solution)/shard_map/ppermute | solution.py:84
  102.2 0.7 collective-permute-start.19
  103.9 1.4 collective-permute-start.21
  104.6 6.3 %collective-permute-start.20 = (f32[512,128]{1,0:T(8,128)S(1)}, f32[512,128]{1,0:T(8,128)S(1)}, u32[]{:S(2)}, u32[]{:S(2)}) collective-permute-start(f32[512,128]{1,0:T(8,128)S(1)} %shard_map.41.refs_2_), channel_id=1, source_target_pairs={{16,18},{17,19},{18,16},{19,17}} | collective-permute-start | bytes 786440 | tf_op jit(solution)/shard_map/ppermute | solution.py:84
  105.3 25.1 %collective-permute-start.22 = (f32[512,128]{1,0:T(8,128)S(1)}, f32[512,128]{1,0:T(8,128)S(1)}, u32[]{:S(2)}, u32[]{:S(2)}) collective-permute-start(f32[512,128]{1,0:T(8,128)S(1)} %collective-permute-done.21), channel_id=1, source_target_pairs={{0,8},{1,9},{2,10},{3,11}} | collective-permute-start | bytes 786440 | tf_op jit(solution)/shard_map/ppermute | solution.py:84
  106.6 28.3 %collective-permute-start.23 = (f32[512,128]{1,0:T(8,128)S(1)}, f32[512,128]{1,0:T(8,128)S(1)}, u32[]{:S(2)}, u32[]{:S(2)}) collective-permute-start(f32[512,128]{1,0:T(8,128)S(1)} %collective-permute-done.21), channel_id=1, source_target_pairs={{0,10},{1,11},{2,8},{3,9}} | collective-permute-start | bytes 786440 | tf_op jit(solution)/shard_map/ppermute | solution.py:84
  112.0 23.6 %collective-permute-start.24 = (f32[512,128]{1,0:T(8,128)S(1)}, f32[512,128]{1,0:T(8,128)S(1)}, u32[]{:S(2)}, u32[]{:S(2)}) collective-permute-start(f32[512,128]{1,0:T(8,128)S(1)} %get-tuple-element.6), channel_id=1, source_target_pairs={{16,24},{17,25},{18,26},{19,27}} | collective-permute-start | bytes 786440 | tf_op jit(solution)/shard_map/ppermute | solution.py:84
  112.7 25.0 %collective-permute-start.25 = (f32[512,128]{1,0:T(8,128)S(1)}, f32[512,128]{1,0:T(8,128)S(1)}, u32[]{:S(2)}, u32[]{:S(2)}) collective-permute-start(f32[512,128]{1,0:T(8,128)S(1)} %get-tuple-element.6), channel_id=1, source_target_pairs={{16,8},{17,9},{18,10},{19,11}} | collective-permute-start | bytes 786440 | tf_op jit(solution)/shard_map/ppermute | solution.py:84
  116.2 25.4 %collective-permute-start.26 = (f32[512,128]{1,0:T(8,128)S(1)}, f32[512,128]{1,0:T(8,128)S(1)}, u32[]{:S(2)}, u32[]{:S(2)}) collective-permute-start(f32[512,128]{1,0:T(8,128)S(1)} %get-tuple-element.6), channel_id=1, source_target_pairs={{16,26},{17,27},{18,24},{19,25}} | collective-permute-start | bytes 786440 | tf_op jit(solution)/shard_map/ppermute | solution.py:84
  130.4 13.8 %collective-permute-start.27 = (f32[512,128]{1,0:T(8,128)S(1)}, f32[512,128]{1,0:T(8,128)S(1)}, u32[]{:S(2)}, u32[]{:S(2)}) collective-permute-start(f32[512,128]{1,0:T(8,128)S(1)} %get-tuple-element.6), channel_id=1, source_target_pairs={{16,10},{17,11},{18,8},{19,9}} | collective-permute-start | bytes 786440 | tf_op jit(solution)/shard_map/ppermute | solution.py:84
  134.9 11.6 %collective-permute-start.28 = (f32[512,128]{1,0:T(8,128)S(1)}, f32[512,128]{1,0:T(8,128)S(1)}, u32[]{:S(2)}, u32[]{:S(2)}) collective-permute-start(f32[512,128]{1,0:T(8,128)S(1)} %get-tuple-element.6), channel_id=1, source_target_pairs={{0,4},{1,5},{2,6},{3,7},{16,20},{17,21},{18,22},{19,23}} | collective-permute-start | bytes 786440 | tf_op jit(solution)/shard_map/ppermute | solution.py:84
  135.6 12.3 %collective-permute-start.29 = (f32[512,128]{1,0:T(8,128)S(1)}, f32[512,128]{1,0:T(8,128)S(1)}, u32[]{:S(2)}, u32[]{:S(2)}) collective-permute-start(f32[512,128]{1,0:T(8,128)S(1)} %get-tuple-element.6), channel_id=1, source_target_pairs={{16,12},{17,13},{18,14},{19,15}} | collective-permute-start | bytes 786440 | tf_op jit(solution)/shard_map/ppermute | solution.py:84
  137.7 15.6 %collective-permute-start.30 = (f32[512,128]{1,0:T(8,128)S(1)}, f32[512,128]{1,0:T(8,128)S(1)}, u32[]{:S(2)}, u32[]{:S(2)}) collective-permute-start(f32[512,128]{1,0:T(8,128)S(1)} %get-tuple-element.6), channel_id=1, source_target_pairs={{0,6},{1,7},{2,4},{3,5},{16,22},{17,23},{18,20},{19,21}} | collective-permute-start | bytes 786440 | tf_op jit(solution)/shard_map/ppermute | solution.py:84
  141.6 13.1 %collective-permute-start.31 = (f32[512,128]{1,0:T(8,128)S(1)}, f32[512,128]{1,0:T(8,128)S(1)}, u32[]{:S(2)}, u32[]{:S(2)}) collective-permute-start(f32[512,128]{1,0:T(8,128)S(1)} %get-tuple-element.6), channel_id=1, source_target_pairs={{16,14},{17,15},{18,12},{19,13}} | collective-permute-start | bytes 786440 | tf_op jit(solution)/shard_map/ppermute | solution.py:84
  145.2 11.2 %collective-permute-start.32 = (f32[512,128]{1,0:T(8,128)S(1)}, f32[512,128]{1,0:T(8,128)S(1)}, u32[]{:S(2)}, u32[]{:S(2)}) collective-permute-start(f32[512,128]{1,0:T(8,128)S(1)} %shard_map.44), channel_id=1, source_target_pairs={{8,12},{9,13},{10,14},{11,15},{24,28},{25,29},{26,30},{27,31}} | collective-permute-start | bytes 786440 | tf_op jit(solution)/shard_map/ppermute | solution.py:84
  146.6 9.8 %collective-permute-start.33 = (f32[512,128]{1,0:T(8,128)S(1)}, f32[512,128]{1,0:T(8,128)S(1)}, u32[]{:S(2)}, u32[]{:S(2)}) collective-permute-start(f32[512,128]{1,0:T(8,128)S(1)} %shard_map.44), channel_id=1, source_target_pairs={{8,4},{9,5},{10,6},{11,7},{24,20},{25,21},{26,22},{27,23}} | collective-permute-start | bytes 786440 | tf_op jit(solution)/shard_map/ppermute | solution.py:84
  147.9 13.3 %collective-permute-start.34 = (f32[512,128]{1,0:T(8,128)S(1)}, f32[512,128]{1,0:T(8,128)S(1)}, u32[]{:S(2)}, u32[]{:S(2)}) collective-permute-start(f32[512,128]{1,0:T(8,128)S(1)} %shard_map.44), channel_id=1, source_target_pairs={{8,14},{9,15},{10,12},{11,13},{24,30},{25,31},{26,28},{27,29}} | collective-permute-start | bytes 786440 | tf_op jit(solution)/shard_map/ppermute | solution.py:84
  153.3 7.9 %collective-permute-start.35 = (f32[512,128]{1,0:T(8,128)S(1)}, f32[512,128]{1,0:T(8,128)S(1)}, u32[]{:S(2)}, u32[]{:S(2)}) collective-permute-start(f32[512,128]{1,0:T(8,128)S(1)} %shard_map.44), channel_id=1, source_target_pairs={{8,6},{9,7},{10,4},{11,5},{24,22},{25,23},{26,20},{27,21}} | collective-permute-start | bytes 786440 | tf_op jit(solution)/shard_map/ppermute | solution.py:84
  162.2 1.4 collective-permute-start.36

commit v2 on v0

v2 whole, which is shorter than its diff:
```python
import functools

import jax
import jax.numpy as jnp
from jax import lax
from jax.experimental import pallas as pl
from jax.experimental.pallas import tpu as pltpu
from jax.sharding import PartitionSpec as P

AXES = ("layer", "row")
VMEM = pl.BlockSpec(memory_space=pltpu.VMEM)


def halves(value):
    high = value.astype(jnp.bfloat16)
    return high, (value - high.astype(jnp.float32)).astype(jnp.bfloat16)


def product(left, right):
    left_high, left_low = halves(left)
    right_high, right_low = halves(right)
    dot = functools.partial(jnp.dot, preferred_element_type=jnp.float32)
    return dot(left_high, right_high) + (dot(left_high, right_low) + dot(left_low, right_high))


def combine_kernel(shape, sign, level, *refs):
    out_ref = refs[-1]
    count = out_ref.shape[0]
    row = lax.axis_index("row")
    layer = lax.axis_index("layer")
    starts, terms = shape
    if len(starts) == 2:
        total = jnp.where(layer % (2 << level) == (1 << level), refs[starts[0]][...], refs[starts[1]][...])
    else:
        total = refs[starts[0]][...] if starts else None
    for matrix, flip, vector in terms:
        columns = pl.ds(pl.multiple_of((row ^ flip) * count, count), count)
        term = product(refs[matrix][:, columns], refs[vector][...])
        if total is None:
            total = term if sign > 0 else -term
        else:
            total = total + term if sign > 0 else total - term
    out_ref[...] = total


def combine(starts, terms, sign, level=0):
    operands = []

    def place(array):
        for at, known in enumerate(operands):
            if known is array:
                return at
        operands.append(array)
        return len(operands) - 1

    shape = (
        [place(s) for s in starts],
        [(place(matrix), flip, place(vector)) for matrix, flip, vector in terms],
    )
    out = jax.ShapeDtypeStruct(terms[0][2].shape, terms[0][2].dtype)
    return pl.pallas_call(
        functools.partial(combine_kernel, shape, sign, level),
        out_shape=out,
        in_specs=[VMEM] * len(operands),
        out_specs=VMEM,
        cost_estimate=pl.CostEstimate(flops=6 * len(terms) * out.size * out.shape[0], bytes_accessed=0, transcendentals=0),
        compiler_params=pltpu.CompilerParams(vmem_limit_bytes=6 << 20),
    )(*operands)


def load_kernel(levels, reduce_ref, solve_ref, *refs):
    outs, sems = refs[:-1], refs[-1]
    copies = []
    for at, out in enumerate(outs):
        source = reduce_ref.at[at // 2, at % 2] if at < 2 * levels else solve_ref.at[at - 2 * levels]
        copies.append(pltpu.make_async_copy(source, out, sems.at[at]))
    for copy in copies:
        copy.start()
    for copy in copies:
        copy.wait()


def load(reduce_factors, solve_factors):
    levels, shape = reduce_factors.shape[0], reduce_factors.shape[-2:]
    number = 2 * levels + 3
    out = pl.pallas_call(
        functools.partial(load_kernel, levels),
        out_shape=[jax.ShapeDtypeStruct(shape, reduce_factors.dtype)] * number,
        in_specs=[pl.BlockSpec(memory_space=pl.ANY)] * 2,
        out_specs=[VMEM] * number,
        scratch_shapes=[pltpu.SemaphoreType.DMA((number,))],
        cost_estimate=pl.CostEstimate(flops=0, bytes_accessed=0, transcendentals=0),
        compiler_params=pltpu.CompilerParams(vmem_limit_bytes=2 << 20),
    )(reduce_factors, solve_factors)
    return [out[2 * k:2 * k + 2] for k in range(levels)], out[2 * levels:]


def on_device(layers, rows, right_side, reduce_factors, solve_factors):
    levels = reduce_factors.shape[0]
    def move(block, pairs, flip=0):
        hops = [
            (a * rows + r, b * rows + (r ^ flip))
            for a, b in pairs if 0 <= a < layers and 0 <= b < layers for r in range(rows)
        ]
        return lax.ppermute(block, AXES, hops) if hops else None

    def swapped(shards, among=None):
        out = []
        for flip, shard in shards:
            out += [(flip, shard), (flip ^ 1, move(shard, among or every, 1))]
        return out

    def direct(block, pairs):
        return [(flip, move(block, pairs, flip)) for flip in range(0, rows, 2)]

    def within(block, among=None):
        return [(0, block)] + [(flip, move(block, among or every, flip)) for flip in range(2, rows, 2)]

    def apply(starts, sign, *mats_pieces, level=0):
        early = [(m, f, p) for m, ps in mats_pieces for f, p in ps[:2]]
        late = [(m, f, p) for m, ps in mats_pieces for f, p in ps[2:]]
        start = combine(starts, early, sign, level)
        return combine([start], late, sign, level) if late else start

    every = [(i, i) for i in range(layers)]
    current = right_side[0]

    odd = range(1, layers, 2)
    upper = move(current, [(i, i - 1) for i in odd])
    passed = [(flip, move(current, [(i, i + 2) for i in odd], flip)) for flip in range(2, rows, 2)]
    reduce_mats, solve_mats = load(reduce_factors[:, 0], solve_factors[0])
    upper, reduce_mats, solve_mats = lax.optimization_barrier((upper, reduce_mats, solve_mats))
    upper_shards = [(0, upper)] + [(flip, move(upper, [(i - 1, i - 1) for i in odd], flip)) for flip in range(2, rows, 2)]
    lower_shards = [(0, move(upper, [(i - 1, i + 1) for i in odd]))]
    lower_shards += [(flip, move(block, [(i, i - 1) for i in odd])) for flip, block in passed]
    left, right = reduce_mats[0]
    lower, upper = swapped(lower_shards), swapped(upper_shards)
    current = combine([current], [(right, f, p) for f, p in upper[:2]] + [(left, f, p) for f, p in lower[2:]], -1)
    current = combine([current], [(left, f, p) for f, p in lower[:2]] + [(right, f, p) for f, p in upper[2:]], -1)

    inverse, west, east = solve_mats
    for k in range(1, levels - 1):
        stride = 1 << k
        senders = range(stride, layers, 2 * stride)
        left, right = reduce_mats[k]
        lower = swapped(direct(current, [(i, i + stride) for i in senders]))
        upper = swapped(direct(current, [(i, i - stride) for i in senders]))
        current = combine([current], [(left, f, p) for f, p in lower], -1)
        current = combine([current], [(right, f, p) for f, p in upper], -1)

    upper = swapped(direct(current, [(layers // 2, 0)]))
    current = apply([current], -1, (reduce_mats[levels - 1][1], upper))
    base = apply([], 1, (inverse, swapped(within(current))))

    result = base
    for k in reversed(range(levels)):
        stride = 1 << k
        senders = range(0, layers, 2 * stride)
        lower = swapped(direct(result, [(j, j + stride) for j in senders]))
        if k == levels - 1:
            result = apply([base], -1, (west, lower))
        else:
            upper = swapped(direct(result, [(j, j - stride) for j in senders]))
            result = apply([base, result], -1, (west, lower), (east, upper), level=k)
    return result[None]


def solution(mesh):
    placed = (
        P("layer", "row", None),
        P(None, "layer", None, "row", None),
        P("layer", None, "row", None),
    )
    return jax.shard_map(
        functools.partial(on_device, mesh.shape["layer"], mesh.shape["row"]),
        mesh=mesh, in_specs=placed, out_specs=P("layer", "row", None), check_vma=False,
    )
```

time: 428 us -> 146 us (0.34)
  waiting for transfers between devices: 341 us -> 96 us
  matrix products: 30.4 us -> 0 us
  between operations: 13.7 us -> 0.41 us
  Pallas kernels: 0 us -> 9.77 us
  starting transfers between devices: 39.3 us -> 32.8 us
    all_gather x7 -> x0, waiting for transfers between devices: 122 us -> none  [the longest x6 104 us: neighbour_terms(): whole = lax.all_gather(vectors, 'row', axis=1, tiled=True)]
    ppermute x12 -> x44, waiting for transfers between devices: 218 us -> 96 us  [move(): return lax.ppermute(block, AXES, hops) if hops else None]
    dot_general x13 -> x0, matrix products: 30.4 us -> none  [product_of(): jnp.dot(left, right, precision=lax.Precision.HIGHEST, preferred_element_t...]
    pallas_call x0 -> x15, Pallas kernels: none -> 9.77 us  [the longest x14 8.03 us: combine(): pl.pallas_call(functools.partial(combine_kernel, shape, sign, level), out...]
    ppermute x12 -> x44, starting transfers between devices: 38.9 us -> 32.8 us  [move(): return lax.ppermute(block, AXES, hops) if hops else None]
    unnamed x4 -> x6, local copies, waits for them, and re-layouts: 0.01 us -> 4.67 us
  transfers between devices with their start and end apart: 19 -> 44, of which waited for: 16 -> 21; matrix products, arithmetic and copies ran while one was open for 3% -> 0% of each run, Pallas kernels for 0% -> 4%
where the time goes in v2:
time: 146 us; the launch traced here: 144 us
  waiting for transfers between devices  96 us (66%)
  starting transfers between devices  32.8 us (22%)
  Pallas kernels  9.77 us (7%)
  local copies, waits for them, and re-layouts  4.67 us (3%)
    ppermute x44, waiting for transfers between devices, move(): return lax.ppermute(block, AXES, hops) if hops else None  96 us
    ppermute x44, starting transfers between devices, move(): return lax.ppermute(block, AXES, hops) if hops else None  32.8 us
    pallas_call x14, Pallas kernels, combine(): pl.pallas_call(functools.partial(combine_kernel, shape, sign, level), out...  8.03 us
    unnamed x6, local copies, waits for them, and re-layouts  4.67 us
  transfers between devices with their start and end apart: 44, of which 21 were waited for; matrix products, arithmetic and copies ran while one was open for 0% of the time, Pallas kernels for 4%

profile of v2, /device:TPU:8, one launch (start us, length us, event | category | flops | bytes accessed | tf_op | source)
XLA Modules:
  0.0 143.6 jit_solution(13177994013943287372)
XLA Ops:
  0.0 0.7 collective-permute-start.2
  0.7 1.3 collective-permute-start
  2.0 1.3 collective-permute-start.3
  3.3 2.8 %copy-done = f32[3,1,2,256,1024]{4,3,2,1,0:T(8,128)S(1)} copy-done((f32[3,1,2,256,1024]{4,3,2,1,0:T(8,128)S(1)}, f32[3,1,2,256,1024]{4,3,2,1,0:T(8,128)}, u32[]{:S(2)}) %copy-start) | copy-done | bytes 6291480
  6.1 1.9 %copy-done.1 = f32[1,3,256,1024]{3,2,1,0:T(8,128)S(1)} copy-done((f32[1,3,256,1024]{3,2,1,0:T(8,128)S(1)}, f32[1,3,256,1024]{3,2,1,0:T(8,128)}, u32[]{:S(2)}) %copy-start.1) | copy-done | bytes 3145752
  8.0 1.7 %shard_map.37 = (f32[256,1024]{1,0:T(8,128)S(1)}, f32[256,1024]{1,0:T(8,128)S(1)}, f32[256,1024]{1,0:T(8,128)S(1)}, f32[256,1024]{1,0:T(8,128)S(1)}, f32[256,102...) custom-call(f32[3,2,256,1024]{3,2,1,0:T(8,128)S(1)} %bitcast.4, ...), custom_call_target="tpu_custom_call" | custom-call | tf_op jit(solution)/shard_map/pallas_call | solution.py:86
  9.7 3.7 %collective-permute-done.refs_2_ = f32[256,256]{1,0:T(8,128)S(1)} collective-permute-done((f32[256,256]{1,0:T(8,128)}, f32[256,256]{1,0:T(8,128)S(1)}, u32[]{:S(2)}, u32[]{:S(2)}) %collective-permute-start) | collective-permute-done | bytes 262176 | tf_op jit(solution)/shard_map/ppermute | solution.py:105
  13.4 3.5 %collective-permute-start.5 = (f32[256,256]{1,0:T(8,128)S(1)}, f32[256,256]{1,0:T(8,128)S(1)}, u32[]{:S(2)}, u32[]{:S(2)}) collective-permute-start(f32[256,256]{1,0:T(8,128)S(1)} %collective-permute-done.refs_2_), channel_id=1, source_target_pairs={{0,8},{1,9},{2,10},{3,11},{8,16},{9,17},{10,18},{11,19},{16,24},{1... | collective-permute-start | bytes 786440 | tf_op jit(solution)/shard_map/ppermute | solution.py:105
  16.9 2.4 %collective-permute-start.7 = (f32[256,256]{1,0:T(8,128)S(1)}, f32[256,256]{1,0:T(8,128)S(1)}, u32[]{:S(2)}, u32[]{:S(2)}) collective-permute-start(f32[256,256]{1,0:T(8,128)S(1)} %collective-permute-done.refs_2_), channel_id=1, source_target_pairs={{0,2},{1,3},{2,0},{3,1},{8,10},{9,11},{10,8},{11,9},{16,18},{17,19... | collective-permute-start | bytes 786440 | tf_op jit(solution)/shard_map/ppermute | solution.py:105
  19.9 2.6 %collective-permute-done.5.refs_2_ = f32[256,256]{1,0:T(8,128)S(1)} collective-permute-done((f32[256,256]{1,0:T(8,128)S(1)}, f32[256,256]{1,0:T(8,128)S(1)}, u32[]{:S(2)}, u32[]{:S(2)}) %collective-permute-start.5) | collective-permute-done | bytes 262176 | tf_op jit(solution)/shard_map/ppermute | solution.py:105
  22.5 3.2 %collective-permute-done.7.refs_5_ = f32[256,256]{1,0:T(8,128)S(1)} collective-permute-done((f32[256,256]{1,0:T(8,128)S(1)}, f32[256,256]{1,0:T(8,128)S(1)}, u32[]{:S(2)}, u32[]{:S(2)}) %collective-permute-start.7) | collective-permute-done | bytes 262176 | tf_op jit(solution)/shard_map/ppermute | solution.py:105
  25.7 0.6 shard_map.38.refs_0_
  26.4 0.9 collective-permute-done.8.refs_6_
  27.2 0.6 shard_map.39.refs_0_
  27.9 2.2 %collective-permute-start.9 = (f32[256,256]{1,0:T(8,128)S(1)}, f32[256,256]{1,0:T(8,128)S(1)}, u32[]{:S(2)}, u32[]{:S(2)}) collective-permute-start(f32[256,256]{1,0:T(8,128)S(1)} %shard_map.39.refs_0_), channel_id=1, source_target_pairs={{8,16},{9,17},{10,18},{11,19}} | collective-permute-start | bytes 786440 | tf_op jit(solution)/shard_map/ppermute | solution.py:105
  30.1 1.3 collective-permute-start.11
  31.4 1.3 collective-permute-start.13
  32.7 1.3 collective-permute-start.15
  34.0 2.7 %collective-permute-done.9.refs_2_ = f32[256,256]{1,0:T(8,128)S(1)} collective-permute-done((f32[256,256]{1,0:T(8,128)S(1)}, f32[256,256]{1,0:T(8,128)S(1)}, u32[]{:S(2)}, u32[]{:S(2)}) %collective-permute-start.9) | collective-permute-done | bytes 262176 | tf_op jit(solution)/shard_map/ppermute | solution.py:105
  36.7 7.1 %collective-permute-done.11.refs_4_ = f32[256,256]{1,0:T(8,128)S(1)} collective-permute-done((f32[256,256]{1,0:T(8,128)S(1)}, f32[256,256]{1,0:T(8,128)S(1)}, u32[]{:S(2)}, u32[]{:S(2)}) %collective-permute-start.11) | collective-permute-done | bytes 262176 | tf_op jit(solution)/shard_map/ppermute | solution.py:105
  44.5 0.9 collective-permute-done.12.refs_5_
  46.8 0.7 collective-permute-start.17
  47.5 0.7 collective-permute-start.19
  48.7 1.0 collective-permute-done.18.refs_3_
  50.6 1.0 collective-permute-start.22
  51.6 7.3 %collective-permute-done.22.refs_2_ = f32[256,256]{1,0:T(8,128)S(1)} collective-permute-done((f32[256,256]{1,0:T(8,128)S(1)}, f32[256,256]{1,0:T(8,128)S(1)}, u32[]{:S(2)}, u32[]{:S(2)}) %collective-permute-start.22) | collective-permute-done | bytes 262176 | tf_op jit(solution)/shard_map/ppermute | solution.py:105
  59.4 1.1 collective-permute-done.23.refs_3_
  60.9 0.7 collective-permute-start.24
  61.6 0.7 collective-permute-start.26
  62.9 1.0 collective-permute-done.25.refs_3_
  64.7 1.3 collective-permute-start.28
  66.0 1.3 collective-permute-start.30
  67.3 1.3 collective-permute-start.32
  68.6 1.3 collective-permute-start.34
  69.9 33.3 %collective-permute-done.28.refs_3_ = f32[256,256]{1,0:T(8,128)S(1)} collective-permute-done((f32[256,256]{1,0:T(8,128)S(1)}, f32[256,256]{1,0:T(8,128)S(1)}, u32[]{:S(2)}, u32[]{:S(2)}) %collective-permute-start.28) | collective-permute-done | bytes 262176 | tf_op jit(solution)/shard_map/ppermute | solution.py:105
  103.3 3.2 %collective-permute-done.30.refs_6_ = f32[256,256]{1,0:T(8,128)S(1)} collective-permute-done((f32[256,256]{1,0:T(8,128)S(1)}, f32[256,256]{1,0:T(8,128)S(1)}, u32[]{:S(2)}, u32[]{:S(2)}) %collective-permute-start.30) | collective-permute-done | bytes 262176 | tf_op jit(solution)/shard_map/ppermute | solution.py:105
  106.5 3.3 %collective-permute-done.32.refs_2_ = f32[256,256]{1,0:T(8,128)S(1)} collective-permute-done((f32[256,256]{1,0:T(8,128)S(1)}, f32[256,256]{1,0:T(8,128)S(1)}, u32[]{:S(2)}, u32[]{:S(2)}) %collective-permute-start.32) | collective-permute-done | bytes 262176 | tf_op jit(solution)/shard_map/ppermute | solution.py:105
  109.8 4.2 %collective-permute-done.34.refs_5_ = f32[256,256]{1,0:T(8,128)S(1)} collective-permute-done((f32[256,256]{1,0:T(8,128)S(1)}, f32[256,256]{1,0:T(8,128)S(1)}, u32[]{:S(2)}, u32[]{:S(2)}) %collective-permute-start.34) | collective-permute-done | bytes 262176 | tf_op jit(solution)/shard_map/ppermute | solution.py:105
  114.0 0.6 shard_map.48.refs_0_
  114.6 0.9 collective-permute-done.35.refs_6_
  116.1 1.3 collective-permute-start.36
  117.4 1.3 collective-permute-start.38
  118.8 1.3 collective-permute-start.40
  120.1 1.3 collective-permute-start.42
  121.4 13.7 %collective-permute-done.36.refs_3_ = f32[256,256]{1,0:T(8,128)S(1)} collective-permute-done((f32[256,256]{1,0:T(8,128)S(1)}, f32[256,256]{1,0:T(8,128)S(1)}, u32[]{:S(2)}, u32[]{:S(2)}) %collective-permute-start.36) | collective-permute-done | bytes 262176 | tf_op jit(solution)/shard_map/ppermute | solution.py:105
  135.6 4.8 %collective-permute-done.40.refs_2_ = f32[256,256]{1,0:T(8,128)S(1)} collective-permute-done((f32[256,256]{1,0:T(8,128)S(1)}, f32[256,256]{1,0:T(8,128)S(1)}, u32[]{:S(2)}, u32[]{:S(2)}) %collective-permute-start.40) | collective-permute-done | bytes 262176 | tf_op jit(solution)/shard_map/ppermute | solution.py:105
  140.9 0.6 shard_map.50.refs_0_
  142.3 1.3 shard_map.51
  (61 shorter events, 8.5 us)
Async XLA Ops:
  0.0 2.0 %collective-permute-start.2 = (f32[256,256]{1,0:T(8,128)}, f32[256,256]{1,0:T(8,128)S(1)}, u32[]{:S(2)}, u32[]{:S(2)}) collective-permute-start(f32[256,256]{1,0:T(8,128)} %bitcast.6), channel_id=1, source_target_pairs={{4,14},{5,15},{6,12},{7,13},{12,22},{13,23},{14,20},{15,21},{20,30... | collective-permute-start | bytes 786440 | tf_op jit(solution)/shard_map/ppermute | solution.py:105
  0.7 12.8 %collective-permute-start = (f32[256,256]{1,0:T(8,128)}, f32[256,256]{1,0:T(8,128)S(1)}, u32[]{:S(2)}, u32[]{:S(2)}) collective-permute-start(f32[256,256]{1,0:T(8,128)} %bitcast.7), channel_id=1, source_target_pairs={{4,0},{5,1},{6,2},{7,3},{12,8},{13,9},{14,10},{15,11},{20,16},{21,... | collective-permute-start | bytes 786440 | tf_op jit(solution)/shard_map/ppermute | solution.py:105
  2.0 17.4 %collective-permute-start.3 = (f32[256,256]{1,0:T(8,128)S(1)}, f32[256,256]{1,0:T(8,128)S(1)}, u32[]{:S(2)}, u32[]{:S(2)}) collective-permute-start(f32[256,256]{1,0:T(8,128)S(1)} %collective-permute-done.2), channel_id=1, source_target_pairs={{4,0},{5,1},{6,2},{7,3},{12,8},{13,9},{14,10},{15,11},{20,16},{21,... | collective-permute-start | bytes 786440 | tf_op jit(solution)/shard_map/ppermute | solution.py:105
  3.3 2.8 %copy-start = (f32[3,1,2,256,1024]{4,3,2,1,0:T(8,128)S(1)}, f32[3,1,2,256,1024]{4,3,2,1,0:T(8,128)}, u32[]{:S(2)}) copy-start(f32[3,1,2,256,1024]{4,3,2,1,0:T(8,128)} %param.4) | copy-start | bytes 18874372
  6.1 1.9 %copy-start.1 = (f32[1,3,256,1024]{3,2,1,0:T(8,128)S(1)}, f32[1,3,256,1024]{3,2,1,0:T(8,128)}, u32[]{:S(2)}) copy-start(f32[1,3,256,1024]{3,2,1,0:T(8,128)} %param.5) | copy-start | bytes 9437188
  8.0 17.8 %copy-start.2 = (f32[1,256,256]{2,1,0:T(8,128)S(1)}, f32[1,256,256]{2,1,0:T(8,128)}, u32[]{:S(2)}) copy-start(f32[1,256,256]{2,1,0:T(8,128)} %param.3) | copy-start | bytes 786436
  13.4 9.1 %collective-permute-start.5 = (f32[256,256]{1,0:T(8,128)S(1)}, f32[256,256]{1,0:T(8,128)S(1)}, u32[]{:S(2)}, u32[]{:S(2)}) collective-permute-start(f32[256,256]{1,0:T(8,128)S(1)} %collective-permute-done.refs_2_), channel_id=1, source_target_pairs={{0,8},{1,9},{2,10},{3,11},{8,16},{9,17},{10,18},{11,19},{16,24},{1... | collective-permute-start | bytes 786440 | tf_op jit(solution)/shard_map/ppermute | solution.py:105
  16.9 8.8 %collective-permute-start.7 = (f32[256,256]{1,0:T(8,128)S(1)}, f32[256,256]{1,0:T(8,128)S(1)}, u32[]{:S(2)}, u32[]{:S(2)}) collective-permute-start(f32[256,256]{1,0:T(8,128)S(1)} %collective-permute-done.refs_2_), channel_id=1, source_target_pairs={{0,2},{1,3},{2,0},{3,1},{8,10},{9,11},{10,8},{11,9},{16,18},{17,19... | collective-permute-start | bytes 786440 | tf_op jit(solution)/shard_map/ppermute | solution.py:105
  19.3 6.4 %collective-permute-start.1 = (f32[256,256]{1,0:T(8,128)S(1)}, f32[256,256]{1,0:T(8,128)S(1)}, u32[]{:S(2)}, u32[]{:S(2)}) collective-permute-start(f32[256,256]{1,0:T(8,128)S(1)} %collective-permute-done.refs_2_), channel_id=1, source_target_pairs={{0,1},{1,0},{2,3},{3,2},{4,5},{5,4},{6,7},{7,6},{8,9},{9,8},{10,11... | collective-permute-start | bytes 786440 | tf_op jit(solution)/shard_map/ppermute | solution.py:105
  19.4 6.3 %collective-permute-start.4 = (f32[256,256]{1,0:T(8,128)S(1)}, f32[256,256]{1,0:T(8,128)S(1)}, u32[]{:S(2)}, u32[]{:S(2)}) collective-permute-start(f32[256,256]{1,0:T(8,128)S(1)} %collective-permute-done.3.refs_5_), channel_id=1, source_target_pairs={{0,1},{1,0},{2,3},{3,2},{4,5},{5,4},{6,7},{7,6},{8,9},{9,8},{10,11... | collective-permute-start | bytes 786440 | tf_op jit(solution)/shard_map/ppermute | solution.py:105
  22.5 3.9 %collective-permute-start.6 = (f32[256,256]{1,0:T(8,128)S(1)}, f32[256,256]{1,0:T(8,128)S(1)}, u32[]{:S(2)}, u32[]{:S(2)}) collective-permute-start(f32[256,256]{1,0:T(8,128)S(1)} %collective-permute-done.5.refs_2_), channel_id=1, source_target_pairs={{0,1},{1,0},{2,3},{3,2},{4,5},{5,4},{6,7},{7,6},{8,9},{9,8},{10,11... | collective-permute-start | bytes 786440 | tf_op jit(solution)/shard_map/ppermute | solution.py:105
  25.7 1.5 %collective-permute-start.8 = (f32[256,256]{1,0:T(8,128)S(1)}, f32[256,256]{1,0:T(8,128)S(1)}, u32[]{:S(2)}, u32[]{:S(2)}) collective-permute-start(f32[256,256]{1,0:T(8,128)S(1)} %collective-permute-done.7.refs_5_), channel_id=1, source_target_pairs={{0,1},{1,0},{2,3},{3,2},{4,5},{5,4},{6,7},{7,6},{8,9},{9,8},{10,11... | collective-permute-start | bytes 786440 | tf_op jit(solution)/shard_map/ppermute | solution.py:105
  27.9 8.9 %collective-permute-start.9 = (f32[256,256]{1,0:T(8,128)S(1)}, f32[256,256]{1,0:T(8,128)S(1)}, u32[]{:S(2)}, u32[]{:S(2)}) collective-permute-start(f32[256,256]{1,0:T(8,128)S(1)} %shard_map.39.refs_0_), channel_id=1, source_target_pairs={{8,16},{9,17},{10,18},{11,19}} | collective-permute-start | bytes 786440 | tf_op jit(solution)/shard_map/ppermute | solution.py:105
  30.1 13.8 %collective-permute-start.11 = (f32[256,256]{1,0:T(8,128)S(1)}, f32[256,256]{1,0:T(8,128)S(1)}, u32[]{:S(2)}, u32[]{:S(2)}) collective-permute-start(f32[256,256]{1,0:T(8,128)S(1)} %shard_map.39.refs_0_), channel_id=1, source_target_pairs={{8,18},{9,19},{10,16},{11,17}} | collective-permute-start | bytes 786440 | tf_op jit(solution)/shard_map/ppermute | solution.py:105
  31.4 12.5 %collective-permute-start.13 = (f32[256,256]{1,0:T(8,128)S(1)}, f32[256,256]{1,0:T(8,128)S(1)}, u32[]{:S(2)}, u32[]{:S(2)}) collective-permute-start(f32[256,256]{1,0:T(8,128)S(1)} %shard_map.39.refs_0_), channel_id=1, source_target_pairs={{8,0},{9,1},{10,2},{11,3},{24,16},{25,17},{26,18},{27,19}} | collective-permute-start | bytes 786440 | tf_op jit(solution)/shard_map/ppermute | solution.py:105
  32.7 11.7 %collective-permute-start.15 = (f32[256,256]{1,0:T(8,128)S(1)}, f32[256,256]{1,0:T(8,128)S(1)}, u32[]{:S(2)}, u32[]{:S(2)}) collective-permute-start(f32[256,256]{1,0:T(8,128)S(1)} %shard_map.39.refs_0_), channel_id=1, source_target_pairs={{8,2},{9,3},{10,0},{11,1},{24,18},{25,19},{26,16},{27,17}} | collective-permute-start | bytes 786440 | tf_op jit(solution)/shard_map/ppermute | solution.py:105
  36.7 7.7 %collective-permute-start.10 = (f32[256,256]{1,0:T(8,128)S(1)}, f32[256,256]{1,0:T(8,128)S(1)}, u32[]{:S(2)}, u32[]{:S(2)}) collective-permute-start(f32[256,256]{1,0:T(8,128)S(1)} %collective-permute-done.9.refs_2_), channel_id=1, source_target_pairs={{0,1},{1,0},{2,3},{3,2},{4,5},{5,4},{6,7},{7,6},{8,9},{9,8},{10,11... | collective-permute-start | bytes 786440 | tf_op jit(solution)/shard_map/ppermute | solution.py:105
  43.9 1.5 %collective-permute-start.12 = (f32[256,256]{1,0:T(8,128)S(1)}, f32[256,256]{1,0:T(8,128)S(1)}, u32[]{:S(2)}, u32[]{:S(2)}) collective-permute-start(f32[256,256]{1,0:T(8,128)S(1)} %collective-permute-done.11.refs_4_), channel_id=1, source_target_pairs={{0,1},{1,0},{2,3},{3,2},{4,5},{5,4},{6,7},{7,6},{8,9},{9,8},{10,11... | collective-permute-start | bytes 786440 | tf_op jit(solution)/shard_map/ppermute | solution.py:105
  43.9 2.2 %collective-permute-start.14 = (f32[256,256]{1,0:T(8,128)S(1)}, f32[256,256]{1,0:T(8,128)S(1)}, u32[]{:S(2)}, u32[]{:S(2)}) collective-permute-start(f32[256,256]{1,0:T(8,128)S(1)} %collective-permute-done.13.refs_2_), channel_id=1, source_target_pairs={{0,1},{1,0},{2,3},{3,2},{4,5},{5,4},{6,7},{7,6},{8,9},{9,8},{10,11... | collective-permute-start | bytes 786440 | tf_op jit(solution)/shard_map/ppermute | solution.py:105
  44.4 1.8 %collective-permute-start.16 = (f32[256,256]{1,0:T(8,128)S(1)}, f32[256,256]{1,0:T(8,128)S(1)}, u32[]{:S(2)}, u32[]{:S(2)}) collective-permute-start(f32[256,256]{1,0:T(8,128)S(1)} %collective-permute-done.15.refs_4_), channel_id=1, source_target_pairs={{0,1},{1,0},{2,3},{3,2},{4,5},{5,4},{6,7},{7,6},{8,9},{9,8},{10,11... | collective-permute-start | bytes 786440 | tf_op jit(solution)/shard_map/ppermute | solution.py:105
  46.8 1.4 collective-permute-start.17
  47.5 0.9 collective-permute-start.19
  48.2 1.6 %collective-permute-start.18 = (f32[256,256]{1,0:T(8,128)S(1)}, f32[256,256]{1,0:T(8,128)S(1)}, u32[]{:S(2)}, u32[]{:S(2)}) collective-permute-start(f32[256,256]{1,0:T(8,128)S(1)} %collective-permute-done.17.refs_2_), channel_id=1, source_target_pairs={{0,1},{1,0},{2,3},{3,2},{4,5},{5,4},{6,7},{7,6},{8,9},{9,8},{10,11... | collective-permute-start | bytes 786440 | tf_op jit(solution)/shard_map/ppermute | solution.py:105
  48.4 1.8 %collective-permute-start.20 = (f32[256,256]{1,0:T(8,128)S(1)}, f32[256,256]{1,0:T(8,128)S(1)}, u32[]{:S(2)}, u32[]{:S(2)}) collective-permute-start(f32[256,256]{1,0:T(8,128)S(1)} %collective-permute-done.19.refs_2_), channel_id=1, source_target_pairs={{0,1},{1,0},{2,3},{3,2},{4,5},{5,4},{6,7},{7,6},{8,9},{9,8},{10,11... | collective-permute-start | bytes 786440 | tf_op jit(solution)/shard_map/ppermute | solution.py:105
  50.6 8.4 %collective-permute-start.22 = (f32[256,256]{1,0:T(8,128)S(1)}, f32[256,256]{1,0:T(8,128)S(1)}, u32[]{:S(2)}, u32[]{:S(2)}) collective-permute-start(f32[256,256]{1,0:T(8,128)S(1)} %shard_map.43.refs_1_), channel_id=1, source_target_pairs={{0,2},{1,3},{2,0},{3,1},{4,6},{5,7},{6,4},{7,5},{8,10},{9,11},{10,... | collective-permute-start | bytes 786440 | tf_op jit(solution)/shard_map/ppermute | solution.py:105
  51.6 7.4 %collective-permute-start.21 = (f32[256,256]{1,0:T(8,128)S(1)}, f32[256,256]{1,0:T(8,128)S(1)}, u32[]{:S(2)}, u32[]{:S(2)}) collective-permute-start(f32[256,256]{1,0:T(8,128)S(1)} %shard_map.43.refs_1_), channel_id=1, source_target_pairs={{0,1},{1,0},{2,3},{3,2},{4,5},{5,4},{6,7},{7,6},{8,9},{9,8},{10,11... | collective-permute-start | bytes 786440 | tf_op jit(solution)/shard_map/ppermute | solution.py:105
  59.0 1.5 %collective-permute-start.23 = (f32[256,256]{1,0:T(8,128)S(1)}, f32[256,256]{1,0:T(8,128)S(1)}, u32[]{:S(2)}, u32[]{:S(2)}) collective-permute-start(f32[256,256]{1,0:T(8,128)S(1)} %collective-permute-done.22.refs_2_), channel_id=1, source_target_pairs={{0,1},{1,0},{2,3},{3,2},{4,5},{5,4},{6,7},{7,6},{8,9},{9,8},{10,11... | collective-permute-start | bytes 786440 | tf_op jit(solution)/shard_map/ppermute | solution.py:105
  60.9 1.4 collective-permute-start.24
  61.6 0.9 collective-permute-start.26
  62.3 1.6 %collective-permute-start.25 = (f32[256,256]{1,0:T(8,128)S(1)}, f32[256,256]{1,0:T(8,128)S(1)}, u32[]{:S(2)}, u32[]{:S(2)}) collective-permute-start(f32[256,256]{1,0:T(8,128)S(1)} %collective-permute-done.24.refs_2_), channel_id=1, source_target_pairs={{0,1},{1,0},{2,3},{3,2},{4,5},{5,4},{6,7},{7,6},{8,9},{9,8},{10,11... | collective-permute-start | bytes 786440 | tf_op jit(solution)/shard_map/ppermute | solution.py:105
  62.5 1.8 %collective-permute-start.27 = (f32[256,256]{1,0:T(8,128)S(1)}, f32[256,256]{1,0:T(8,128)S(1)}, u32[]{:S(2)}, u32[]{:S(2)}) collective-permute-start(f32[256,256]{1,0:T(8,128)S(1)} %collective-permute-done.26.refs_2_), channel_id=1, source_target_pairs={{0,1},{1,0},{2,3},{3,2},{4,5},{5,4},{6,7},{7,6},{8,9},{9,8},{10,11... | collective-permute-start | bytes 786440 | tf_op jit(solution)/shard_map/ppermute | solution.py:105
  64.7 38.5 %collective-permute-start.28 = (f32[256,256]{1,0:T(8,128)S(1)}, f32[256,256]{1,0:T(8,128)S(1)}, u32[]{:S(2)}, u32[]{:S(2)}) collective-permute-start(f32[256,256]{1,0:T(8,128)S(1)} %shard_map.47.refs_1_), channel_id=1, source_target_pairs={{0,8},{1,9},{2,10},{3,11},{16,24},{17,25},{18,26},{19,27}} | collective-permute-start | bytes 786440 | tf_op jit(solution)/shard_map/ppermute | solution.py:105
  66.0 40.4 %collective-permute-start.30 = (f32[256,256]{1,0:T(8,128)S(1)}, f32[256,256]{1,0:T(8,128)S(1)}, u32[]{:S(2)}, u32[]{:S(2)}) collective-permute-start(f32[256,256]{1,0:T(8,128)S(1)} %shard_map.47.refs_1_), channel_id=1, source_target_pairs={{16,8},{17,9},{18,10},{19,11}} | collective-permute-start | bytes 786440 | tf_op jit(solution)/shard_map/ppermute | solution.py:105
  67.3 42.4 %collective-permute-start.32 = (f32[256,256]{1,0:T(8,128)S(1)}, f32[256,256]{1,0:T(8,128)S(1)}, u32[]{:S(2)}, u32[]{:S(2)}) collective-permute-start(f32[256,256]{1,0:T(8,128)S(1)} %shard_map.47.refs_1_), channel_id=1, source_target_pairs={{0,10},{1,11},{2,8},{3,9},{16,26},{17,27},{18,24},{19,25}} | collective-permute-start | bytes 786440 | tf_op jit(solution)/shard_map/ppermute | solution.py:105
  68.6 45.3 %collective-permute-start.34 = (f32[256,256]{1,0:T(8,128)S(1)}, f32[256,256]{1,0:T(8,128)S(1)}, u32[]{:S(2)}, u32[]{:S(2)}) collective-permute-start(f32[256,256]{1,0:T(8,128)S(1)} %shard_map.47.refs_1_), channel_id=1, source_target_pairs={{16,10},{17,11},{18,8},{19,9}} | collective-permute-start | bytes 786440 | tf_op jit(solution)/shard_map/ppermute | solution.py:105
  103.3 10.7 %collective-permute-start.29 = (f32[256,256]{1,0:T(8,128)S(1)}, f32[256,256]{1,0:T(8,128)S(1)}, u32[]{:S(2)}, u32[]{:S(2)}) collective-permute-start(f32[256,256]{1,0:T(8,128)S(1)} %collective-permute-done.28.refs_3_), channel_id=1, source_target_pairs={{0,1},{1,0},{2,3},{3,2},{4,5},{5,4},{6,7},{7,6},{8,9},{9,8},{10,11... | collective-permute-start | bytes 786440 | tf_op jit(solution)/shard_map/ppermute | solution.py:105
  106.4 7.5 %collective-permute-start.31 = (f32[256,256]{1,0:T(8,128)S(1)}, f32[256,256]{1,0:T(8,128)S(1)}, u32[]{:S(2)}, u32[]{:S(2)}) collective-permute-start(f32[256,256]{1,0:T(8,128)S(1)} %collective-permute-done.30.refs_6_), channel_id=1, source_target_pairs={{0,1},{1,0},{2,3},{3,2},{4,5},{5,4},{6,7},{7,6},{8,9},{9,8},{10,11... | collective-permute-start | bytes 786440 | tf_op jit(solution)/shard_map/ppermute | solution.py:105
  109.8 4.8 %collective-permute-start.33 = (f32[256,256]{1,0:T(8,128)S(1)}, f32[256,256]{1,0:T(8,128)S(1)}, u32[]{:S(2)}, u32[]{:S(2)}) collective-permute-start(f32[256,256]{1,0:T(8,128)S(1)} %collective-permute-done.32.refs_2_), channel_id=1, source_target_pairs={{0,1},{1,0},{2,3},{3,2},{4,5},{5,4},{6,7},{7,6},{8,9},{9,8},{10,11... | collective-permute-start | bytes 786440 | tf_op jit(solution)/shard_map/ppermute | solution.py:105
  114.0 1.5 %collective-permute-start.35 = (f32[256,256]{1,0:T(8,128)S(1)}, f32[256,256]{1,0:T(8,128)S(1)}, u32[]{:S(2)}, u32[]{:S(2)}) collective-permute-start(f32[256,256]{1,0:T(8,128)S(1)} %collective-permute-done.34.refs_5_), channel_id=1, source_target_pairs={{0,1},{1,0},{2,3},{3,2},{4,5},{5,4},{6,7},{7,6},{8,9},{9,8},{10,11... | collective-permute-start | bytes 786440 | tf_op jit(solution)/shard_map/ppermute | solution.py:105
  116.1 19.0 %collective-permute-start.36 = (f32[256,256]{1,0:T(8,128)S(1)}, f32[256,256]{1,0:T(8,128)S(1)}, u32[]{:S(2)}, u32[]{:S(2)}) collective-permute-start(f32[256,256]{1,0:T(8,128)S(1)} %shard_map.49.refs_1_), channel_id=1, source_target_pairs={{0,4},{1,5},{2,6},{3,7},{8,12},{9,13},{10,14},{11,15},{16,20},{17,... | collective-permute-start | bytes 786440 | tf_op jit(solution)/shard_map/ppermute | solution.py:105
  117.4 17.7 %collective-permute-start.38 = (f32[256,256]{1,0:T(8,128)S(1)}, f32[256,256]{1,0:T(8,128)S(1)}, u32[]{:S(2)}, u32[]{:S(2)}) collective-permute-start(f32[256,256]{1,0:T(8,128)S(1)} %shard_map.49.refs_1_), channel_id=1, source_target_pairs={{8,4},{9,5},{10,6},{11,7},{16,12},{17,13},{18,14},{19,15},{24,20},... | collective-permute-start | bytes 786440 | tf_op jit(solution)/shard_map/ppermute | solution.py:105
  118.8 21.6 %collective-permute-start.40 = (f32[256,256]{1,0:T(8,128)S(1)}, f32[256,256]{1,0:T(8,128)S(1)}, u32[]{:S(2)}, u32[]{:S(2)}) collective-permute-start(f32[256,256]{1,0:T(8,128)S(1)} %shard_map.49.refs_1_), channel_id=1, source_target_pairs={{0,6},{1,7},{2,4},{3,5},{8,14},{9,15},{10,12},{11,13},{16,22},{17,... | collective-permute-start | bytes 786440 | tf_op jit(solution)/shard_map/ppermute | solution.py:105
  120.1 20.3 %collective-permute-start.42 = (f32[256,256]{1,0:T(8,128)S(1)}, f32[256,256]{1,0:T(8,128)S(1)}, u32[]{:S(2)}, u32[]{:S(2)}) collective-permute-start(f32[256,256]{1,0:T(8,128)S(1)} %shard_map.49.refs_1_), channel_id=1, source_target_pairs={{8,6},{9,7},{10,4},{11,5},{16,14},{17,15},{18,12},{19,13},{24,22},... | collective-permute-start | bytes 786440 | tf_op jit(solution)/shard_map/ppermute | solution.py:105
  135.1 5.8 %collective-permute-start.37 = (f32[256,256]{1,0:T(8,128)S(1)}, f32[256,256]{1,0:T(8,128)S(1)}, u32[]{:S(2)}, u32[]{:S(2)}) collective-permute-start(f32[256,256]{1,0:T(8,128)S(1)} %collective-permute-done.36.refs_3_), channel_id=1, source_target_pairs={{0,1},{1,0},{2,3},{3,2},{4,5},{5,4},{6,7},{7,6},{8,9},{9,8},{10,11... | collective-permute-start | bytes 786440 | tf_op jit(solution)/shard_map/ppermute | solution.py:105
  135.1 5.8 %collective-permute-start.39 = (f32[256,256]{1,0:T(8,128)S(1)}, f32[256,256]{1,0:T(8,128)S(1)}, u32[]{:S(2)}, u32[]{:S(2)}) collective-permute-start(f32[256,256]{1,0:T(8,128)S(1)} %collective-permute-done.38.refs_6_), channel_id=1, source_target_pairs={{0,1},{1,0},{2,3},{3,2},{4,5},{5,4},{6,7},{7,6},{8,9},{9,8},{10,11... | collective-permute-start | bytes 786440 | tf_op jit(solution)/shard_map/ppermute | solution.py:105
  140.4 1.5 %collective-permute-start.41 = (f32[256,256]{1,0:T(8,128)S(1)}, f32[256,256]{1,0:T(8,128)S(1)}, u32[]{:S(2)}, u32[]{:S(2)}) collective-permute-start(f32[256,256]{1,0:T(8,128)S(1)} %collective-permute-done.40.refs_2_), channel_id=1, source_target_pairs={{0,1},{1,0},{2,3},{3,2},{4,5},{5,4},{6,7},{7,6},{8,9},{9,8},{10,11... | collective-permute-start | bytes 786440 | tf_op jit(solution)/shard_map/ppermute | solution.py:105
  140.4 1.9 %collective-permute-start.43 = (f32[256,256]{1,0:T(8,128)S(1)}, f32[256,256]{1,0:T(8,128)S(1)}, u32[]{:S(2)}, u32[]{:S(2)}) collective-permute-start(f32[256,256]{1,0:T(8,128)S(1)} %collective-permute-done.42.refs_5_), channel_id=1, source_target_pairs={{0,1},{1,0},{2,3},{3,2},{4,5},{5,4},{6,7},{7,6},{8,9},{9,8},{10,11... | collective-permute-start | bytes 786440 | tf_op jit(solution)/shard_map/ppermute | solution.py:105

commit v3 on v2

--- a/solution.py
+++ b/solution.py
@@ -23,27 +23,28 @@
     return dot(left_high, right_high) + (dot(left_high, right_low) + dot(left_low, right_high))
 
 
-def combine_kernel(shape, sign, level, *refs):
+def combine_kernel(shape, sign, only, *refs):
     out_ref = refs[-1]
     count = out_ref.shape[0]
     row = lax.axis_index("row")
     layer = lax.axis_index("layer")
     starts, terms = shape
-    if len(starts) == 2:
-        total = jnp.where(layer % (2 << level) == (1 << level), refs[starts[0]][...], refs[starts[1]][...])
-    else:
-        total = refs[starts[0]][...] if starts else None
-    for matrix, flip, vector in terms:
+    total = refs[starts[0]][...] if starts else None
+    for matrix, flip, vector, within in terms:
         columns = pl.ds(pl.multiple_of((row ^ flip) * count, count), count)
         term = product(refs[matrix][:, columns], refs[vector][...])
+        if within is not None:
+            term = jnp.where((layer >= within[0]) & (layer < within[1]), term, 0.0)
         if total is None:
             total = term if sign > 0 else -term
         else:
             total = total + term if sign > 0 else total - term
+    if only is not None:
+        total = jnp.where(layer % only[0] == only[1], total, refs[starts[-1]][...])
     out_ref[...] = total
 
 
-def combine(starts, terms, sign, level=0):
+def combine(starts, terms, sign, only=None):
     operands = []
 
     def place(array):
@@ -55,11 +56,11 @@
 
     shape = (
         [place(s) for s in starts],
-        [(place(matrix), flip, place(vector)) for matrix, flip, vector in terms],
+        [(place(t[0]), t[1], place(t[2]), t[3] if len(t) > 3 else None) for t in terms],
     )
     out = jax.ShapeDtypeStruct(terms[0][2].shape, terms[0][2].dtype)
     return pl.pallas_call(
-        functools.partial(combine_kernel, shape, sign, level),
+        functools.partial(combine_kernel, shape, sign, only),
         out_shape=out,
         in_specs=[VMEM] * len(operands),
         out_specs=VMEM,
@@ -116,27 +117,36 @@
     def within(block, among=None):
         return [(0, block)] + [(flip, move(block, among or every, flip)) for flip in range(2, rows, 2)]
 
-    def apply(starts, sign, *mats_pieces, level=0):
+    def apply(starts, sign, *mats_pieces, only=None):
         early = [(m, f, p) for m, ps in mats_pieces for f, p in ps[:2]]
         late = [(m, f, p) for m, ps in mats_pieces for f, p in ps[2:]]
-        start = combine(starts, early, sign, level)
-        return combine([start], late, sign, level) if late else start
+        start = combine(starts, early, sign, only)
+        return combine([start], late, sign, only) if late else start
+
+    def ring(by):
+        return [(i, (i + by) % layers) for i in range(layers)]
 
     every = [(i, i) for i in range(layers)]
     current = right_side[0]
 
-    odd = range(1, layers, 2)
-    upper = move(current, [(i, i - 1) for i in odd])
-    passed = [(flip, move(current, [(i, i + 2) for i in odd], flip)) for flip in range(2, rows, 2)]
+    def hop(block, by):
+        return move(block, [(i, i - by) for i in range(1 if by > 0 else 0, layers, 2)])
+
+    def near_shards(near):
+        return within(near)
+
+    def far_shards(near, passed, by):
+        return [(0, move(near, ring(2 * by)))] + [(flip, hop(shard, by)) for flip, shard in passed]
+
+    upper = hop(current, 1)
+    passed = [(flip, move(current, ring(2), flip)) for flip in range(2, rows, 2)]
     reduce_mats, solve_mats = load(reduce_factors[:, 0], solve_factors[0])
     upper, reduce_mats, solve_mats = lax.optimization_barrier((upper, reduce_mats, solve_mats))
-    upper_shards = [(0, upper)] + [(flip, move(upper, [(i - 1, i - 1) for i in odd], flip)) for flip in range(2, rows, 2)]
-    lower_shards = [(0, move(upper, [(i - 1, i + 1) for i in odd]))]
-    lower_shards += [(flip, move(block, [(i, i - 1) for i in odd])) for flip, block in passed]
     left, right = reduce_mats[0]
-    lower, upper = swapped(lower_shards), swapped(upper_shards)
-    current = combine([current], [(right, f, p) for f, p in upper[:2]] + [(left, f, p) for f, p in lower[2:]], -1)
-    current = combine([current], [(left, f, p) for f, p in lower[:2]] + [(right, f, p) for f, p in upper[2:]], -1)
+    lower, upper = swapped(far_shards(upper, passed, 1)), swapped(near_shards(upper))
+    current = combine(
+        [current], [(right, f, p) for f, p in upper] + [(left, f, p, (1, layers)) for f, p in lower], -1, (2, 0)
+    )
 
     inverse, west, east = solve_mats
     for k in range(1, levels - 1):
@@ -155,13 +165,23 @@
     result = base
     for k in reversed(range(levels)):
         stride = 1 << k
+        only = (2 * stride, stride)
         senders = range(0, layers, 2 * stride)
-        lower = swapped(direct(result, [(j, j + stride) for j in senders]))
         if k == levels - 1:
-            result = apply([base], -1, (west, lower))
+            result = apply([base, result], -1, (west, swapped(direct(result, [(0, stride)]))), only=only)
+        elif k > 0:
+            lower = swapped(direct(result, [(j, j + stride) for j in senders]))
+            upper = swapped(direct(result, [(j, j - stride) for j in senders]))
+            result = apply([base, result], -1, (west, lower), (east, upper), only=only)
         else:
-            upper = swapped(direct(result, [(j, j - stride) for j in senders]))
-            result = apply([base, result], -1, (west, lower), (east, upper), level=k)
+            lower = hop(result, -1)
+            passed = [(flip, move(result, ring(-2), flip)) for flip in range(2, rows, 2)]
+            upper = swapped(far_shards(lower, passed, -1))
+            lower = swapped(near_shards(lower))
+            result = combine(
+                [base, result],
+                [(west, f, p) for f, p in lower] + [(east, f, p, (0, layers - 1)) for f, p in upper], -1, only,
+            )
     return result[None]
 
 

time: 146 us -> 139 us (0.952)
  waiting for transfers between devices: 96 us -> 89.1 us
    ppermute x44 -> x45, waiting for transfers between devices: 96 us -> 89.1 us  [move(): return lax.ppermute(block, AXES, hops) if hops else None]
    pallas_call x14 -> x12, Pallas kernels: 8.03 us -> 7.68 us  [combine(): pl.pallas_call(functools.partial(combine_kernel, shape, sign, only), out_...]
    ppermute x44 -> x45, starting transfers between devices: 32.8 us -> 32.8 us  [move(): return lax.ppermute(block, AXES, hops) if hops else None]
  transfers between devices with their start and end apart: 44 -> 45, of which waited for: 21 -> 24; matrix products, arithmetic and copies ran while one was open for 0% -> 0% of each run, Pallas kernels for 4% -> 3%
where the time goes in v3:
time: 139 us; the launch traced here: 136 us
  waiting for transfers between devices  89.1 us (64%)
  starting transfers between devices  32.8 us (24%)
  Pallas kernels  9.41 us (7%)
  local copies, waits for them, and re-layouts  4.68 us (3%)
    ppermute x45, waiting for transfers between devices, move(): return lax.ppermute(block, AXES, hops) if hops else None  89.1 us
    ppermute x45, starting transfers between devices, move(): return lax.ppermute(block, AXES, hops) if hops else None  32.8 us
    pallas_call x12, Pallas kernels, combine(): pl.pallas_call(functools.partial(combine_kernel, shape, sign, only), out_...  7.68 us
    unnamed x6, local copies, waits for them, and re-layouts  4.68 us
  transfers between devices with their start and end apart: 45, of which 24 were waited for; matrix products, arithmetic and copies ran while one was open for 0% of the time, Pallas kernels for 3%

profile of v3, /device:TPU:8, one launch (start us, length us, event | category | flops | bytes accessed | tf_op | source)
XLA Modules:
  0.0 136.3 jit_solution(9685547466510209095)
XLA Ops:
  0.0 1.3 collective-permute-start
  1.3 2.6 %collective-permute-start.6 = (f32[256,256]{1,0:T(8,128)}, f32[256,256]{1,0:T(8,128)S(1)}, u32[]{:S(2)}, u32[]{:S(2)}) collective-permute-start(f32[256,256]{1,0:T(8,128)} %bitcast.7), channel_id=1, source_target_pairs={{0,10},{1,11},{2,8},{3,9},{4,14},{5,15},{6,12},{7,13},{8,18},{9,19... | collective-permute-start | bytes 786440 | tf_op jit(solution)/shard_map/ppermute | solution.py:106
  3.9 2.8 %copy-done = f32[3,1,2,256,1024]{4,3,2,1,0:T(8,128)S(1)} copy-done((f32[3,1,2,256,1024]{4,3,2,1,0:T(8,128)S(1)}, f32[3,1,2,256,1024]{4,3,2,1,0:T(8,128)}, u32[]{:S(2)}) %copy-start) | copy-done | bytes 6291480
  6.7 1.9 %copy-done.1 = f32[1,3,256,1024]{3,2,1,0:T(8,128)S(1)} copy-done((f32[1,3,256,1024]{3,2,1,0:T(8,128)S(1)}, f32[1,3,256,1024]{3,2,1,0:T(8,128)}, u32[]{:S(2)}) %copy-start.1) | copy-done | bytes 3145752
  8.6 1.7 %shard_map.37 = (f32[256,1024]{1,0:T(8,128)S(1)}, f32[256,1024]{1,0:T(8,128)S(1)}, f32[256,1024]{1,0:T(8,128)S(1)}, f32[256,1024]{1,0:T(8,128)S(1)}, f32[256,102...) custom-call(f32[3,2,256,1024]{3,2,1,0:T(8,128)S(1)} %bitcast.4, ...), custom_call_target="tpu_custom_call" | custom-call | tf_op jit(solution)/shard_map/pallas_call | solution.py:87
  10.5 1.3 collective-permute-start.7
  11.8 1.6 %collective-permute-start.4 = (f32[256,256]{1,0:T(8,128)S(1)}, f32[256,256]{1,0:T(8,128)S(1)}, u32[]{:S(2)}, u32[]{:S(2)}) collective-permute-start(f32[256,256]{1,0:T(8,128)S(1)} %collective-permute-done.refs_2_), channel_id=1, source_target_pairs={{0,8},{1,9},{2,10},{3,11},{4,12},{5,13},{6,14},{7,15},{8,16},{9,17... | collective-permute-start | bytes 786440 | tf_op jit(solution)/shard_map/ppermute | solution.py:106
  13.4 1.5 %collective-permute-start.2 = (f32[256,256]{1,0:T(8,128)S(1)}, f32[256,256]{1,0:T(8,128)S(1)}, u32[]{:S(2)}, u32[]{:S(2)}) collective-permute-start(f32[256,256]{1,0:T(8,128)S(1)} %collective-permute-done.refs_2_), channel_id=1, source_target_pairs={{0,2},{1,3},{2,0},{3,1},{4,6},{5,7},{6,4},{7,5},{8,10},{9,11},{10,... | collective-permute-start | bytes 786440 | tf_op jit(solution)/shard_map/ppermute | solution.py:106
  14.9 5.0 %collective-permute-done.7.refs_9_ = f32[256,256]{1,0:T(8,128)S(1)} collective-permute-done((f32[256,256]{1,0:T(8,128)S(1)}, f32[256,256]{1,0:T(8,128)S(1)}, u32[]{:S(2)}, u32[]{:S(2)}) %collective-permute-start.7) | collective-permute-done | bytes 262176 | tf_op jit(solution)/shard_map/ppermute | solution.py:106
  20.7 0.8 collective-permute-done.8.refs_10_
  22.3 1.1 shard_map.38.refs_0_
  23.3 4.0 %collective-permute-start.11 = (f32[256,256]{1,0:T(8,128)S(1)}, f32[256,256]{1,0:T(8,128)S(1)}, u32[]{:S(2)}, u32[]{:S(2)}) collective-permute-start(f32[256,256]{1,0:T(8,128)S(1)} %shard_map.38.refs_0_), channel_id=1, source_target_pairs={{8,18},{9,19},{10,16},{11,17}} | collective-permute-start | bytes 786440 | tf_op jit(solution)/shard_map/ppermute | solution.py:106
  27.4 1.3 collective-permute-start.9
  28.7 1.6 %collective-permute-start.15 = (f32[256,256]{1,0:T(8,128)S(1)}, f32[256,256]{1,0:T(8,128)S(1)}, u32[]{:S(2)}, u32[]{:S(2)}) collective-permute-start(f32[256,256]{1,0:T(8,128)S(1)} %shard_map.38.refs_0_), channel_id=1, source_target_pairs={{8,2},{9,3},{10,0},{11,1},{24,18},{25,19},{26,16},{27,17}} | collective-permute-start | bytes 786440 | tf_op jit(solution)/shard_map/ppermute | solution.py:106
  30.3 1.3 collective-permute-start.13
  31.6 3.6 %collective-permute-done.11.refs_4_ = f32[256,256]{1,0:T(8,128)S(1)} collective-permute-done((f32[256,256]{1,0:T(8,128)S(1)}, f32[256,256]{1,0:T(8,128)S(1)}, u32[]{:S(2)}, u32[]{:S(2)}) %collective-permute-start.11) | collective-permute-done | bytes 262176 | tf_op jit(solution)/shard_map/ppermute | solution.py:106
  35.2 4.8 %collective-permute-done.9.refs_2_ = f32[256,256]{1,0:T(8,128)S(1)} collective-permute-done((f32[256,256]{1,0:T(8,128)S(1)}, f32[256,256]{1,0:T(8,128)S(1)}, u32[]{:S(2)}, u32[]{:S(2)}) %collective-permute-start.9) | collective-permute-done | bytes 262176 | tf_op jit(solution)/shard_map/ppermute | solution.py:106
  40.0 0.5 collective-permute-start.16
  40.5 1.2 collective-permute-done.13.refs_2_
  41.8 0.6 shard_map.39.refs_0_
  42.4 0.9 collective-permute-done.14.refs_3_
  43.3 0.6 shard_map.40.refs_0_
  43.9 0.7 collective-permute-start.17
  44.6 0.7 collective-permute-start.19
  45.9 1.0 collective-permute-done.18.refs_3_
  47.7 1.0 collective-permute-start.22
  48.7 7.4 %collective-permute-done.22.refs_2_ = f32[256,256]{1,0:T(8,128)S(1)} collective-permute-done((f32[256,256]{1,0:T(8,128)S(1)}, f32[256,256]{1,0:T(8,128)S(1)}, u32[]{:S(2)}, u32[]{:S(2)}) %collective-permute-start.22) | collective-permute-done | bytes 262176 | tf_op jit(solution)/shard_map/ppermute | solution.py:106
  56.5 1.1 collective-permute-done.23.refs_3_
  58.0 0.7 collective-permute-start.24
  58.7 0.7 collective-permute-start.26
  60.0 1.0 collective-permute-done.25.refs_3_
  61.9 1.3 collective-permute-start.30
  63.2 1.3 collective-permute-start.28
  64.5 1.3 collective-permute-start.34
  65.8 1.3 collective-permute-start.32
  67.1 35.4 %collective-permute-done.30.refs_6_ = f32[256,256]{1,0:T(8,128)S(1)} collective-permute-done((f32[256,256]{1,0:T(8,128)S(1)}, f32[256,256]{1,0:T(8,128)S(1)}, u32[]{:S(2)}, u32[]{:S(2)}) %collective-permute-start.30) | collective-permute-done | bytes 262176 | tf_op jit(solution)/shard_map/ppermute | solution.py:106
  102.9 9.0 %collective-permute-done.34.refs_5_ = f32[256,256]{1,0:T(8,128)S(1)} collective-permute-done((f32[256,256]{1,0:T(8,128)S(1)}, f32[256,256]{1,0:T(8,128)S(1)}, u32[]{:S(2)}, u32[]{:S(2)}) %collective-permute-start.34) | collective-permute-done | bytes 262176 | tf_op jit(solution)/shard_map/ppermute | solution.py:106
  111.9 0.5 collective-permute-start.33
  112.5 0.6 shard_map.47.refs_0_
  113.8 0.6 shard_map.48.refs_1_
  114.5 1.3 collective-permute-start.36
  115.9 7.9 %collective-permute-done.42 = f32[256,256]{1,0:T(8,128)S(1)} collective-permute-done((f32[256,256]{1,0:T(8,128)S(1)}, f32[256,256]{1,0:T(8,128)S(1)}, u32[]{:S(2)}, u32[]{:S(2)}) %collective-permute-start.42) | collective-permute-done | bytes 262176 | tf_op jit(solution)/shard_map/ppermute | solution.py:106
  123.8 1.3 collective-permute-start.43
  125.2 1.0 collective-permute-start.38
  126.2 4.2 %collective-permute-done.43.refs_10_ = f32[256,256]{1,0:T(8,128)S(1)} collective-permute-done((f32[256,256]{1,0:T(8,128)S(1)}, f32[256,256]{1,0:T(8,128)S(1)}, u32[]{:S(2)}, u32[]{:S(2)}) %collective-permute-start.43) | collective-permute-done | bytes 262176 | tf_op jit(solution)/shard_map/ppermute | solution.py:106
  130.4 2.3 %collective-permute-done.40.refs_8_ = f32[256,256]{1,0:T(8,128)S(1)} collective-permute-done((f32[256,256]{1,0:T(8,128)S(1)}, f32[256,256]{1,0:T(8,128)S(1)}, u32[]{:S(2)}, u32[]{:S(2)}) %collective-permute-start.40) | collective-permute-done | bytes 262176 | tf_op jit(solution)/shard_map/ppermute | solution.py:106
  133.2 1.0 collective-permute-done.41.refs_9_
  134.6 1.8 %shard_map.49 = f32[256,256]{1,0:T(8,128)} custom-call(f32[256,256]{1,0:T(8,128)S(1)} %shard_map.44.refs_0_, f32[256,256]{1,0:T(8,128)S(1)} %shard_map.48.refs_1_, f32[256,1024]{1,0:T(8,128)S(1)} %get-tuple-element.37.refs_1_.refs_2_, f32[256,256]{1,0:T(8,128)S(1)} %collective-permute-done.36.refs_3_, f32[256,256]{1,0:T(8,128)S(1)} %collective-permute-done.37.refs_4_, ...), custom_call_target="tpu_custom_call" | custom-call | flops 805306368 | tf_op jit(solution)/shard_map/pallas_call | solution.py:62
  (61 shorter events, 7.6 us)
Async XLA Ops:
  0.0 10.3 %collective-permute-start = (f32[256,256]{1,0:T(8,128)}, f32[256,256]{1,0:T(8,128)S(1)}, u32[]{:S(2)}, u32[]{:S(2)}) collective-permute-start(f32[256,256]{1,0:T(8,128)} %bitcast.6), channel_id=1, source_target_pairs={{4,0},{5,1},{6,2},{7,3},{12,8},{13,9},{14,10},{15,11},{20,16},{21,... | collective-permute-start | bytes 786440 | tf_op jit(solution)/shard_map/ppermute | solution.py:106
  1.3 9.2 %collective-permute-start.6 = (f32[256,256]{1,0:T(8,128)}, f32[256,256]{1,0:T(8,128)S(1)}, u32[]{:S(2)}, u32[]{:S(2)}) collective-permute-start(f32[256,256]{1,0:T(8,128)} %bitcast.7), channel_id=1, source_target_pairs={{0,10},{1,11},{2,8},{3,9},{4,14},{5,15},{6,12},{7,13},{8,18},{9,19... | collective-permute-start | bytes 786440 | tf_op jit(solution)/shard_map/ppermute | solution.py:106
  3.9 2.8 %copy-start = (f32[3,1,2,256,1024]{4,3,2,1,0:T(8,128)S(1)}, f32[3,1,2,256,1024]{4,3,2,1,0:T(8,128)}, u32[]{:S(2)}) copy-start(f32[3,1,2,256,1024]{4,3,2,1,0:T(8,128)} %param.4) | copy-start | bytes 18874372
  6.7 1.9 %copy-start.1 = (f32[1,3,256,1024]{3,2,1,0:T(8,128)S(1)}, f32[1,3,256,1024]{3,2,1,0:T(8,128)}, u32[]{:S(2)}) copy-start(f32[1,3,256,1024]{3,2,1,0:T(8,128)} %param.5) | copy-start | bytes 9437188
  8.5 13.7 %copy-start.2 = (f32[1,256,256]{2,1,0:T(8,128)S(1)}, f32[1,256,256]{2,1,0:T(8,128)}, u32[]{:S(2)}) copy-start(f32[1,256,256]{2,1,0:T(8,128)} %param.3) | copy-start | bytes 786436
  10.5 9.5 %collective-permute-start.7 = (f32[256,256]{1,0:T(8,128)S(1)}, f32[256,256]{1,0:T(8,128)S(1)}, u32[]{:S(2)}, u32[]{:S(2)}) collective-permute-start(f32[256,256]{1,0:T(8,128)S(1)} %collective-permute-done.6), channel_id=1, source_target_pairs={{4,0},{5,1},{6,2},{7,3},{12,8},{13,9},{14,10},{15,11},{20,16},{21,... | collective-permute-start | bytes 786440 | tf_op jit(solution)/shard_map/ppermute | solution.py:106
  11.8 8.2 %collective-permute-start.4 = (f32[256,256]{1,0:T(8,128)S(1)}, f32[256,256]{1,0:T(8,128)S(1)}, u32[]{:S(2)}, u32[]{:S(2)}) collective-permute-start(f32[256,256]{1,0:T(8,128)S(1)} %collective-permute-done.refs_2_), channel_id=1, source_target_pairs={{0,8},{1,9},{2,10},{3,11},{4,12},{5,13},{6,14},{7,15},{8,16},{9,17... | collective-permute-start | bytes 786440 | tf_op jit(solution)/shard_map/ppermute | solution.py:106
  13.4 7.3 %collective-permute-start.2 = (f32[256,256]{1,0:T(8,128)S(1)}, f32[256,256]{1,0:T(8,128)S(1)}, u32[]{:S(2)}, u32[]{:S(2)}) collective-permute-start(f32[256,256]{1,0:T(8,128)S(1)} %collective-permute-done.refs_2_), channel_id=1, source_target_pairs={{0,2},{1,3},{2,0},{3,1},{4,6},{5,7},{6,4},{7,5},{8,10},{9,11},{10,... | collective-permute-start | bytes 786440 | tf_op jit(solution)/shard_map/ppermute | solution.py:106
  14.9 5.8 %collective-permute-start.1 = (f32[256,256]{1,0:T(8,128)S(1)}, f32[256,256]{1,0:T(8,128)S(1)}, u32[]{:S(2)}, u32[]{:S(2)}) collective-permute-start(f32[256,256]{1,0:T(8,128)S(1)} %collective-permute-done.refs_2_), channel_id=1, source_target_pairs={{0,1},{1,0},{2,3},{3,2},{4,5},{5,4},{6,7},{7,6},{8,9},{9,8},{10,11... | collective-permute-start | bytes 786440 | tf_op jit(solution)/shard_map/ppermute | solution.py:106
  20.0 1.5 %collective-permute-start.8 = (f32[256,256]{1,0:T(8,128)S(1)}, f32[256,256]{1,0:T(8,128)S(1)}, u32[]{:S(2)}, u32[]{:S(2)}) collective-permute-start(f32[256,256]{1,0:T(8,128)S(1)} %collective-permute-done.7.refs_9_), channel_id=1, source_target_pairs={{0,1},{1,0},{2,3},{3,2},{4,5},{5,4},{6,7},{7,6},{8,9},{9,8},{10,11... | collective-permute-start | bytes 786440 | tf_op jit(solution)/shard_map/ppermute | solution.py:106
  20.0 1.9 %collective-permute-start.5 = (f32[256,256]{1,0:T(8,128)S(1)}, f32[256,256]{1,0:T(8,128)S(1)}, u32[]{:S(2)}, u32[]{:S(2)}) collective-permute-start(f32[256,256]{1,0:T(8,128)S(1)} %collective-permute-done.4.refs_7_), channel_id=1, source_target_pairs={{0,1},{1,0},{2,3},{3,2},{4,5},{5,4},{6,7},{7,6},{8,9},{9,8},{10,11... | collective-permute-start | bytes 786440 | tf_op jit(solution)/shard_map/ppermute | solution.py:106
  20.7 1.5 %collective-permute-start.3 = (f32[256,256]{1,0:T(8,128)S(1)}, f32[256,256]{1,0:T(8,128)S(1)}, u32[]{:S(2)}, u32[]{:S(2)}) collective-permute-start(f32[256,256]{1,0:T(8,128)S(1)} %collective-permute-done.2.refs_4_), channel_id=1, source_target_pairs={{0,1},{1,0},{2,3},{3,2},{4,5},{5,4},{6,7},{7,6},{8,9},{9,8},{10,11... | collective-permute-start | bytes 786440 | tf_op jit(solution)/shard_map/ppermute | solution.py:106
  23.3 11.9 %collective-permute-start.11 = (f32[256,256]{1,0:T(8,128)S(1)}, f32[256,256]{1,0:T(8,128)S(1)}, u32[]{:S(2)}, u32[]{:S(2)}) collective-permute-start(f32[256,256]{1,0:T(8,128)S(1)} %shard_map.38.refs_0_), channel_id=1, source_target_pairs={{8,18},{9,19},{10,16},{11,17}} | collective-permute-start | bytes 786440 | tf_op jit(solution)/shard_map/ppermute | solution.py:106
  27.4 12.6 %collective-permute-start.9 = (f32[256,256]{1,0:T(8,128)S(1)}, f32[256,256]{1,0:T(8,128)S(1)}, u32[]{:S(2)}, u32[]{:S(2)}) collective-permute-start(f32[256,256]{1,0:T(8,128)S(1)} %shard_map.38.refs_0_), channel_id=1, source_target_pairs={{8,16},{9,17},{10,18},{11,19}} | collective-permute-start | bytes 786440 | tf_op jit(solution)/shard_map/ppermute | solution.py:106
  28.7 11.3 %collective-permute-start.15 = (f32[256,256]{1,0:T(8,128)S(1)}, f32[256,256]{1,0:T(8,128)S(1)}, u32[]{:S(2)}, u32[]{:S(2)}) collective-permute-start(f32[256,256]{1,0:T(8,128)S(1)} %shard_map.38.refs_0_), channel_id=1, source_target_pairs={{8,2},{9,3},{10,0},{11,1},{24,18},{25,19},{26,16},{27,17}} | collective-permute-start | bytes 786440 | tf_op jit(solution)/shard_map/ppermute | solution.py:106
  30.3 11.4 %collective-permute-start.13 = (f32[256,256]{1,0:T(8,128)S(1)}, f32[256,256]{1,0:T(8,128)S(1)}, u32[]{:S(2)}, u32[]{:S(2)}) collective-permute-start(f32[256,256]{1,0:T(8,128)S(1)} %shard_map.38.refs_0_), channel_id=1, source_target_pairs={{8,0},{9,1},{10,2},{11,3},{24,16},{25,17},{26,18},{27,19}} | collective-permute-start | bytes 786440 | tf_op jit(solution)/shard_map/ppermute | solution.py:106
  35.2 6.5 %collective-permute-start.12 = (f32[256,256]{1,0:T(8,128)S(1)}, f32[256,256]{1,0:T(8,128)S(1)}, u32[]{:S(2)}, u32[]{:S(2)}) collective-permute-start(f32[256,256]{1,0:T(8,128)S(1)} %collective-permute-done.11.refs_4_), channel_id=1, source_target_pairs={{0,1},{1,0},{2,3},{3,2},{4,5},{5,4},{6,7},{7,6},{8,9},{9,8},{10,11... | collective-permute-start | bytes 786440 | tf_op jit(solution)/shard_map/ppermute | solution.py:106
  40.0 1.7 %collective-permute-start.10 = (f32[256,256]{1,0:T(8,128)S(1)}, f32[256,256]{1,0:T(8,128)S(1)}, u32[]{:S(2)}, u32[]{:S(2)}) collective-permute-start(f32[256,256]{1,0:T(8,128)S(1)} %collective-permute-done.9.refs_2_), channel_id=1, source_target_pairs={{0,1},{1,0},{2,3},{3,2},{4,5},{5,4},{6,7},{7,6},{8,9},{9,8},{10,11... | collective-permute-start | bytes 786440 | tf_op jit(solution)/shard_map/ppermute | solution.py:106
  40.0 2.4 %collective-permute-start.16 = (f32[256,256]{1,0:T(8,128)S(1)}, f32[256,256]{1,0:T(8,128)S(1)}, u32[]{:S(2)}, u32[]{:S(2)}) collective-permute-start(f32[256,256]{1,0:T(8,128)S(1)} %collective-permute-done.15.refs_4_), channel_id=1, source_target_pairs={{0,1},{1,0},{2,3},{3,2},{4,5},{5,4},{6,7},{7,6},{8,9},{9,8},{10,11... | collective-permute-start | bytes 786440 | tf_op jit(solution)/shard_map/ppermute | solution.py:106
  41.7 1.5 %collective-permute-start.14 = (f32[256,256]{1,0:T(8,128)S(1)}, f32[256,256]{1,0:T(8,128)S(1)}, u32[]{:S(2)}, u32[]{:S(2)}) collective-permute-start(f32[256,256]{1,0:T(8,128)S(1)} %collective-permute-done.13.refs_2_), channel_id=1, source_target_pairs={{0,1},{1,0},{2,3},{3,2},{4,5},{5,4},{6,7},{7,6},{8,9},{9,8},{10,11... | collective-permute-start | bytes 786440 | tf_op jit(solution)/shard_map/ppermute | solution.py:106
  43.9 1.4 %collective-permute-start.17 = (f32[256,256]{1,0:T(8,128)S(1)}, f32[256,256]{1,0:T(8,128)S(1)}, u32[]{:S(2)}, u32[]{:S(2)}) collective-permute-start(f32[256,256]{1,0:T(8,128)S(1)} %shard_map.40.refs_0_), channel_id=1, source_target_pairs={{16,0},{17,1},{18,2},{19,3}} | collective-permute-start | bytes 786440 | tf_op jit(solution)/shard_map/ppermute | solution.py:106
  44.6 0.9 collective-permute-start.19
  45.3 1.6 %collective-permute-start.18 = (f32[256,256]{1,0:T(8,128)S(1)}, f32[256,256]{1,0:T(8,128)S(1)}, u32[]{:S(2)}, u32[]{:S(2)}) collective-permute-start(f32[256,256]{1,0:T(8,128)S(1)} %collective-permute-done.17.refs_2_), channel_id=1, source_target_pairs={{0,1},{1,0},{2,3},{3,2},{4,5},{5,4},{6,7},{7,6},{8,9},{9,8},{10,11... | collective-permute-start | bytes 786440 | tf_op jit(solution)/shard_map/ppermute | solution.py:106
  45.5 1.8 %collective-permute-start.20 = (f32[256,256]{1,0:T(8,128)S(1)}, f32[256,256]{1,0:T(8,128)S(1)}, u32[]{:S(2)}, u32[]{:S(2)}) collective-permute-start(f32[256,256]{1,0:T(8,128)S(1)} %collective-permute-done.19.refs_2_), channel_id=1, source_target_pairs={{0,1},{1,0},{2,3},{3,2},{4,5},{5,4},{6,7},{7,6},{8,9},{9,8},{10,11... | collective-permute-start | bytes 786440 | tf_op jit(solution)/shard_map/ppermute | solution.py:106
  47.7 8.4 %collective-permute-start.22 = (f32[256,256]{1,0:T(8,128)S(1)}, f32[256,256]{1,0:T(8,128)S(1)}, u32[]{:S(2)}, u32[]{:S(2)}) collective-permute-start(f32[256,256]{1,0:T(8,128)S(1)} %shard_map.42.refs_1_), channel_id=1, source_target_pairs={{0,2},{1,3},{2,0},{3,1},{4,6},{5,7},{6,4},{7,5},{8,10},{9,11},{10,... | collective-permute-start | bytes 786440 | tf_op jit(solution)/shard_map/ppermute | solution.py:106
  48.7 7.4 %collective-permute-start.21 = (f32[256,256]{1,0:T(8,128)S(1)}, f32[256,256]{1,0:T(8,128)S(1)}, u32[]{:S(2)}, u32[]{:S(2)}) collective-permute-start(f32[256,256]{1,0:T(8,128)S(1)} %shard_map.42.refs_1_), channel_id=1, source_target_pairs={{0,1},{1,0},{2,3},{3,2},{4,5},{5,4},{6,7},{7,6},{8,9},{9,8},{10,11... | collective-permute-start | bytes 786440 | tf_op jit(solution)/shard_map/ppermute | solution.py:106
  56.1 1.5 %collective-permute-start.23 = (f32[256,256]{1,0:T(8,128)S(1)}, f32[256,256]{1,0:T(8,128)S(1)}, u32[]{:S(2)}, u32[]{:S(2)}) collective-permute-start(f32[256,256]{1,0:T(8,128)S(1)} %collective-permute-done.22.refs_2_), channel_id=1, source_target_pairs={{0,1},{1,0},{2,3},{3,2},{4,5},{5,4},{6,7},{7,6},{8,9},{9,8},{10,11... | collective-permute-start | bytes 786440 | tf_op jit(solution)/shard_map/ppermute | solution.py:106
  58.0 1.4 %collective-permute-start.24 = (f32[256,256]{1,0:T(8,128)S(1)}, f32[256,256]{1,0:T(8,128)S(1)}, u32[]{:S(2)}, u32[]{:S(2)}) collective-permute-start(f32[256,256]{1,0:T(8,128)S(1)} %shard_map.44.refs_0_), channel_id=1, source_target_pairs={{0,16},{1,17},{2,18},{3,19}} | collective-permute-start | bytes 786440 | tf_op jit(solution)/shard_map/ppermute | solution.py:106
  58.7 0.9 collective-permute-start.26
  59.4 1.6 %collective-permute-start.25 = (f32[256,256]{1,0:T(8,128)S(1)}, f32[256,256]{1,0:T(8,128)S(1)}, u32[]{:S(2)}, u32[]{:S(2)}) collective-permute-start(f32[256,256]{1,0:T(8,128)S(1)} %collective-permute-done.24.refs_2_), channel_id=1, source_target_pairs={{0,1},{1,0},{2,3},{3,2},{4,5},{5,4},{6,7},{7,6},{8,9},{9,8},{10,11... | collective-permute-start | bytes 786440 | tf_op jit(solution)/shard_map/ppermute | solution.py:106
  59.6 1.8 %collective-permute-start.27 = (f32[256,256]{1,0:T(8,128)S(1)}, f32[256,256]{1,0:T(8,128)S(1)}, u32[]{:S(2)}, u32[]{:S(2)}) collective-permute-start(f32[256,256]{1,0:T(8,128)S(1)} %collective-permute-done.26.refs_2_), channel_id=1, source_target_pairs={{0,1},{1,0},{2,3},{3,2},{4,5},{5,4},{6,7},{7,6},{8,9},{9,8},{10,11... | collective-permute-start | bytes 786440 | tf_op jit(solution)/shard_map/ppermute | solution.py:106
  61.9 40.6 %collective-permute-start.30 = (f32[256,256]{1,0:T(8,128)S(1)}, f32[256,256]{1,0:T(8,128)S(1)}, u32[]{:S(2)}, u32[]{:S(2)}) collective-permute-start(f32[256,256]{1,0:T(8,128)S(1)} %shard_map.46.refs_1_), channel_id=1, source_target_pairs={{16,8},{17,9},{18,10},{19,11}} | collective-permute-start | bytes 786440 | tf_op jit(solution)/shard_map/ppermute | solution.py:106
  63.2 39.3 %collective-permute-start.28 = (f32[256,256]{1,0:T(8,128)S(1)}, f32[256,256]{1,0:T(8,128)S(1)}, u32[]{:S(2)}, u32[]{:S(2)}) collective-permute-start(f32[256,256]{1,0:T(8,128)S(1)} %shard_map.46.refs_1_), channel_id=1, source_target_pairs={{0,8},{1,9},{2,10},{3,11},{16,24},{17,25},{18,26},{19,27}} | collective-permute-start | bytes 786440 | tf_op jit(solution)/shard_map/ppermute | solution.py:106
  64.5 47.5 %collective-permute-start.34 = (f32[256,256]{1,0:T(8,128)S(1)}, f32[256,256]{1,0:T(8,128)S(1)}, u32[]{:S(2)}, u32[]{:S(2)}) collective-permute-start(f32[256,256]{1,0:T(8,128)S(1)} %shard_map.46.refs_1_), channel_id=1, source_target_pairs={{16,10},{17,11},{18,8},{19,9}} | collective-permute-start | bytes 786440 | tf_op jit(solution)/shard_map/ppermute | solution.py:106
  65.8 46.2 %collective-permute-start.32 = (f32[256,256]{1,0:T(8,128)S(1)}, f32[256,256]{1,0:T(8,128)S(1)}, u32[]{:S(2)}, u32[]{:S(2)}) collective-permute-start(f32[256,256]{1,0:T(8,128)S(1)} %shard_map.46.refs_1_), channel_id=1, source_target_pairs={{0,10},{1,11},{2,8},{3,9},{16,26},{17,27},{18,24},{19,25}} | collective-permute-start | bytes 786440 | tf_op jit(solution)/shard_map/ppermute | solution.py:106
  102.4 10.0 %collective-permute-start.31 = (f32[256,256]{1,0:T(8,128)S(1)}, f32[256,256]{1,0:T(8,128)S(1)}, u32[]{:S(2)}, u32[]{:S(2)}) collective-permute-start(f32[256,256]{1,0:T(8,128)S(1)} %collective-permute-done.30.refs_6_), channel_id=1, source_target_pairs={{0,1},{1,0},{2,3},{3,2},{4,5},{5,4},{6,7},{7,6},{8,9},{9,8},{10,11... | collective-permute-start | bytes 786440 | tf_op jit(solution)/shard_map/ppermute | solution.py:106
  102.4 10.0 %collective-permute-start.29 = (f32[256,256]{1,0:T(8,128)S(1)}, f32[256,256]{1,0:T(8,128)S(1)}, u32[]{:S(2)}, u32[]{:S(2)}) collective-permute-start(f32[256,256]{1,0:T(8,128)S(1)} %collective-permute-done.28.refs_3_), channel_id=1, source_target_pairs={{0,1},{1,0},{2,3},{3,2},{4,5},{5,4},{6,7},{7,6},{8,9},{9,8},{10,11... | collective-permute-start | bytes 786440 | tf_op jit(solution)/shard_map/ppermute | solution.py:106
  111.9 1.5 %collective-permute-start.35 = (f32[256,256]{1,0:T(8,128)S(1)}, f32[256,256]{1,0:T(8,128)S(1)}, u32[]{:S(2)}, u32[]{:S(2)}) collective-permute-start(f32[256,256]{1,0:T(8,128)S(1)} %collective-permute-done.34.refs_5_), channel_id=1, source_target_pairs={{0,1},{1,0},{2,3},{3,2},{4,5},{5,4},{6,7},{7,6},{8,9},{9,8},{10,11... | collective-permute-start | bytes 786440 | tf_op jit(solution)/shard_map/ppermute | solution.py:106
  111.9 1.9 %collective-permute-start.33 = (f32[256,256]{1,0:T(8,128)S(1)}, f32[256,256]{1,0:T(8,128)S(1)}, u32[]{:S(2)}, u32[]{:S(2)}) collective-permute-start(f32[256,256]{1,0:T(8,128)S(1)} %collective-permute-done.32.refs_2_), channel_id=1, source_target_pairs={{0,1},{1,0},{2,3},{3,2},{4,5},{5,4},{6,7},{7,6},{8,9},{9,8},{10,11... | collective-permute-start | bytes 786440 | tf_op jit(solution)/shard_map/ppermute | solution.py:106
  114.5 9.3 %collective-permute-start.42 = (f32[256,256]{1,0:T(8,128)S(1)}, f32[256,256]{1,0:T(8,128)S(1)}, u32[]{:S(2)}, u32[]{:S(2)}) collective-permute-start(f32[256,256]{1,0:T(8,128)S(1)} %shard_map.48.refs_1_), channel_id=1, source_target_pairs={{0,26},{1,27},{2,24},{3,25},{4,30},{5,31},{6,28},{7,29},{8,2},{9,3... | collective-permute-start | bytes 786440 | tf_op jit(solution)/shard_map/ppermute | solution.py:106
  114.5 10.5 %collective-permute-start.36 = (f32[256,256]{1,0:T(8,128)S(1)}, f32[256,256]{1,0:T(8,128)S(1)}, u32[]{:S(2)}, u32[]{:S(2)}) collective-permute-start(f32[256,256]{1,0:T(8,128)S(1)} %shard_map.48.refs_1_), channel_id=1, source_target_pairs={{0,4},{1,5},{2,6},{3,7},{8,12},{9,13},{10,14},{11,15},{16,20},{17,... | collective-permute-start | bytes 786440 | tf_op jit(solution)/shard_map/ppermute | solution.py:106
  123.8 6.6 %collective-permute-start.43 = (f32[256,256]{1,0:T(8,128)S(1)}, f32[256,256]{1,0:T(8,128)S(1)}, u32[]{:S(2)}, u32[]{:S(2)}) collective-permute-start(f32[256,256]{1,0:T(8,128)S(1)} %collective-permute-done.42), channel_id=1, source_target_pairs={{0,4},{1,5},{2,6},{3,7},{8,12},{9,13},{10,14},{11,15},{16,20},{17,... | collective-permute-start | bytes 786440 | tf_op jit(solution)/shard_map/ppermute | solution.py:106
  125.1 7.6 %collective-permute-start.40 = (f32[256,256]{1,0:T(8,128)S(1)}, f32[256,256]{1,0:T(8,128)S(1)}, u32[]{:S(2)}, u32[]{:S(2)}) collective-permute-start(f32[256,256]{1,0:T(8,128)S(1)} %collective-permute-done.36.refs_3_), channel_id=1, source_target_pairs={{0,24},{1,25},{2,26},{3,27},{4,28},{5,29},{6,30},{7,31},{8,0},{9,1... | collective-permute-start | bytes 786440 | tf_op jit(solution)/shard_map/ppermute | solution.py:106
  125.2 7.6 %collective-permute-start.38 = (f32[256,256]{1,0:T(8,128)S(1)}, f32[256,256]{1,0:T(8,128)S(1)}, u32[]{:S(2)}, u32[]{:S(2)}) collective-permute-start(f32[256,256]{1,0:T(8,128)S(1)} %collective-permute-done.36.refs_3_), channel_id=1, source_target_pairs={{0,2},{1,3},{2,0},{3,1},{4,6},{5,7},{6,4},{7,5},{8,10},{9,11},{10,... | collective-permute-start | bytes 786440 | tf_op jit(solution)/shard_map/ppermute | solution.py:106
  126.2 7.0 %collective-permute-start.37 = (f32[256,256]{1,0:T(8,128)S(1)}, f32[256,256]{1,0:T(8,128)S(1)}, u32[]{:S(2)}, u32[]{:S(2)}) collective-permute-start(f32[256,256]{1,0:T(8,128)S(1)} %collective-permute-done.36.refs_3_), channel_id=1, source_target_pairs={{0,1},{1,0},{2,3},{3,2},{4,5},{5,4},{6,7},{7,6},{8,9},{9,8},{10,11... | collective-permute-start | bytes 786440 | tf_op jit(solution)/shard_map/ppermute | solution.py:106
  130.4 2.8 %collective-permute-start.44 = (f32[256,256]{1,0:T(8,128)S(1)}, f32[256,256]{1,0:T(8,128)S(1)}, u32[]{:S(2)}, u32[]{:S(2)}) collective-permute-start(f32[256,256]{1,0:T(8,128)S(1)} %collective-permute-done.43.refs_10_), channel_id=1, source_target_pairs={{0,1},{1,0},{2,3},{3,2},{4,5},{5,4},{6,7},{7,6},{8,9},{9,8},{10,11... | collective-permute-start | bytes 786440 | tf_op jit(solution)/shard_map/ppermute | solution.py:106
  132.7 1.5 %collective-permute-start.41 = (f32[256,256]{1,0:T(8,128)S(1)}, f32[256,256]{1,0:T(8,128)S(1)}, u32[]{:S(2)}, u32[]{:S(2)}) collective-permute-start(f32[256,256]{1,0:T(8,128)S(1)} %collective-permute-done.40.refs_8_), channel_id=1, source_target_pairs={{0,1},{1,0},{2,3},{3,2},{4,5},{5,4},{6,7},{7,6},{8,9},{9,8},{10,11... | collective-permute-start | bytes 786440 | tf_op jit(solution)/shard_map/ppermute | solution.py:106
  132.7 1.8 %collective-permute-start.39 = (f32[256,256]{1,0:T(8,128)S(1)}, f32[256,256]{1,0:T(8,128)S(1)}, u32[]{:S(2)}, u32[]{:S(2)}) collective-permute-start(f32[256,256]{1,0:T(8,128)S(1)} %collective-permute-done.38.refs_5_), channel_id=1, source_target_pairs={{0,1},{1,0},{2,3},{3,2},{4,5},{5,4},{6,7},{7,6},{8,9},{9,8},{10,11... | collective-permute-start | bytes 786440 | tf_op jit(solution)/shard_map/ppermute | solution.py:106

commit v4 on v3

--- a/solution.py
+++ b/solution.py
@@ -117,9 +117,11 @@
     def within(block, among=None):
         return [(0, block)] + [(flip, move(block, among or every, flip)) for flip in range(2, rows, 2)]
 
-    def apply(starts, sign, *mats_pieces, only=None):
+    def apply(starts, sign, *mats_pieces, only=None, far_first=False):
         early = [(m, f, p) for m, ps in mats_pieces for f, p in ps[:2]]
         late = [(m, f, p) for m, ps in mats_pieces for f, p in ps[2:]]
+        if far_first and late:
+            early, late = late, early
         start = combine(starts, early, sign, only)
         return combine([start], late, sign, only) if late else start
 
@@ -155,11 +157,10 @@
         left, right = reduce_mats[k]
         lower = swapped(direct(current, [(i, i + stride) for i in senders]))
         upper = swapped(direct(current, [(i, i - stride) for i in senders]))
-        current = combine([current], [(left, f, p) for f, p in lower], -1)
-        current = combine([current], [(right, f, p) for f, p in upper], -1)
+        current = apply([current], -1, (right, upper), (left, lower), far_first=True)
 
     upper = swapped(direct(current, [(layers // 2, 0)]))
-    current = apply([current], -1, (reduce_mats[levels - 1][1], upper))
+    current = apply([current], -1, (reduce_mats[levels - 1][1], upper), far_first=True)
     base = apply([], 1, (inverse, swapped(within(current))))
 
     result = base
@@ -168,11 +169,11 @@
         only = (2 * stride, stride)
         senders = range(0, layers, 2 * stride)
         if k == levels - 1:
-            result = apply([base, result], -1, (west, swapped(direct(result, [(0, stride)]))), only=only)
+            result = apply([base, result], -1, (west, swapped(direct(result, [(0, stride)]))), only=only, far_first=True)
         elif k > 0:
             lower = swapped(direct(result, [(j, j + stride) for j in senders]))
             upper = swapped(direct(result, [(j, j - stride) for j in senders]))
-            result = apply([base, result], -1, (west, lower), (east, upper), only=only)
+            result = apply([base, result], -1, (east, upper), (west, lower), only=only, far_first=True)
         else:
             lower = hop(result, -1)
             passed = [(flip, move(result, ring(-2), flip)) for flip in range(2, rows, 2)]

time: 139 us -> 136 us (0.978)
  waiting for transfers between devices: 89.1 us -> 86.1 us
    ppermute x45, waiting for transfers between devices: 89.1 us -> 86.1 us  [move(): return lax.ppermute(block, AXES, hops) if hops else None]
where the time goes in v4:
time: 136 us; the launch traced here: 134 us
  waiting for transfers between devices  86.1 us (63%)
  starting transfers between devices  33.6 us (25%)
  Pallas kernels  9.41 us (7%)
  local copies, waits for them, and re-layouts  4.68 us (3%)
    ppermute x45, waiting for transfers between devices, move(): return lax.ppermute(block, AXES, hops) if hops else None  86.1 us
    ppermute x45, starting transfers between devices, move(): return lax.ppermute(block, AXES, hops) if hops else None  33.6 us
    pallas_call x12, Pallas kernels, combine(): pl.pallas_call(functools.partial(combine_kernel, shape, sign, only), out_...  7.68 us
    unnamed x6, local copies, waits for them, and re-layouts  4.68 us
  transfers between devices with their start and end apart: 45, of which 24 were waited for; matrix products, arithmetic and copies ran while one was open for 0% of the time, Pallas kernels for 3%

profile of v4, /device:TPU:8, one launch (start us, length us, event | category | flops | bytes accessed | tf_op | source)
XLA Modules:
  0.0 134.1 jit_solution(17074148542556587255)
XLA Ops:
  0.0 1.3 collective-permute-start
  1.3 2.6 %collective-permute-start.6 = (f32[256,256]{1,0:T(8,128)}, f32[256,256]{1,0:T(8,128)S(1)}, u32[]{:S(2)}, u32[]{:S(2)}) collective-permute-start(f32[256,256]{1,0:T(8,128)} %bitcast.7), channel_id=1, source_target_pairs={{0,10},{1,11},{2,8},{3,9},{4,14},{5,15},{6,12},{7,13},{8,18},{9,19... | collective-permute-start | bytes 786440 | tf_op jit(solution)/shard_map/ppermute | solution.py:106
  3.9 2.8 %copy-done = f32[3,1,2,256,1024]{4,3,2,1,0:T(8,128)S(1)} copy-done((f32[3,1,2,256,1024]{4,3,2,1,0:T(8,128)S(1)}, f32[3,1,2,256,1024]{4,3,2,1,0:T(8,128)}, u32[]{:S(2)}) %copy-start) | copy-done | bytes 6291480
  6.7 1.9 %copy-done.1 = f32[1,3,256,1024]{3,2,1,0:T(8,128)S(1)} copy-done((f32[1,3,256,1024]{3,2,1,0:T(8,128)S(1)}, f32[1,3,256,1024]{3,2,1,0:T(8,128)}, u32[]{:S(2)}) %copy-start.1) | copy-done | bytes 3145752
  8.6 1.7 %shard_map.37 = (f32[256,1024]{1,0:T(8,128)S(1)}, f32[256,1024]{1,0:T(8,128)S(1)}, f32[256,1024]{1,0:T(8,128)S(1)}, f32[256,1024]{1,0:T(8,128)S(1)}, f32[256,102...) custom-call(f32[3,2,256,1024]{3,2,1,0:T(8,128)S(1)} %bitcast.4, ...), custom_call_target="tpu_custom_call" | custom-call | tf_op jit(solution)/shard_map/pallas_call | solution.py:87
  10.5 1.3 collective-permute-start.7
  11.8 1.6 %collective-permute-start.4 = (f32[256,256]{1,0:T(8,128)S(1)}, f32[256,256]{1,0:T(8,128)S(1)}, u32[]{:S(2)}, u32[]{:S(2)}) collective-permute-start(f32[256,256]{1,0:T(8,128)S(1)} %collective-permute-done.refs_2_), channel_id=1, source_target_pairs={{0,8},{1,9},{2,10},{3,11},{4,12},{5,13},{6,14},{7,15},{8,16},{9,17... | collective-permute-start | bytes 786440 | tf_op jit(solution)/shard_map/ppermute | solution.py:106
  13.4 1.5 %collective-permute-start.2 = (f32[256,256]{1,0:T(8,128)S(1)}, f32[256,256]{1,0:T(8,128)S(1)}, u32[]{:S(2)}, u32[]{:S(2)}) collective-permute-start(f32[256,256]{1,0:T(8,128)S(1)} %collective-permute-done.refs_2_), channel_id=1, source_target_pairs={{0,2},{1,3},{2,0},{3,1},{4,6},{5,7},{6,4},{7,5},{8,10},{9,11},{10,... | collective-permute-start | bytes 786440 | tf_op jit(solution)/shard_map/ppermute | solution.py:106
  14.9 5.0 %collective-permute-done.7.refs_9_ = f32[256,256]{1,0:T(8,128)S(1)} collective-permute-done((f32[256,256]{1,0:T(8,128)S(1)}, f32[256,256]{1,0:T(8,128)S(1)}, u32[]{:S(2)}, u32[]{:S(2)}) %collective-permute-start.7) | collective-permute-done | bytes 262176 | tf_op jit(solution)/shard_map/ppermute | solution.py:106
  20.0 0.5 collective-permute-start.5
  20.7 0.8 collective-permute-done.8.refs_10_
  22.3 1.1 shard_map.38.refs_0_
  23.3 4.0 %collective-permute-start.11 = (f32[256,256]{1,0:T(8,128)S(1)}, f32[256,256]{1,0:T(8,128)S(1)}, u32[]{:S(2)}, u32[]{:S(2)}) collective-permute-start(f32[256,256]{1,0:T(8,128)S(1)} %shard_map.38.refs_0_), channel_id=1, source_target_pairs={{8,18},{9,19},{10,16},{11,17}} | collective-permute-start | bytes 786440 | tf_op jit(solution)/shard_map/ppermute | solution.py:106
  27.4 2.2 %collective-permute-start.9 = (f32[256,256]{1,0:T(8,128)S(1)}, f32[256,256]{1,0:T(8,128)S(1)}, u32[]{:S(2)}, u32[]{:S(2)}) collective-permute-start(f32[256,256]{1,0:T(8,128)S(1)} %shard_map.38.refs_0_), channel_id=1, source_target_pairs={{8,2},{9,3},{10,0},{11,1},{24,18},{25,19},{26,16},{27,17}} | collective-permute-start | bytes 786440 | tf_op jit(solution)/shard_map/ppermute | solution.py:106
  29.6 1.3 collective-permute-start.15
  30.9 1.3 collective-permute-start.13
  32.2 4.3 %collective-permute-done.11.refs_5_ = f32[256,256]{1,0:T(8,128)S(1)} collective-permute-done((f32[256,256]{1,0:T(8,128)S(1)}, f32[256,256]{1,0:T(8,128)S(1)}, u32[]{:S(2)}, u32[]{:S(2)}) %collective-permute-start.11) | collective-permute-done | bytes 262176 | tf_op jit(solution)/shard_map/ppermute | solution.py:106
  36.5 0.5 collective-permute-start.10
  37.0 4.3 %collective-permute-done.15.refs_5_ = f32[256,256]{1,0:T(8,128)S(1)} collective-permute-done((f32[256,256]{1,0:T(8,128)S(1)}, f32[256,256]{1,0:T(8,128)S(1)}, u32[]{:S(2)}, u32[]{:S(2)}) %collective-permute-start.15) | collective-permute-done | bytes 262176 | tf_op jit(solution)/shard_map/ppermute | solution.py:106
  41.8 0.6 shard_map.39.refs_0_
  43.2 0.6 shard_map.40.refs_0_
  43.9 0.7 collective-permute-start.17
  44.5 0.7 collective-permute-start.19
  45.8 1.0 collective-permute-done.18.refs_3_
  47.7 1.0 collective-permute-start.22
  48.7 7.4 %collective-permute-done.22.refs_2_ = f32[256,256]{1,0:T(8,128)S(1)} collective-permute-done((f32[256,256]{1,0:T(8,128)S(1)}, f32[256,256]{1,0:T(8,128)S(1)}, u32[]{:S(2)}, u32[]{:S(2)}) %collective-permute-start.22) | collective-permute-done | bytes 262176 | tf_op jit(solution)/shard_map/ppermute | solution.py:106
  56.5 1.1 collective-permute-done.23.refs_3_
  58.0 0.7 collective-permute-start.24
  58.7 0.7 collective-permute-start.26
  60.0 1.0 collective-permute-done.25.refs_3_
  61.8 1.3 collective-permute-start.30
  63.1 1.3 collective-permute-start.28
  64.4 1.3 collective-permute-start.34
  65.7 1.3 collective-permute-start.32
  67.0 34.8 %collective-permute-done.30.refs_6_ = f32[256,256]{1,0:T(8,128)S(1)} collective-permute-done((f32[256,256]{1,0:T(8,128)S(1)}, f32[256,256]{1,0:T(8,128)S(1)}, u32[]{:S(2)}, u32[]{:S(2)}) %collective-permute-start.30) | collective-permute-done | bytes 262176 | tf_op jit(solution)/shard_map/ppermute | solution.py:106
  101.8 3.7 %collective-permute-done.28.refs_3_ = f32[256,256]{1,0:T(8,128)S(1)} collective-permute-done((f32[256,256]{1,0:T(8,128)S(1)}, f32[256,256]{1,0:T(8,128)S(1)}, u32[]{:S(2)}, u32[]{:S(2)}) %collective-permute-start.28) | collective-permute-done | bytes 262176 | tf_op jit(solution)/shard_map/ppermute | solution.py:106
  106.0 4.1 %collective-permute-done.32.refs_2_ = f32[256,256]{1,0:T(8,128)S(1)} collective-permute-done((f32[256,256]{1,0:T(8,128)S(1)}, f32[256,256]{1,0:T(8,128)S(1)}, u32[]{:S(2)}, u32[]{:S(2)}) %collective-permute-start.32) | collective-permute-done | bytes 262176 | tf_op jit(solution)/shard_map/ppermute | solution.py:106
  110.1 0.6 shard_map.47.refs_0_
  110.7 0.9 collective-permute-done.33.refs_3_
  111.6 0.6 shard_map.48.refs_1_
  112.3 1.3 collective-permute-start.36
  113.6 7.9 %collective-permute-done.42 = f32[256,256]{1,0:T(8,128)S(1)} collective-permute-done((f32[256,256]{1,0:T(8,128)S(1)}, f32[256,256]{1,0:T(8,128)S(1)}, u32[]{:S(2)}, u32[]{:S(2)}) %collective-permute-start.42) | collective-permute-done | bytes 262176 | tf_op jit(solution)/shard_map/ppermute | solution.py:106
  121.5 1.3 collective-permute-start.43
  122.9 1.2 collective-permute-start.38
  124.1 4.0 %collective-permute-done.43.refs_10_ = f32[256,256]{1,0:T(8,128)S(1)} collective-permute-done((f32[256,256]{1,0:T(8,128)S(1)}, f32[256,256]{1,0:T(8,128)S(1)}, u32[]{:S(2)}, u32[]{:S(2)}) %collective-permute-start.43) | collective-permute-done | bytes 262176 | tf_op jit(solution)/shard_map/ppermute | solution.py:106
  128.1 2.3 %collective-permute-done.40.refs_8_ = f32[256,256]{1,0:T(8,128)S(1)} collective-permute-done((f32[256,256]{1,0:T(8,128)S(1)}, f32[256,256]{1,0:T(8,128)S(1)}, u32[]{:S(2)}, u32[]{:S(2)}) %collective-permute-start.40) | collective-permute-done | bytes 262176 | tf_op jit(solution)/shard_map/ppermute | solution.py:106
  130.9 1.0 collective-permute-done.41.refs_9_
  132.3 1.8 %shard_map.49 = f32[256,256]{1,0:T(8,128)} custom-call(f32[256,256]{1,0:T(8,128)S(1)} %shard_map.44.refs_0_, f32[256,256]{1,0:T(8,128)S(1)} %shard_map.48.refs_1_, f32[256,1024]{1,0:T(8,128)S(1)} %get-tuple-element.37.refs_1_.refs_5_.refs_4_.refs_2_, f32[256,256]{1,0:T(8,128)S(1)} %collective-permute-done.36.refs_3_, ...), custom_call_target="tpu_custom_call" | custom-call | flops 805306368 | tf_op jit(solution)/shard_map/pallas_call | solution.py:62
  (61 shorter events, 7.6 us)
Async XLA Ops:
  0.0 10.3 %collective-permute-start = (f32[256,256]{1,0:T(8,128)}, f32[256,256]{1,0:T(8,128)S(1)}, u32[]{:S(2)}, u32[]{:S(2)}) collective-permute-start(f32[256,256]{1,0:T(8,128)} %bitcast.6), channel_id=1, source_target_pairs={{4,0},{5,1},{6,2},{7,3},{12,8},{13,9},{14,10},{15,11},{20,16},{21,... | collective-permute-start | bytes 786440 | tf_op jit(solution)/shard_map/ppermute | solution.py:106
  1.3 9.2 %collective-permute-start.6 = (f32[256,256]{1,0:T(8,128)}, f32[256,256]{1,0:T(8,128)S(1)}, u32[]{:S(2)}, u32[]{:S(2)}) collective-permute-start(f32[256,256]{1,0:T(8,128)} %bitcast.7), channel_id=1, source_target_pairs={{0,10},{1,11},{2,8},{3,9},{4,14},{5,15},{6,12},{7,13},{8,18},{9,19... | collective-permute-start | bytes 786440 | tf_op jit(solution)/shard_map/ppermute | solution.py:106
  3.9 2.8 %copy-start = (f32[3,1,2,256,1024]{4,3,2,1,0:T(8,128)S(1)}, f32[3,1,2,256,1024]{4,3,2,1,0:T(8,128)}, u32[]{:S(2)}) copy-start(f32[3,1,2,256,1024]{4,3,2,1,0:T(8,128)} %param.4) | copy-start | bytes 18874372
  6.7 1.9 %copy-start.1 = (f32[1,3,256,1024]{3,2,1,0:T(8,128)S(1)}, f32[1,3,256,1024]{3,2,1,0:T(8,128)}, u32[]{:S(2)}) copy-start(f32[1,3,256,1024]{3,2,1,0:T(8,128)} %param.5) | copy-start | bytes 9437188
  8.5 13.7 %copy-start.2 = (f32[1,256,256]{2,1,0:T(8,128)S(1)}, f32[1,256,256]{2,1,0:T(8,128)}, u32[]{:S(2)}) copy-start(f32[1,256,256]{2,1,0:T(8,128)} %param.3) | copy-start | bytes 786436
  10.5 9.5 %collective-permute-start.7 = (f32[256,256]{1,0:T(8,128)S(1)}, f32[256,256]{1,0:T(8,128)S(1)}, u32[]{:S(2)}, u32[]{:S(2)}) collective-permute-start(f32[256,256]{1,0:T(8,128)S(1)} %collective-permute-done.6), channel_id=1, source_target_pairs={{4,0},{5,1},{6,2},{7,3},{12,8},{13,9},{14,10},{15,11},{20,16},{21,... | collective-permute-start | bytes 786440 | tf_op jit(solution)/shard_map/ppermute | solution.py:106
  11.8 8.2 %collective-permute-start.4 = (f32[256,256]{1,0:T(8,128)S(1)}, f32[256,256]{1,0:T(8,128)S(1)}, u32[]{:S(2)}, u32[]{:S(2)}) collective-permute-start(f32[256,256]{1,0:T(8,128)S(1)} %collective-permute-done.refs_2_), channel_id=1, source_target_pairs={{0,8},{1,9},{2,10},{3,11},{4,12},{5,13},{6,14},{7,15},{8,16},{9,17... | collective-permute-start | bytes 786440 | tf_op jit(solution)/shard_map/ppermute | solution.py:106
  13.4 7.3 %collective-permute-start.2 = (f32[256,256]{1,0:T(8,128)S(1)}, f32[256,256]{1,0:T(8,128)S(1)}, u32[]{:S(2)}, u32[]{:S(2)}) collective-permute-start(f32[256,256]{1,0:T(8,128)S(1)} %collective-permute-done.refs_2_), channel_id=1, source_target_pairs={{0,2},{1,3},{2,0},{3,1},{4,6},{5,7},{6,4},{7,5},{8,10},{9,11},{10,... | collective-permute-start | bytes 786440 | tf_op jit(solution)/shard_map/ppermute | solution.py:106
  14.9 5.8 %collective-permute-start.1 = (f32[256,256]{1,0:T(8,128)S(1)}, f32[256,256]{1,0:T(8,128)S(1)}, u32[]{:S(2)}, u32[]{:S(2)}) collective-permute-start(f32[256,256]{1,0:T(8,128)S(1)} %collective-permute-done.refs_2_), channel_id=1, source_target_pairs={{0,1},{1,0},{2,3},{3,2},{4,5},{5,4},{6,7},{7,6},{8,9},{9,8},{10,11... | collective-permute-start | bytes 786440 | tf_op jit(solution)/shard_map/ppermute | solution.py:106
  20.0 1.5 %collective-permute-start.8 = (f32[256,256]{1,0:T(8,128)S(1)}, f32[256,256]{1,0:T(8,128)S(1)}, u32[]{:S(2)}, u32[]{:S(2)}) collective-permute-start(f32[256,256]{1,0:T(8,128)S(1)} %collective-permute-done.7.refs_9_), channel_id=1, source_target_pairs={{0,1},{1,0},{2,3},{3,2},{4,5},{5,4},{6,7},{7,6},{8,9},{9,8},{10,11... | collective-permute-start | bytes 786440 | tf_op jit(solution)/shard_map/ppermute | solution.py:106
  20.0 1.9 %collective-permute-start.5 = (f32[256,256]{1,0:T(8,128)S(1)}, f32[256,256]{1,0:T(8,128)S(1)}, u32[]{:S(2)}, u32[]{:S(2)}) collective-permute-start(f32[256,256]{1,0:T(8,128)S(1)} %collective-permute-done.4.refs_7_), channel_id=1, source_target_pairs={{0,1},{1,0},{2,3},{3,2},{4,5},{5,4},{6,7},{7,6},{8,9},{9,8},{10,11... | collective-permute-start | bytes 786440 | tf_op jit(solution)/shard_map/ppermute | solution.py:106
  20.7 1.5 %collective-permute-start.3 = (f32[256,256]{1,0:T(8,128)S(1)}, f32[256,256]{1,0:T(8,128)S(1)}, u32[]{:S(2)}, u32[]{:S(2)}) collective-permute-start(f32[256,256]{1,0:T(8,128)S(1)} %collective-permute-done.2.refs_4_), channel_id=1, source_target_pairs={{0,1},{1,0},{2,3},{3,2},{4,5},{5,4},{6,7},{7,6},{8,9},{9,8},{10,11... | collective-permute-start | bytes 786440 | tf_op jit(solution)/shard_map/ppermute | solution.py:106
  23.3 13.2 %collective-permute-start.11 = (f32[256,256]{1,0:T(8,128)S(1)}, f32[256,256]{1,0:T(8,128)S(1)}, u32[]{:S(2)}, u32[]{:S(2)}) collective-permute-start(f32[256,256]{1,0:T(8,128)S(1)} %shard_map.38.refs_0_), channel_id=1, source_target_pairs={{8,18},{9,19},{10,16},{11,17}} | collective-permute-start | bytes 786440 | tf_op jit(solution)/shard_map/ppermute | solution.py:106
  27.4 9.1 %collective-permute-start.9 = (f32[256,256]{1,0:T(8,128)S(1)}, f32[256,256]{1,0:T(8,128)S(1)}, u32[]{:S(2)}, u32[]{:S(2)}) collective-permute-start(f32[256,256]{1,0:T(8,128)S(1)} %shard_map.38.refs_0_), channel_id=1, source_target_pairs={{8,2},{9,3},{10,0},{11,1},{24,18},{25,19},{26,16},{27,17}} | collective-permute-start | bytes 786440 | tf_op jit(solution)/shard_map/ppermute | solution.py:106
  29.6 11.7 %collective-permute-start.15 = (f32[256,256]{1,0:T(8,128)S(1)}, f32[256,256]{1,0:T(8,128)S(1)}, u32[]{:S(2)}, u32[]{:S(2)}) collective-permute-start(f32[256,256]{1,0:T(8,128)S(1)} %shard_map.38.refs_0_), channel_id=1, source_target_pairs={{8,16},{9,17},{10,18},{11,19}} | collective-permute-start | bytes 786440 | tf_op jit(solution)/shard_map/ppermute | solution.py:106
  30.9 10.4 %collective-permute-start.13 = (f32[256,256]{1,0:T(8,128)S(1)}, f32[256,256]{1,0:T(8,128)S(1)}, u32[]{:S(2)}, u32[]{:S(2)}) collective-permute-start(f32[256,256]{1,0:T(8,128)S(1)} %shard_map.38.refs_0_), channel_id=1, source_target_pairs={{8,0},{9,1},{10,2},{11,3},{24,16},{25,17},{26,18},{27,19}} | collective-permute-start | bytes 786440 | tf_op jit(solution)/shard_map/ppermute | solution.py:106
  36.5 5.3 %collective-permute-start.12 = (f32[256,256]{1,0:T(8,128)S(1)}, f32[256,256]{1,0:T(8,128)S(1)}, u32[]{:S(2)}, u32[]{:S(2)}) collective-permute-start(f32[256,256]{1,0:T(8,128)S(1)} %collective-permute-done.11.refs_5_), channel_id=1, source_target_pairs={{0,1},{1,0},{2,3},{3,2},{4,5},{5,4},{6,7},{7,6},{8,9},{9,8},{10,11... | collective-permute-start | bytes 786440 | tf_op jit(solution)/shard_map/ppermute | solution.py:106
  36.5 5.3 %collective-permute-start.10 = (f32[256,256]{1,0:T(8,128)S(1)}, f32[256,256]{1,0:T(8,128)S(1)}, u32[]{:S(2)}, u32[]{:S(2)}) collective-permute-start(f32[256,256]{1,0:T(8,128)S(1)} %collective-permute-done.9.refs_2_), channel_id=1, source_target_pairs={{0,1},{1,0},{2,3},{3,2},{4,5},{5,4},{6,7},{7,6},{8,9},{9,8},{10,11... | collective-permute-start | bytes 786440 | tf_op jit(solution)/shard_map/ppermute | solution.py:106
  41.3 1.5 %collective-permute-start.16 = (f32[256,256]{1,0:T(8,128)S(1)}, f32[256,256]{1,0:T(8,128)S(1)}, u32[]{:S(2)}, u32[]{:S(2)}) collective-permute-start(f32[256,256]{1,0:T(8,128)S(1)} %collective-permute-done.15.refs_5_), channel_id=1, source_target_pairs={{0,1},{1,0},{2,3},{3,2},{4,5},{5,4},{6,7},{7,6},{8,9},{9,8},{10,11... | collective-permute-start | bytes 786440 | tf_op jit(solution)/shard_map/ppermute | solution.py:106
  41.3 1.9 %collective-permute-start.14 = (f32[256,256]{1,0:T(8,128)S(1)}, f32[256,256]{1,0:T(8,128)S(1)}, u32[]{:S(2)}, u32[]{:S(2)}) collective-permute-start(f32[256,256]{1,0:T(8,128)S(1)} %collective-permute-done.13.refs_2_), channel_id=1, source_target_pairs={{0,1},{1,0},{2,3},{3,2},{4,5},{5,4},{6,7},{7,6},{8,9},{9,8},{10,11... | collective-permute-start | bytes 786440 | tf_op jit(solution)/shard_map/ppermute | solution.py:106
  43.9 1.4 %collective-permute-start.17 = (f32[256,256]{1,0:T(8,128)S(1)}, f32[256,256]{1,0:T(8,128)S(1)}, u32[]{:S(2)}, u32[]{:S(2)}) collective-permute-start(f32[256,256]{1,0:T(8,128)S(1)} %shard_map.40.refs_0_), channel_id=1, source_target_pairs={{16,2},{17,3},{18,0},{19,1}} | collective-permute-start | bytes 786440 | tf_op jit(solution)/shard_map/ppermute | solution.py:106
  44.5 0.9 collective-permute-start.19
  45.2 1.6 %collective-permute-start.18 = (f32[256,256]{1,0:T(8,128)S(1)}, f32[256,256]{1,0:T(8,128)S(1)}, u32[]{:S(2)}, u32[]{:S(2)}) collective-permute-start(f32[256,256]{1,0:T(8,128)S(1)} %collective-permute-done.17.refs_2_), channel_id=1, source_target_pairs={{0,1},{1,0},{2,3},{3,2},{4,5},{5,4},{6,7},{7,6},{8,9},{9,8},{10,11... | collective-permute-start | bytes 786440 | tf_op jit(solution)/shard_map/ppermute | solution.py:106
  45.4 1.8 %collective-permute-start.20 = (f32[256,256]{1,0:T(8,128)S(1)}, f32[256,256]{1,0:T(8,128)S(1)}, u32[]{:S(2)}, u32[]{:S(2)}) collective-permute-start(f32[256,256]{1,0:T(8,128)S(1)} %collective-permute-done.19.refs_2_), channel_id=1, source_target_pairs={{0,1},{1,0},{2,3},{3,2},{4,5},{5,4},{6,7},{7,6},{8,9},{9,8},{10,11... | collective-permute-start | bytes 786440 | tf_op jit(solution)/shard_map/ppermute | solution.py:106
  47.7 8.4 %collective-permute-start.22 = (f32[256,256]{1,0:T(8,128)S(1)}, f32[256,256]{1,0:T(8,128)S(1)}, u32[]{:S(2)}, u32[]{:S(2)}) collective-permute-start(f32[256,256]{1,0:T(8,128)S(1)} %shard_map.42.refs_1_), channel_id=1, source_target_pairs={{0,2},{1,3},{2,0},{3,1},{4,6},{5,7},{6,4},{7,5},{8,10},{9,11},{10,... | collective-permute-start | bytes 786440 | tf_op jit(solution)/shard_map/ppermute | solution.py:106
  48.7 7.4 %collective-permute-start.21 = (f32[256,256]{1,0:T(8,128)S(1)}, f32[256,256]{1,0:T(8,128)S(1)}, u32[]{:S(2)}, u32[]{:S(2)}) collective-permute-start(f32[256,256]{1,0:T(8,128)S(1)} %shard_map.42.refs_1_), channel_id=1, source_target_pairs={{0,1},{1,0},{2,3},{3,2},{4,5},{5,4},{6,7},{7,6},{8,9},{9,8},{10,11... | collective-permute-start | bytes 786440 | tf_op jit(solution)/shard_map/ppermute | solution.py:106
  56.1 1.5 %collective-permute-start.23 = (f32[256,256]{1,0:T(8,128)S(1)}, f32[256,256]{1,0:T(8,128)S(1)}, u32[]{:S(2)}, u32[]{:S(2)}) collective-permute-start(f32[256,256]{1,0:T(8,128)S(1)} %collective-permute-done.22.refs_2_), channel_id=1, source_target_pairs={{0,1},{1,0},{2,3},{3,2},{4,5},{5,4},{6,7},{7,6},{8,9},{9,8},{10,11... | collective-permute-start | bytes 786440 | tf_op jit(solution)/shard_map/ppermute | solution.py:106
  58.0 1.4 %collective-permute-start.24 = (f32[256,256]{1,0:T(8,128)S(1)}, f32[256,256]{1,0:T(8,128)S(1)}, u32[]{:S(2)}, u32[]{:S(2)}) collective-permute-start(f32[256,256]{1,0:T(8,128)S(1)} %shard_map.44.refs_0_), channel_id=1, source_target_pairs={{0,18},{1,19},{2,16},{3,17}} | collective-permute-start | bytes 786440 | tf_op jit(solution)/shard_map/ppermute | solution.py:106
  58.7 0.9 collective-permute-start.26
  59.4 1.6 %collective-permute-start.25 = (f32[256,256]{1,0:T(8,128)S(1)}, f32[256,256]{1,0:T(8,128)S(1)}, u32[]{:S(2)}, u32[]{:S(2)}) collective-permute-start(f32[256,256]{1,0:T(8,128)S(1)} %collective-permute-done.24.refs_2_), channel_id=1, source_target_pairs={{0,1},{1,0},{2,3},{3,2},{4,5},{5,4},{6,7},{7,6},{8,9},{9,8},{10,11... | collective-permute-start | bytes 786440 | tf_op jit(solution)/shard_map/ppermute | solution.py:106
  59.6 1.8 %collective-permute-start.27 = (f32[256,256]{1,0:T(8,128)S(1)}, f32[256,256]{1,0:T(8,128)S(1)}, u32[]{:S(2)}, u32[]{:S(2)}) collective-permute-start(f32[256,256]{1,0:T(8,128)S(1)} %collective-permute-done.26.refs_2_), channel_id=1, source_target_pairs={{0,1},{1,0},{2,3},{3,2},{4,5},{5,4},{6,7},{7,6},{8,9},{9,8},{10,11... | collective-permute-start | bytes 786440 | tf_op jit(solution)/shard_map/ppermute | solution.py:106
  61.8 40.0 %collective-permute-start.30 = (f32[256,256]{1,0:T(8,128)S(1)}, f32[256,256]{1,0:T(8,128)S(1)}, u32[]{:S(2)}, u32[]{:S(2)}) collective-permute-start(f32[256,256]{1,0:T(8,128)S(1)} %shard_map.46.refs_1_), channel_id=1, source_target_pairs={{0,10},{1,11},{2,8},{3,9},{16,26},{17,27},{18,24},{19,25}} | collective-permute-start | bytes 786440 | tf_op jit(solution)/shard_map/ppermute | solution.py:106
  63.1 42.4 %collective-permute-start.28 = (f32[256,256]{1,0:T(8,128)S(1)}, f32[256,256]{1,0:T(8,128)S(1)}, u32[]{:S(2)}, u32[]{:S(2)}) collective-permute-start(f32[256,256]{1,0:T(8,128)S(1)} %shard_map.46.refs_1_), channel_id=1, source_target_pairs={{16,10},{17,11},{18,8},{19,9}} | collective-permute-start | bytes 786440 | tf_op jit(solution)/shard_map/ppermute | solution.py:106
  64.4 41.1 %collective-permute-start.34 = (f32[256,256]{1,0:T(8,128)S(1)}, f32[256,256]{1,0:T(8,128)S(1)}, u32[]{:S(2)}, u32[]{:S(2)}) collective-permute-start(f32[256,256]{1,0:T(8,128)S(1)} %shard_map.46.refs_1_), channel_id=1, source_target_pairs={{0,8},{1,9},{2,10},{3,11},{16,24},{17,25},{18,26},{19,27}} | collective-permute-start | bytes 786440 | tf_op jit(solution)/shard_map/ppermute | solution.py:106
  65.7 44.4 %collective-permute-start.32 = (f32[256,256]{1,0:T(8,128)S(1)}, f32[256,256]{1,0:T(8,128)S(1)}, u32[]{:S(2)}, u32[]{:S(2)}) collective-permute-start(f32[256,256]{1,0:T(8,128)S(1)} %shard_map.46.refs_1_), channel_id=1, source_target_pairs={{16,8},{17,9},{18,10},{19,11}} | collective-permute-start | bytes 786440 | tf_op jit(solution)/shard_map/ppermute | solution.py:106
  101.8 8.3 %collective-permute-start.31 = (f32[256,256]{1,0:T(8,128)S(1)}, f32[256,256]{1,0:T(8,128)S(1)}, u32[]{:S(2)}, u32[]{:S(2)}) collective-permute-start(f32[256,256]{1,0:T(8,128)S(1)} %collective-permute-done.30.refs_6_), channel_id=1, source_target_pairs={{0,1},{1,0},{2,3},{3,2},{4,5},{5,4},{6,7},{7,6},{8,9},{9,8},{10,11... | collective-permute-start | bytes 786440 | tf_op jit(solution)/shard_map/ppermute | solution.py:106
  105.5 4.6 %collective-permute-start.29 = (f32[256,256]{1,0:T(8,128)S(1)}, f32[256,256]{1,0:T(8,128)S(1)}, u32[]{:S(2)}, u32[]{:S(2)}) collective-permute-start(f32[256,256]{1,0:T(8,128)S(1)} %collective-permute-done.28.refs_3_), channel_id=1, source_target_pairs={{0,1},{1,0},{2,3},{3,2},{4,5},{5,4},{6,7},{7,6},{8,9},{9,8},{10,11... | collective-permute-start | bytes 786440 | tf_op jit(solution)/shard_map/ppermute | solution.py:106
  105.5 5.2 %collective-permute-start.35 = (f32[256,256]{1,0:T(8,128)S(1)}, f32[256,256]{1,0:T(8,128)S(1)}, u32[]{:S(2)}, u32[]{:S(2)}) collective-permute-start(f32[256,256]{1,0:T(8,128)S(1)} %collective-permute-done.34.refs_5_), channel_id=1, source_target_pairs={{0,1},{1,0},{2,3},{3,2},{4,5},{5,4},{6,7},{7,6},{8,9},{9,8},{10,11... | collective-permute-start | bytes 786440 | tf_op jit(solution)/shard_map/ppermute | solution.py:106
  110.1 1.5 %collective-permute-start.33 = (f32[256,256]{1,0:T(8,128)S(1)}, f32[256,256]{1,0:T(8,128)S(1)}, u32[]{:S(2)}, u32[]{:S(2)}) collective-permute-start(f32[256,256]{1,0:T(8,128)S(1)} %collective-permute-done.32.refs_2_), channel_id=1, source_target_pairs={{0,1},{1,0},{2,3},{3,2},{4,5},{5,4},{6,7},{7,6},{8,9},{9,8},{10,11... | collective-permute-start | bytes 786440 | tf_op jit(solution)/shard_map/ppermute | solution.py:106
  112.2 9.3 %collective-permute-start.42 = (f32[256,256]{1,0:T(8,128)S(1)}, f32[256,256]{1,0:T(8,128)S(1)}, u32[]{:S(2)}, u32[]{:S(2)}) collective-permute-start(f32[256,256]{1,0:T(8,128)S(1)} %shard_map.48.refs_1_), channel_id=1, source_target_pairs={{0,26},{1,27},{2,24},{3,25},{4,30},{5,31},{6,28},{7,29},{8,2},{9,3... | collective-permute-start | bytes 786440 | tf_op jit(solution)/shard_map/ppermute | solution.py:106
  112.3 10.5 %collective-permute-start.36 = (f32[256,256]{1,0:T(8,128)S(1)}, f32[256,256]{1,0:T(8,128)S(1)}, u32[]{:S(2)}, u32[]{:S(2)}) collective-permute-start(f32[256,256]{1,0:T(8,128)S(1)} %shard_map.48.refs_1_), channel_id=1, source_target_pairs={{0,4},{1,5},{2,6},{3,7},{8,12},{9,13},{10,14},{11,15},{16,20},{17,... | collective-permute-start | bytes 786440 | tf_op jit(solution)/shard_map/ppermute | solution.py:106
  121.5 6.6 %collective-permute-start.43 = (f32[256,256]{1,0:T(8,128)S(1)}, f32[256,256]{1,0:T(8,128)S(1)}, u32[]{:S(2)}, u32[]{:S(2)}) collective-permute-start(f32[256,256]{1,0:T(8,128)S(1)} %collective-permute-done.42), channel_id=1, source_target_pairs={{0,4},{1,5},{2,6},{3,7},{8,12},{9,13},{10,14},{11,15},{16,20},{17,... | collective-permute-start | bytes 786440 | tf_op jit(solution)/shard_map/ppermute | solution.py:106
  122.8 7.6 %collective-permute-start.40 = (f32[256,256]{1,0:T(8,128)S(1)}, f32[256,256]{1,0:T(8,128)S(1)}, u32[]{:S(2)}, u32[]{:S(2)}) collective-permute-start(f32[256,256]{1,0:T(8,128)S(1)} %collective-permute-done.36.refs_3_), channel_id=1, source_target_pairs={{0,24},{1,25},{2,26},{3,27},{4,28},{5,29},{6,30},{7,31},{8,0},{9,1... | collective-permute-start | bytes 786440 | tf_op jit(solution)/shard_map/ppermute | solution.py:106
  122.9 7.6 %collective-permute-start.38 = (f32[256,256]{1,0:T(8,128)S(1)}, f32[256,256]{1,0:T(8,128)S(1)}, u32[]{:S(2)}, u32[]{:S(2)}) collective-permute-start(f32[256,256]{1,0:T(8,128)S(1)} %collective-permute-done.36.refs_3_), channel_id=1, source_target_pairs={{0,2},{1,3},{2,0},{3,1},{4,6},{5,7},{6,4},{7,5},{8,10},{9,11},{10,... | collective-permute-start | bytes 786440 | tf_op jit(solution)/shard_map/ppermute | solution.py:106
  124.1 6.8 %collective-permute-start.37 = (f32[256,256]{1,0:T(8,128)S(1)}, f32[256,256]{1,0:T(8,128)S(1)}, u32[]{:S(2)}, u32[]{:S(2)}) collective-permute-start(f32[256,256]{1,0:T(8,128)S(1)} %collective-permute-done.36.refs_3_), channel_id=1, source_target_pairs={{0,1},{1,0},{2,3},{3,2},{4,5},{5,4},{6,7},{7,6},{8,9},{9,8},{10,11... | collective-permute-start | bytes 786440 | tf_op jit(solution)/shard_map/ppermute | solution.py:106
  128.1 2.8 %collective-permute-start.44 = (f32[256,256]{1,0:T(8,128)S(1)}, f32[256,256]{1,0:T(8,128)S(1)}, u32[]{:S(2)}, u32[]{:S(2)}) collective-permute-start(f32[256,256]{1,0:T(8,128)S(1)} %collective-permute-done.43.refs_10_), channel_id=1, source_target_pairs={{0,1},{1,0},{2,3},{3,2},{4,5},{5,4},{6,7},{7,6},{8,9},{9,8},{10,11... | collective-permute-start | bytes 786440 | tf_op jit(solution)/shard_map/ppermute | solution.py:106
  130.4 1.5 %collective-permute-start.41 = (f32[256,256]{1,0:T(8,128)S(1)}, f32[256,256]{1,0:T(8,128)S(1)}, u32[]{:S(2)}, u32[]{:S(2)}) collective-permute-start(f32[256,256]{1,0:T(8,128)S(1)} %collective-permute-done.40.refs_8_), channel_id=1, source_target_pairs={{0,1},{1,0},{2,3},{3,2},{4,5},{5,4},{6,7},{7,6},{8,9},{9,8},{10,11... | collective-permute-start | bytes 786440 | tf_op jit(solution)/shard_map/ppermute | solution.py:106
  130.5 1.8 %collective-permute-start.39 = (f32[256,256]{1,0:T(8,128)S(1)}, f32[256,256]{1,0:T(8,128)S(1)}, u32[]{:S(2)}, u32[]{:S(2)}) collective-permute-start(f32[256,256]{1,0:T(8,128)S(1)} %collective-permute-done.38.refs_5_), channel_id=1, source_target_pairs={{0,1},{1,0},{2,3},{3,2},{4,5},{5,4},{6,7},{7,6},{8,9},{9,8},{10,11... | collective-permute-start | bytes 786440 | tf_op jit(solution)/shard_map/ppermute | solution.py:106

commit v5 on v4

--- a/solution.py
+++ b/solution.py
@@ -159,18 +159,23 @@
         upper = swapped(direct(current, [(i, i - stride) for i in senders]))
         current = apply([current], -1, (right, upper), (left, lower), far_first=True)
 
-    upper = swapped(direct(current, [(layers // 2, 0)]))
-    current = apply([current], -1, (reduce_mats[levels - 1][1], upper), far_first=True)
-    base = apply([], 1, (inverse, swapped(within(current))))
-
-    result = base
-    for k in reversed(range(levels)):
+    half = layers // 2
+    width = current.shape[1] // 2
+    blocks = [current[:, :width], current[:, width:]]
+    bases, results = [], []
+    for block in blocks:
+        upper = swapped(direct(block, [(half, 0)]))
+        block = apply([block], -1, (reduce_mats[levels - 1][1], upper), far_first=True)
+        base = apply([], 1, (inverse, swapped(within(block))))
+        bases.append(base)
+        results.append(apply([base, base], -1, (west, swapped(direct(base, [(0, half)]))), only=(2 * half, half), far_first=True))
+    base, result = jnp.concatenate(bases, 1), jnp.concatenate(results, 1)
+
+    for k in reversed(range(levels - 1)):
         stride = 1 << k
         only = (2 * stride, stride)
         senders = range(0, layers, 2 * stride)
-        if k == levels - 1:
-            result = apply([base, result], -1, (west, swapped(direct(result, [(0, stride)]))), only=only, far_first=True)
-        elif k > 0:
+        if k > 0:
             lower = swapped(direct(result, [(j, j + stride) for j in senders]))
             upper = swapped(direct(result, [(j, j - stride) for j in senders]))
             result = apply([base, result], -1, (east, upper), (west, lower), only=only, far_first=True)
@@ -179,9 +184,12 @@
             passed = [(flip, move(result, ring(-2), flip)) for flip in range(2, rows, 2)]
             upper = swapped(far_shards(lower, passed, -1))
             lower = swapped(near_shards(lower))
+            part = combine(
+                [base, result], [(west, f, p) for f, p in lower[:2]] + [(east, f, p, (0, layers - 1)) for f, p in upper[2:]],
+                -1, only,
+            )
             result = combine(
-                [base, result],
-                [(west, f, p) for f, p in lower] + [(east, f, p, (0, layers - 1)) for f, p in upper], -1, only,
+                [part], [(west, f, p) for f, p in lower[2:]] + [(east, f, p, (0, layers - 1)) for f, p in upper[:2]], -1, only,
             )
     return result[None]
 

time: 136 us -> 135 us (level)
  waiting for transfers between devices: 86.1 us -> 76.9 us
  starting transfers between devices: 33.6 us -> 38.7 us
  Pallas kernels: 9.41 us -> 11.7 us
    ppermute x45 -> x56, waiting for transfers between devices: 86.1 us -> 76.9 us  [move(): return lax.ppermute(block, AXES, hops) if hops else None]
    ppermute x45 -> x56, starting transfers between devices: 33.6 us -> 38.7 us  [move(): return lax.ppermute(block, AXES, hops) if hops else None]
    pallas_call x12 -> x19, Pallas kernels: 7.68 us -> 9.99 us  [combine(): pl.pallas_call(functools.partial(combine_kernel, shape, sign, only), out_...]
  transfers between devices with their start and end apart: 45 -> 56, of which waited for: 24 -> 25; matrix products, arithmetic and copies ran while one was open for 0% -> 0% of each run, Pallas kernels for 3% -> 6%
where the time goes in v5:
time: 135 us; the launch traced here: 133 us
  waiting for transfers between devices  76.9 us (57%)
  starting transfers between devices  38.7 us (29%)
  Pallas kernels  11.7 us (9%)
  local copies, waits for them, and re-layouts  4.7 us (3%)
    ppermute x56, waiting for transfers between devices, move(): return lax.ppermute(block, AXES, hops) if hops else None  76.9 us
    ppermute x56, starting transfers between devices, move(): return lax.ppermute(block, AXES, hops) if hops else None  38.7 us
    pallas_call x19, Pallas kernels, combine(): pl.pallas_call(functools.partial(combine_kernel, shape, sign, only), out_...  9.99 us
    unnamed x6, local copies, waits for them, and re-layouts  4.68 us
  transfers between devices with their start and end apart: 56, of which 25 were waited for; matrix products, arithmetic and copies ran while one was open for 0% of the time, Pallas kernels for 6%

profile of v5, /device:TPU:8, one launch (start us, length us, event | category | flops | bytes accessed | tf_op | source)
XLA Modules:
  0.0 132.5 jit_solution(16866352061143308975)
XLA Ops:
  0.0 1.3 collective-permute-start
  1.3 2.6 %collective-permute-start.6 = (f32[256,256]{1,0:T(8,128)}, f32[256,256]{1,0:T(8,128)S(1)}, u32[]{:S(2)}, u32[]{:S(2)}) collective-permute-start(f32[256,256]{1,0:T(8,128)} %bitcast.7), channel_id=1, source_target_pairs={{0,10},{1,11},{2,8},{3,9},{4,14},{5,15},{6,12},{7,13},{8,18},{9,19... | collective-permute-start | bytes 786440 | tf_op jit(solution)/shard_map/ppermute | solution.py:106
  3.9 2.8 %copy-done = f32[3,1,2,256,1024]{4,3,2,1,0:T(8,128)S(1)} copy-done((f32[3,1,2,256,1024]{4,3,2,1,0:T(8,128)S(1)}, f32[3,1,2,256,1024]{4,3,2,1,0:T(8,128)}, u32[]{:S(2)}) %copy-start) | copy-done | bytes 6291480
  6.7 1.9 %copy-done.1 = f32[1,3,256,1024]{3,2,1,0:T(8,128)S(1)} copy-done((f32[1,3,256,1024]{3,2,1,0:T(8,128)S(1)}, f32[1,3,256,1024]{3,2,1,0:T(8,128)}, u32[]{:S(2)}) %copy-start.1) | copy-done | bytes 3145752
  8.6 1.7 %shard_map.37 = (f32[256,1024]{1,0:T(8,128)S(1)}, f32[256,1024]{1,0:T(8,128)S(1)}, f32[256,1024]{1,0:T(8,128)S(1)}, f32[256,1024]{1,0:T(8,128)S(1)}, f32[256,102...) custom-call(f32[3,2,256,1024]{3,2,1,0:T(8,128)S(1)} %bitcast.4, ...), custom_call_target="tpu_custom_call" | custom-call | tf_op jit(solution)/shard_map/pallas_call | solution.py:87
  10.5 1.3 collective-permute-start.7
  11.8 1.6 %collective-permute-start.4 = (f32[256,256]{1,0:T(8,128)S(1)}, f32[256,256]{1,0:T(8,128)S(1)}, u32[]{:S(2)}, u32[]{:S(2)}) collective-permute-start(f32[256,256]{1,0:T(8,128)S(1)} %collective-permute-done.refs_2_), channel_id=1, source_target_pairs={{0,8},{1,9},{2,10},{3,11},{4,12},{5,13},{6,14},{7,15},{8,16},{9,17... | collective-permute-start | bytes 786440 | tf_op jit(solution)/shard_map/ppermute | solution.py:106
  13.4 1.5 %collective-permute-start.2 = (f32[256,256]{1,0:T(8,128)S(1)}, f32[256,256]{1,0:T(8,128)S(1)}, u32[]{:S(2)}, u32[]{:S(2)}) collective-permute-start(f32[256,256]{1,0:T(8,128)S(1)} %collective-permute-done.refs_2_), channel_id=1, source_target_pairs={{0,2},{1,3},{2,0},{3,1},{4,6},{5,7},{6,4},{7,5},{8,10},{9,11},{10,... | collective-permute-start | bytes 786440 | tf_op jit(solution)/shard_map/ppermute | solution.py:106
  14.9 5.1 %collective-permute-done.7.refs_9_ = f32[256,256]{1,0:T(8,128)S(1)} collective-permute-done((f32[256,256]{1,0:T(8,128)S(1)}, f32[256,256]{1,0:T(8,128)S(1)}, u32[]{:S(2)}, u32[]{:S(2)}) %collective-permute-start.7) | collective-permute-done | bytes 262176 | tf_op jit(solution)/shard_map/ppermute | solution.py:106
  20.7 0.8 collective-permute-done.8.refs_10_
  22.3 1.1 shard_map.38.refs_0_
  23.3 4.0 %collective-permute-start.11 = (f32[256,256]{1,0:T(8,128)S(1)}, f32[256,256]{1,0:T(8,128)S(1)}, u32[]{:S(2)}, u32[]{:S(2)}) collective-permute-start(f32[256,256]{1,0:T(8,128)S(1)} %shard_map.38.refs_0_), channel_id=1, source_target_pairs={{8,18},{9,19},{10,16},{11,17}} | collective-permute-start | bytes 786440 | tf_op jit(solution)/shard_map/ppermute | solution.py:106
  27.4 2.2 %collective-permute-start.9 = (f32[256,256]{1,0:T(8,128)S(1)}, f32[256,256]{1,0:T(8,128)S(1)}, u32[]{:S(2)}, u32[]{:S(2)}) collective-permute-start(f32[256,256]{1,0:T(8,128)S(1)} %shard_map.38.refs_0_), channel_id=1, source_target_pairs={{8,2},{9,3},{10,0},{11,1},{24,18},{25,19},{26,16},{27,17}} | collective-permute-start | bytes 786440 | tf_op jit(solution)/shard_map/ppermute | solution.py:106
  29.6 1.3 collective-permute-start.15
  30.9 1.3 collective-permute-start.13
  32.2 4.3 %collective-permute-done.11.refs_5_ = f32[256,256]{1,0:T(8,128)S(1)} collective-permute-done((f32[256,256]{1,0:T(8,128)S(1)}, f32[256,256]{1,0:T(8,128)S(1)}, u32[]{:S(2)}, u32[]{:S(2)}) %collective-permute-start.11) | collective-permute-done | bytes 262176 | tf_op jit(solution)/shard_map/ppermute | solution.py:106
  37.0 4.3 %collective-permute-done.15.refs_5_ = f32[256,256]{1,0:T(8,128)S(1)} collective-permute-done((f32[256,256]{1,0:T(8,128)S(1)}, f32[256,256]{1,0:T(8,128)S(1)}, u32[]{:S(2)}, u32[]{:S(2)}) %collective-permute-start.15) | collective-permute-done | bytes 262176 | tf_op jit(solution)/shard_map/ppermute | solution.py:106
  41.8 0.6 shard_map.39.refs_0_
  43.9 0.7 collective-permute-start.17
  44.6 0.7 collective-permute-start.19
  45.2 0.7 collective-permute-start.24
  45.9 0.7 collective-permute-start.26
  48.8 1.0 collective-permute-start.22
  50.5 1.1 collective-permute-start.29
  52.2 3.0 %collective-permute-done.22.refs_2_ = f32[256,128]{1,0:T(8,128)S(1)} collective-permute-done((f32[256,128]{1,0:T(8,128)S(1)}, f32[256,128]{1,0:T(8,128)S(1)}, u32[]{:S(2)}, u32[]{:S(2)}) %collective-permute-start.22) | collective-permute-done | bytes 131104 | tf_op jit(solution)/shard_map/ppermute | solution.py:106
  55.2 2.0 %collective-permute-done.29.refs_2_ = f32[256,128]{1,0:T(8,128)S(1)} collective-permute-done((f32[256,128]{1,0:T(8,128)S(1)}, f32[256,128]{1,0:T(8,128)S(1)}, u32[]{:S(2)}, u32[]{:S(2)}) %collective-permute-start.29) | collective-permute-done | bytes 131104 | tf_op jit(solution)/shard_map/ppermute | solution.py:106
  58.4 0.7 collective-permute-start.31
  59.4 0.7 collective-permute-start.35
  60.1 0.7 collective-permute-start.33
  60.8 0.7 collective-permute-start.37
  64.6 1.3 collective-permute-start.41
  65.9 1.3 collective-permute-start.39
  67.2 1.3 collective-permute-start.45
  68.5 1.3 collective-permute-start.43
  69.8 30.9 %collective-permute-done.41.refs_6_ = f32[256,256]{1,0:T(8,128)S(1)} collective-permute-done((f32[256,256]{1,0:T(8,128)S(1)}, f32[256,256]{1,0:T(8,128)S(1)}, u32[]{:S(2)}, u32[]{:S(2)}) %collective-permute-start.41) | collective-permute-done | bytes 262176 | tf_op jit(solution)/shard_map/ppermute | solution.py:106
  100.7 3.5 %collective-permute-done.39.refs_3_ = f32[256,256]{1,0:T(8,128)S(1)} collective-permute-done((f32[256,256]{1,0:T(8,128)S(1)}, f32[256,256]{1,0:T(8,128)S(1)}, u32[]{:S(2)}, u32[]{:S(2)}) %collective-permute-start.39) | collective-permute-done | bytes 262176 | tf_op jit(solution)/shard_map/ppermute | solution.py:106
  104.7 4.2 %collective-permute-done.43.refs_2_ = f32[256,256]{1,0:T(8,128)S(1)} collective-permute-done((f32[256,256]{1,0:T(8,128)S(1)}, f32[256,256]{1,0:T(8,128)S(1)}, u32[]{:S(2)}, u32[]{:S(2)}) %collective-permute-start.43) | collective-permute-done | bytes 262176 | tf_op jit(solution)/shard_map/ppermute | solution.py:106
  109.0 0.7 shard_map.53.refs_0_
  109.7 0.8 collective-permute-done.44.refs_3_
  110.5 0.6 shard_map.54.refs_1_
  111.2 1.3 collective-permute-start.47
  112.5 7.9 %collective-permute-done.49 = f32[256,256]{1,0:T(8,128)S(1)} collective-permute-done((f32[256,256]{1,0:T(8,128)S(1)}, f32[256,256]{1,0:T(8,128)S(1)}, u32[]{:S(2)}, u32[]{:S(2)}) %collective-permute-start.49) | collective-permute-done | bytes 262176 | tf_op jit(solution)/shard_map/ppermute | solution.py:106
  120.4 1.3 collective-permute-start.50
  121.8 1.1 collective-permute-start.52
  123.0 4.0 %collective-permute-done.50.refs_6_ = f32[256,256]{1,0:T(8,128)S(1)} collective-permute-done((f32[256,256]{1,0:T(8,128)S(1)}, f32[256,256]{1,0:T(8,128)S(1)}, u32[]{:S(2)}, u32[]{:S(2)}) %collective-permute-start.50) | collective-permute-done | bytes 262176 | tf_op jit(solution)/shard_map/ppermute | solution.py:106
  127.0 2.3 %collective-permute-done.54.refs_5_ = f32[256,256]{1,0:T(8,128)S(1)} collective-permute-done((f32[256,256]{1,0:T(8,128)S(1)}, f32[256,256]{1,0:T(8,128)S(1)}, u32[]{:S(2)}, u32[]{:S(2)}) %collective-permute-start.54) | collective-permute-done | bytes 262176 | tf_op jit(solution)/shard_map/ppermute | solution.py:106
  129.8 0.6 shard_map.55.refs_0_
  131.2 1.3 %shard_map.56 = f32[256,256]{1,0:T(8,128)} custom-call(f32[256,256]{1,0:T(8,128)S(1)} %shard_map.55.refs_0_, f32[256,1024]{1,0:T(8,128)S(1)} %get-tuple-element.37.refs_1_.refs_5_.refs_4_.refs_2_, f32[256,256]{1,0:T(8,128)S(1)} %collective-permute-done.52.refs_2_, f32[256,256]{1,0:T(8,128)S(1)} %collective-permute-done.53.refs_3_, ...), custom_call_target="tpu_custom_call" | custom-call | flops 402653184 | tf_op jit(solution)/shard_map/pallas_call | solution.py:62
  (93 shorter events, 14.0 us)
Async XLA Ops:
  0.0 10.3 %collective-permute-start = (f32[256,256]{1,0:T(8,128)}, f32[256,256]{1,0:T(8,128)S(1)}, u32[]{:S(2)}, u32[]{:S(2)}) collective-permute-start(f32[256,256]{1,0:T(8,128)} %bitcast.6), channel_id=1, source_target_pairs={{4,0},{5,1},{6,2},{7,3},{12,8},{13,9},{14,10},{15,11},{20,16},{21,... | collective-permute-start | bytes 786440 | tf_op jit(solution)/shard_map/ppermute | solution.py:106
  1.3 9.2 %collective-permute-start.6 = (f32[256,256]{1,0:T(8,128)}, f32[256,256]{1,0:T(8,128)S(1)}, u32[]{:S(2)}, u32[]{:S(2)}) collective-permute-start(f32[256,256]{1,0:T(8,128)} %bitcast.7), channel_id=1, source_target_pairs={{0,10},{1,11},{2,8},{3,9},{4,14},{5,15},{6,12},{7,13},{8,18},{9,19... | collective-permute-start | bytes 786440 | tf_op jit(solution)/shard_map/ppermute | solution.py:106
  10.5 9.5 %collective-permute-start.7 = (f32[256,256]{1,0:T(8,128)S(1)}, f32[256,256]{1,0:T(8,128)S(1)}, u32[]{:S(2)}, u32[]{:S(2)}) collective-permute-start(f32[256,256]{1,0:T(8,128)S(1)} %collective-permute-done.6), channel_id=1, source_target_pairs={{4,0},{5,1},{6,2},{7,3},{12,8},{13,9},{14,10},{15,11},{20,16},{21,... | collective-permute-start | bytes 786440 | tf_op jit(solution)/shard_map/ppermute | solution.py:106
  11.8 8.2 %collective-permute-start.4 = (f32[256,256]{1,0:T(8,128)S(1)}, f32[256,256]{1,0:T(8,128)S(1)}, u32[]{:S(2)}, u32[]{:S(2)}) collective-permute-start(f32[256,256]{1,0:T(8,128)S(1)} %collective-permute-done.refs_2_), channel_id=1, source_target_pairs={{0,8},{1,9},{2,10},{3,11},{4,12},{5,13},{6,14},{7,15},{8,16},{9,17... | collective-permute-start | bytes 786440 | tf_op jit(solution)/shard_map/ppermute | solution.py:106
  13.4 7.3 %collective-permute-start.2 = (f32[256,256]{1,0:T(8,128)S(1)}, f32[256,256]{1,0:T(8,128)S(1)}, u32[]{:S(2)}, u32[]{:S(2)}) collective-permute-start(f32[256,256]{1,0:T(8,128)S(1)} %collective-permute-done.refs_2_), channel_id=1, source_target_pairs={{0,2},{1,3},{2,0},{3,1},{4,6},{5,7},{6,4},{7,5},{8,10},{9,11},{10,... | collective-permute-start | bytes 786440 | tf_op jit(solution)/shard_map/ppermute | solution.py:106
  14.9 5.8 %collective-permute-start.1 = (f32[256,256]{1,0:T(8,128)S(1)}, f32[256,256]{1,0:T(8,128)S(1)}, u32[]{:S(2)}, u32[]{:S(2)}) collective-permute-start(f32[256,256]{1,0:T(8,128)S(1)} %collective-permute-done.refs_2_), channel_id=1, source_target_pairs={{0,1},{1,0},{2,3},{3,2},{4,5},{5,4},{6,7},{7,6},{8,9},{9,8},{10,11... | collective-permute-start | bytes 786440 | tf_op jit(solution)/shard_map/ppermute | solution.py:106
  20.0 1.9 %collective-permute-start.5 = (f32[256,256]{1,0:T(8,128)S(1)}, f32[256,256]{1,0:T(8,128)S(1)}, u32[]{:S(2)}, u32[]{:S(2)}) collective-permute-start(f32[256,256]{1,0:T(8,128)S(1)} %collective-permute-done.4.refs_7_), channel_id=1, source_target_pairs={{0,1},{1,0},{2,3},{3,2},{4,5},{5,4},{6,7},{7,6},{8,9},{9,8},{10,11... | collective-permute-start | bytes 786440 | tf_op jit(solution)/shard_map/ppermute | solution.py:106
  23.3 13.2 %collective-permute-start.11 = (f32[256,256]{1,0:T(8,128)S(1)}, f32[256,256]{1,0:T(8,128)S(1)}, u32[]{:S(2)}, u32[]{:S(2)}) collective-permute-start(f32[256,256]{1,0:T(8,128)S(1)} %shard_map.38.refs_0_), channel_id=1, source_target_pairs={{8,18},{9,19},{10,16},{11,17}} | collective-permute-start | bytes 786440 | tf_op jit(solution)/shard_map/ppermute | solution.py:106
  27.4 9.1 %collective-permute-start.9 = (f32[256,256]{1,0:T(8,128)S(1)}, f32[256,256]{1,0:T(8,128)S(1)}, u32[]{:S(2)}, u32[]{:S(2)}) collective-permute-start(f32[256,256]{1,0:T(8,128)S(1)} %shard_map.38.refs_0_), channel_id=1, source_target_pairs={{8,2},{9,3},{10,0},{11,1},{24,18},{25,19},{26,16},{27,17}} | collective-permute-start | bytes 786440 | tf_op jit(solution)/shard_map/ppermute | solution.py:106
  29.6 11.7 %collective-permute-start.15 = (f32[256,256]{1,0:T(8,128)S(1)}, f32[256,256]{1,0:T(8,128)S(1)}, u32[]{:S(2)}, u32[]{:S(2)}) collective-permute-start(f32[256,256]{1,0:T(8,128)S(1)} %shard_map.38.refs_0_), channel_id=1, source_target_pairs={{8,16},{9,17},{10,18},{11,19}} | collective-permute-start | bytes 786440 | tf_op jit(solution)/shard_map/ppermute | solution.py:106
  30.9 10.4 %collective-permute-start.13 = (f32[256,256]{1,0:T(8,128)S(1)}, f32[256,256]{1,0:T(8,128)S(1)}, u32[]{:S(2)}, u32[]{:S(2)}) collective-permute-start(f32[256,256]{1,0:T(8,128)S(1)} %shard_map.38.refs_0_), channel_id=1, source_target_pairs={{8,0},{9,1},{10,2},{11,3},{24,16},{25,17},{26,18},{27,19}} | collective-permute-start | bytes 786440 | tf_op jit(solution)/shard_map/ppermute | solution.py:106
  36.5 5.3 %collective-permute-start.12 = (f32[256,256]{1,0:T(8,128)S(1)}, f32[256,256]{1,0:T(8,128)S(1)}, u32[]{:S(2)}, u32[]{:S(2)}) collective-permute-start(f32[256,256]{1,0:T(8,128)S(1)} %collective-permute-done.11.refs_5_), channel_id=1, source_target_pairs={{0,1},{1,0},{2,3},{3,2},{4,5},{5,4},{6,7},{7,6},{8,9},{9,8},{10,11... | collective-permute-start | bytes 786440 | tf_op jit(solution)/shard_map/ppermute | solution.py:106
  36.5 5.3 %collective-permute-start.10 = (f32[256,256]{1,0:T(8,128)S(1)}, f32[256,256]{1,0:T(8,128)S(1)}, u32[]{:S(2)}, u32[]{:S(2)}) collective-permute-start(f32[256,256]{1,0:T(8,128)S(1)} %collective-permute-done.9.refs_2_), channel_id=1, source_target_pairs={{0,1},{1,0},{2,3},{3,2},{4,5},{5,4},{6,7},{7,6},{8,9},{9,8},{10,11... | collective-permute-start | bytes 786440 | tf_op jit(solution)/shard_map/ppermute | solution.py:106
  41.3 1.9 %collective-permute-start.14 = (f32[256,256]{1,0:T(8,128)S(1)}, f32[256,256]{1,0:T(8,128)S(1)}, u32[]{:S(2)}, u32[]{:S(2)}) collective-permute-start(f32[256,256]{1,0:T(8,128)S(1)} %collective-permute-done.13.refs_2_), channel_id=1, source_target_pairs={{0,1},{1,0},{2,3},{3,2},{4,5},{5,4},{6,7},{7,6},{8,9},{9,8},{10,11... | collective-permute-start | bytes 786440 | tf_op jit(solution)/shard_map/ppermute | solution.py:106
  43.9 2.7 %collective-permute-start.17 = (f32[256,128]{1,0:T(8,128)S(1)}, f32[256,128]{1,0:T(8,128)S(1)}, u32[]{:S(2)}, u32[]{:S(2)}) collective-permute-start(f32[256,128]{1,0:T(8,128)S(1)} %get-tuple-element.39.refs_0_), channel_id=1, source_target_pairs={{16,2},{17,3},{18,0},{19,1}} | collective-permute-start | bytes 393224 | tf_op jit(solution)/shard_map/ppermute | solution.py:106
  44.6 2.2 %collective-permute-start.19 = (f32[256,128]{1,0:T(8,128)S(1)}, f32[256,128]{1,0:T(8,128)S(1)}, u32[]{:S(2)}, u32[]{:S(2)}) collective-permute-start(f32[256,128]{1,0:T(8,128)S(1)} %get-tuple-element.39.refs_0_), channel_id=1, source_target_pairs={{16,0},{17,1},{18,2},{19,3}} | collective-permute-start | bytes 393224 | tf_op jit(solution)/shard_map/ppermute | solution.py:106
  45.2 1.9 %collective-permute-start.24 = (f32[256,128]{1,0:T(8,128)S(1)}, f32[256,128]{1,0:T(8,128)S(1)}, u32[]{:S(2)}, u32[]{:S(2)}) collective-permute-start(f32[256,128]{1,0:T(8,128)S(1)} %get-tuple-element.40.refs_0_), channel_id=1, source_target_pairs={{16,2},{17,3},{18,0},{19,1}} | collective-permute-start | bytes 393224 | tf_op jit(solution)/shard_map/ppermute | solution.py:106
  46.8 1.6 %collective-permute-start.20 = (f32[256,128]{1,0:T(8,128)S(1)}, f32[256,128]{1,0:T(8,128)S(1)}, u32[]{:S(2)}, u32[]{:S(2)}) collective-permute-start(f32[256,128]{1,0:T(8,128)S(1)} %collective-permute-done.19.refs_2_), channel_id=1, source_target_pairs={{0,1},{1,0},{2,3},{3,2},{4,5},{5,4},{6,7},{7,6},{8,9},{9,8},{10,11... | collective-permute-start | bytes 393224 | tf_op jit(solution)/shard_map/ppermute | solution.py:106
  47.2 2.6 %collective-permute-start.25 = (f32[256,128]{1,0:T(8,128)S(1)}, f32[256,128]{1,0:T(8,128)S(1)}, u32[]{:S(2)}, u32[]{:S(2)}) collective-permute-start(f32[256,128]{1,0:T(8,128)S(1)} %collective-permute-done.24.refs_2_), channel_id=1, source_target_pairs={{0,1},{1,0},{2,3},{3,2},{4,5},{5,4},{6,7},{7,6},{8,9},{9,8},{10,11... | collective-permute-start | bytes 393224 | tf_op jit(solution)/shard_map/ppermute | solution.py:106
  47.3 2.8 %collective-permute-start.27 = (f32[256,128]{1,0:T(8,128)S(1)}, f32[256,128]{1,0:T(8,128)S(1)}, u32[]{:S(2)}, u32[]{:S(2)}) collective-permute-start(f32[256,128]{1,0:T(8,128)S(1)} %collective-permute-done.26.refs_2_), channel_id=1, source_target_pairs={{0,1},{1,0},{2,3},{3,2},{4,5},{5,4},{6,7},{7,6},{8,9},{9,8},{10,11... | collective-permute-start | bytes 393224 | tf_op jit(solution)/shard_map/ppermute | solution.py:106
  48.8 6.4 %collective-permute-start.22 = (f32[256,128]{1,0:T(8,128)S(1)}, f32[256,128]{1,0:T(8,128)S(1)}, u32[]{:S(2)}, u32[]{:S(2)}) collective-permute-start(f32[256,128]{1,0:T(8,128)S(1)} %shard_map.42.refs_1_), channel_id=1, source_target_pairs={{0,2},{1,3},{2,0},{3,1},{4,6},{5,7},{6,4},{7,5},{8,10},{9,11},{10,... | collective-permute-start | bytes 393224 | tf_op jit(solution)/shard_map/ppermute | solution.py:106
  50.5 6.7 %collective-permute-start.29 = (f32[256,128]{1,0:T(8,128)S(1)}, f32[256,128]{1,0:T(8,128)S(1)}, u32[]{:S(2)}, u32[]{:S(2)}) collective-permute-start(f32[256,128]{1,0:T(8,128)S(1)} %shard_map.46.refs_1_), channel_id=1, source_target_pairs={{0,2},{1,3},{2,0},{3,1},{4,6},{5,7},{6,4},{7,5},{8,10},{9,11},{10,... | collective-permute-start | bytes 393224 | tf_op jit(solution)/shard_map/ppermute | solution.py:106
  51.7 5.5 %collective-permute-start.21 = (f32[256,128]{1,0:T(8,128)S(1)}, f32[256,128]{1,0:T(8,128)S(1)}, u32[]{:S(2)}, u32[]{:S(2)}) collective-permute-start(f32[256,128]{1,0:T(8,128)S(1)} %shard_map.42.refs_1_), channel_id=1, source_target_pairs={{0,1},{1,0},{2,3},{3,2},{4,5},{5,4},{6,7},{7,6},{8,9},{9,8},{10,11... | collective-permute-start | bytes 393224 | tf_op jit(solution)/shard_map/ppermute | solution.py:106
  51.7 5.9 %collective-permute-start.28 = (f32[256,128]{1,0:T(8,128)S(1)}, f32[256,128]{1,0:T(8,128)S(1)}, u32[]{:S(2)}, u32[]{:S(2)}) collective-permute-start(f32[256,128]{1,0:T(8,128)S(1)} %shard_map.46.refs_1_), channel_id=1, source_target_pairs={{0,1},{1,0},{2,3},{3,2},{4,5},{5,4},{6,7},{7,6},{8,9},{9,8},{10,11... | collective-permute-start | bytes 393224 | tf_op jit(solution)/shard_map/ppermute | solution.py:106
  55.2 2.8 %collective-permute-start.23 = (f32[256,128]{1,0:T(8,128)S(1)}, f32[256,128]{1,0:T(8,128)S(1)}, u32[]{:S(2)}, u32[]{:S(2)}) collective-permute-start(f32[256,128]{1,0:T(8,128)S(1)} %collective-permute-done.22.refs_2_), channel_id=1, source_target_pairs={{0,1},{1,0},{2,3},{3,2},{4,5},{5,4},{6,7},{7,6},{8,9},{9,8},{10,11... | collective-permute-start | bytes 393224 | tf_op jit(solution)/shard_map/ppermute | solution.py:106
  57.2 1.8 %collective-permute-start.30 = (f32[256,128]{1,0:T(8,128)S(1)}, f32[256,128]{1,0:T(8,128)S(1)}, u32[]{:S(2)}, u32[]{:S(2)}) collective-permute-start(f32[256,128]{1,0:T(8,128)S(1)} %collective-permute-done.29.refs_2_), channel_id=1, source_target_pairs={{0,1},{1,0},{2,3},{3,2},{4,5},{5,4},{6,7},{7,6},{8,9},{9,8},{10,11... | collective-permute-start | bytes 393224 | tf_op jit(solution)/shard_map/ppermute | solution.py:106
  58.4 3.1 %collective-permute-start.31 = (f32[256,128]{1,0:T(8,128)S(1)}, f32[256,128]{1,0:T(8,128)S(1)}, u32[]{:S(2)}, u32[]{:S(2)}) collective-permute-start(f32[256,128]{1,0:T(8,128)S(1)} %shard_map.44.refs_0_), channel_id=1, source_target_pairs={{0,18},{1,19},{2,16},{3,17}} | collective-permute-start | bytes 393224 | tf_op jit(solution)/shard_map/ppermute | solution.py:106
  59.4 2.6 %collective-permute-start.35 = (f32[256,128]{1,0:T(8,128)S(1)}, f32[256,128]{1,0:T(8,128)S(1)}, u32[]{:S(2)}, u32[]{:S(2)}) collective-permute-start(f32[256,128]{1,0:T(8,128)S(1)} %shard_map.48.refs_0_), channel_id=1, source_target_pairs={{0,18},{1,19},{2,16},{3,17}} | collective-permute-start | bytes 393224 | tf_op jit(solution)/shard_map/ppermute | solution.py:106
  60.1 2.0 %collective-permute-start.33 = (f32[256,128]{1,0:T(8,128)S(1)}, f32[256,128]{1,0:T(8,128)S(1)}, u32[]{:S(2)}, u32[]{:S(2)}) collective-permute-start(f32[256,128]{1,0:T(8,128)S(1)} %shard_map.44.refs_0_), channel_id=1, source_target_pairs={{0,16},{1,17},{2,18},{3,19}} | collective-permute-start | bytes 393224 | tf_op jit(solution)/shard_map/ppermute | solution.py:106
  60.8 1.8 %collective-permute-start.37 = (f32[256,128]{1,0:T(8,128)S(1)}, f32[256,128]{1,0:T(8,128)S(1)}, u32[]{:S(2)}, u32[]{:S(2)}) collective-permute-start(f32[256,128]{1,0:T(8,128)S(1)} %shard_map.48.refs_0_), channel_id=1, source_target_pairs={{0,16},{1,17},{2,18},{3,19}} | collective-permute-start | bytes 393224 | tf_op jit(solution)/shard_map/ppermute | solution.py:106
  61.5 1.6 %collective-permute-start.32 = (f32[256,128]{1,0:T(8,128)S(1)}, f32[256,128]{1,0:T(8,128)S(1)}, u32[]{:S(2)}, u32[]{:S(2)}) collective-permute-start(f32[256,128]{1,0:T(8,128)S(1)} %collective-permute-done.31.refs_2_), channel_id=1, source_target_pairs={{0,1},{1,0},{2,3},{3,2},{4,5},{5,4},{6,7},{7,6},{8,9},{9,8},{10,11... | collective-permute-start | bytes 393224 | tf_op jit(solution)/shard_map/ppermute | solution.py:106
  62.1 1.7 %collective-permute-start.34 = (f32[256,128]{1,0:T(8,128)S(1)}, f32[256,128]{1,0:T(8,128)S(1)}, u32[]{:S(2)}, u32[]{:S(2)}) collective-permute-start(f32[256,128]{1,0:T(8,128)S(1)} %collective-permute-done.33.refs_2_), channel_id=1, source_target_pairs={{0,1},{1,0},{2,3},{3,2},{4,5},{5,4},{6,7},{7,6},{8,9},{9,8},{10,11... | collective-permute-start | bytes 393224 | tf_op jit(solution)/shard_map/ppermute | solution.py:106
  62.6 1.6 %collective-permute-start.38 = (f32[256,128]{1,0:T(8,128)S(1)}, f32[256,128]{1,0:T(8,128)S(1)}, u32[]{:S(2)}, u32[]{:S(2)}) collective-permute-start(f32[256,128]{1,0:T(8,128)S(1)} %collective-permute-done.37.refs_2_), channel_id=1, source_target_pairs={{0,1},{1,0},{2,3},{3,2},{4,5},{5,4},{6,7},{7,6},{8,9},{9,8},{10,11... | collective-permute-start | bytes 393224 | tf_op jit(solution)/shard_map/ppermute | solution.py:106
  64.6 36.1 %collective-permute-start.41 = (f32[256,256]{1,0:T(8,128)S(1)}, f32[256,256]{1,0:T(8,128)S(1)}, u32[]{:S(2)}, u32[]{:S(2)}) collective-permute-start(f32[256,256]{1,0:T(8,128)S(1)} %pad_maximum_fusion.1.refs_1_), channel_id=1, source_target_pairs={{0,10},{1,11},{2,8},{3,9},{16,26},{17,27},{18,24},{19,25}} | collective-permute-start | bytes 786440 | tf_op jit(solution)/shard_map/ppermute | solution.py:106
  65.9 38.3 %collective-permute-start.39 = (f32[256,256]{1,0:T(8,128)S(1)}, f32[256,256]{1,0:T(8,128)S(1)}, u32[]{:S(2)}, u32[]{:S(2)}) collective-permute-start(f32[256,256]{1,0:T(8,128)S(1)} %pad_maximum_fusion.1.refs_1_), channel_id=1, source_target_pairs={{16,10},{17,11},{18,8},{19,9}} | collective-permute-start | bytes 786440 | tf_op jit(solution)/shard_map/ppermute | solution.py:106
  67.2 37.2 %collective-permute-start.45 = (f32[256,256]{1,0:T(8,128)S(1)}, f32[256,256]{1,0:T(8,128)S(1)}, u32[]{:S(2)}, u32[]{:S(2)}) collective-permute-start(f32[256,256]{1,0:T(8,128)S(1)} %pad_maximum_fusion.1.refs_1_), channel_id=1, source_target_pairs={{0,8},{1,9},{2,10},{3,11},{16,24},{17,25},{18,26},{19,27}} | collective-permute-start | bytes 786440 | tf_op jit(solution)/shard_map/ppermute | solution.py:106
  68.5 40.5 %collective-permute-start.43 = (f32[256,256]{1,0:T(8,128)S(1)}, f32[256,256]{1,0:T(8,128)S(1)}, u32[]{:S(2)}, u32[]{:S(2)}) collective-permute-start(f32[256,256]{1,0:T(8,128)S(1)} %pad_maximum_fusion.1.refs_1_), channel_id=1, source_target_pairs={{16,8},{17,9},{18,10},{19,11}} | collective-permute-start | bytes 786440 | tf_op jit(solution)/shard_map/ppermute | solution.py:106
  100.7 8.3 %collective-permute-start.42 = (f32[256,256]{1,0:T(8,128)S(1)}, f32[256,256]{1,0:T(8,128)S(1)}, u32[]{:S(2)}, u32[]{:S(2)}) collective-permute-start(f32[256,256]{1,0:T(8,128)S(1)} %collective-permute-done.41.refs_6_), channel_id=1, source_target_pairs={{0,1},{1,0},{2,3},{3,2},{4,5},{5,4},{6,7},{7,6},{8,9},{9,8},{10,11... | collective-permute-start | bytes 786440 | tf_op jit(solution)/shard_map/ppermute | solution.py:106
  104.2 4.8 %collective-permute-start.40 = (f32[256,256]{1,0:T(8,128)S(1)}, f32[256,256]{1,0:T(8,128)S(1)}, u32[]{:S(2)}, u32[]{:S(2)}) collective-permute-start(f32[256,256]{1,0:T(8,128)S(1)} %collective-permute-done.39.refs_3_), channel_id=1, source_target_pairs={{0,1},{1,0},{2,3},{3,2},{4,5},{5,4},{6,7},{7,6},{8,9},{9,8},{10,11... | collective-permute-start | bytes 786440 | tf_op jit(solution)/shard_map/ppermute | solution.py:106
  104.4 5.3 %collective-permute-start.46 = (f32[256,256]{1,0:T(8,128)S(1)}, f32[256,256]{1,0:T(8,128)S(1)}, u32[]{:S(2)}, u32[]{:S(2)}) collective-permute-start(f32[256,256]{1,0:T(8,128)S(1)} %collective-permute-done.45.refs_5_), channel_id=1, source_target_pairs={{0,1},{1,0},{2,3},{3,2},{4,5},{5,4},{6,7},{7,6},{8,9},{9,8},{10,11... | collective-permute-start | bytes 786440 | tf_op jit(solution)/shard_map/ppermute | solution.py:106
  111.1 9.3 %collective-permute-start.49 = (f32[256,256]{1,0:T(8,128)S(1)}, f32[256,256]{1,0:T(8,128)S(1)}, u32[]{:S(2)}, u32[]{:S(2)}) collective-permute-start(f32[256,256]{1,0:T(8,128)S(1)} %shard_map.54.refs_1_), channel_id=1, source_target_pairs={{0,26},{1,27},{2,24},{3,25},{4,30},{5,31},{6,28},{7,29},{8,2},{9,3... | collective-permute-start | bytes 786440 | tf_op jit(solution)/shard_map/ppermute | solution.py:106
  111.2 10.5 %collective-permute-start.47 = (f32[256,256]{1,0:T(8,128)S(1)}, f32[256,256]{1,0:T(8,128)S(1)}, u32[]{:S(2)}, u32[]{:S(2)}) collective-permute-start(f32[256,256]{1,0:T(8,128)S(1)} %shard_map.54.refs_1_), channel_id=1, source_target_pairs={{0,4},{1,5},{2,6},{3,7},{8,12},{9,13},{10,14},{11,15},{16,20},{17,... | collective-permute-start | bytes 786440 | tf_op jit(solution)/shard_map/ppermute | solution.py:106
  120.4 6.6 %collective-permute-start.50 = (f32[256,256]{1,0:T(8,128)S(1)}, f32[256,256]{1,0:T(8,128)S(1)}, u32[]{:S(2)}, u32[]{:S(2)}) collective-permute-start(f32[256,256]{1,0:T(8,128)S(1)} %collective-permute-done.49), channel_id=1, source_target_pairs={{0,4},{1,5},{2,6},{3,7},{8,12},{9,13},{10,14},{11,15},{16,20},{17,... | collective-permute-start | bytes 786440 | tf_op jit(solution)/shard_map/ppermute | solution.py:106
  121.7 7.6 %collective-permute-start.54 = (f32[256,256]{1,0:T(8,128)S(1)}, f32[256,256]{1,0:T(8,128)S(1)}, u32[]{:S(2)}, u32[]{:S(2)}) collective-permute-start(f32[256,256]{1,0:T(8,128)S(1)} %collective-permute-done.47.refs_3_), channel_id=1, source_target_pairs={{0,24},{1,25},{2,26},{3,27},{4,28},{5,29},{6,30},{7,31},{8,0},{9,1... | collective-permute-start | bytes 786440 | tf_op jit(solution)/shard_map/ppermute | solution.py:106
  121.8 7.6 %collective-permute-start.52 = (f32[256,256]{1,0:T(8,128)S(1)}, f32[256,256]{1,0:T(8,128)S(1)}, u32[]{:S(2)}, u32[]{:S(2)}) collective-permute-start(f32[256,256]{1,0:T(8,128)S(1)} %collective-permute-done.47.refs_3_), channel_id=1, source_target_pairs={{0,2},{1,3},{2,0},{3,1},{4,6},{5,7},{6,4},{7,5},{8,10},{9,11},{10,... | collective-permute-start | bytes 786440 | tf_op jit(solution)/shard_map/ppermute | solution.py:106
  123.0 6.9 %collective-permute-start.48 = (f32[256,256]{1,0:T(8,128)S(1)}, f32[256,256]{1,0:T(8,128)S(1)}, u32[]{:S(2)}, u32[]{:S(2)}) collective-permute-start(f32[256,256]{1,0:T(8,128)S(1)} %collective-permute-done.47.refs_3_), channel_id=1, source_target_pairs={{0,1},{1,0},{2,3},{3,2},{4,5},{5,4},{6,7},{7,6},{8,9},{9,8},{10,11... | collective-permute-start | bytes 786440 | tf_op jit(solution)/shard_map/ppermute | solution.py:106
  127.0 2.8 %collective-permute-start.51 = (f32[256,256]{1,0:T(8,128)S(1)}, f32[256,256]{1,0:T(8,128)S(1)}, u32[]{:S(2)}, u32[]{:S(2)}) collective-permute-start(f32[256,256]{1,0:T(8,128)S(1)} %collective-permute-done.50.refs_6_), channel_id=1, source_target_pairs={{0,1},{1,0},{2,3},{3,2},{4,5},{5,4},{6,7},{7,6},{8,9},{9,8},{10,11... | collective-permute-start | bytes 786440 | tf_op jit(solution)/shard_map/ppermute | solution.py:106
  129.4 1.8 %collective-permute-start.53 = (f32[256,256]{1,0:T(8,128)S(1)}, f32[256,256]{1,0:T(8,128)S(1)}, u32[]{:S(2)}, u32[]{:S(2)}) collective-permute-start(f32[256,256]{1,0:T(8,128)S(1)} %collective-permute-done.52.refs_2_), channel_id=1, source_target_pairs={{0,1},{1,0},{2,3},{3,2},{4,5},{5,4},{6,7},{7,6},{8,9},{9,8},{10,11... | collective-permute-start | bytes 786440 | tf_op jit(solution)/shard_map/ppermute | solution.py:106
  (11 other events, 30.3 us)

commit v6 on v5

--- a/solution.py
+++ b/solution.py
@@ -114,12 +114,23 @@
     def direct(block, pairs):
         return [(flip, move(block, pairs, flip)) for flip in range(0, rows, 2)]
 
+    def traded(block, pairs):
+        partner = {a: b for a, b in pairs} | {b: a for a, b in pairs}
+        out = []
+        for flip in range(0, rows, 2):
+            hops = [
+                (a * rows + r, partner.get(a, a) * rows + (r ^ (flip if a in partner else 1)))
+                for a in range(layers) for r in range(rows)
+            ]
+            out.append((flip, lax.ppermute(block, AXES, hops)))
+        return out
+
     def within(block, among=None):
         return [(0, block)] + [(flip, move(block, among or every, flip)) for flip in range(2, rows, 2)]
 
     def apply(starts, sign, *mats_pieces, only=None, far_first=False):
-        early = [(m, f, p) for m, ps in mats_pieces for f, p in ps[:2]]
-        late = [(m, f, p) for m, ps in mats_pieces for f, p in ps[2:]]
+        early = [(m, f, p, *span) for m, ps, *span in mats_pieces for f, p in ps[:2]]
+        late = [(m, f, p, *span) for m, ps, *span in mats_pieces for f, p in ps[2:]]
         if far_first and late:
             early, late = late, early
         start = combine(starts, early, sign, only)
@@ -155,9 +166,11 @@
         stride = 1 << k
         senders = range(stride, layers, 2 * stride)
         left, right = reduce_mats[k]
-        lower = swapped(direct(current, [(i, i + stride) for i in senders]))
-        upper = swapped(direct(current, [(i, i - stride) for i in senders]))
-        current = apply([current], -1, (right, upper), (left, lower), far_first=True)
+        lower = swapped(traded(current, [(i, i + stride) for i in senders if i + stride < layers]))
+        upper = swapped(traded(current, [(i, i - stride) for i in senders]))
+        current = apply(
+            [current], -1, (right, upper), (left, lower, (1, layers)), only=(2 * stride, 0), far_first=True
+        )
 
     half = layers // 2
     width = current.shape[1] // 2

time: 135 us -> 133 us (0.985)
  starting transfers between devices: 38.7 us -> 33.4 us
  waiting for transfers between devices: 76.9 us -> 80.8 us
    ppermute x0 -> x4, waiting for transfers between devices: none -> 15.2 us  [traded(): out.append((flip, lax.ppermute(block, AXES, hops)))]
    ppermute x56 -> x52, waiting for transfers between devices: 76.9 us -> 65.6 us  [move(): return lax.ppermute(block, AXES, hops) if hops else None]
    ppermute x56 -> x52, starting transfers between devices: 38.7 us -> 28.8 us  [move(): return lax.ppermute(block, AXES, hops) if hops else None]
    ppermute x0 -> x4, starting transfers between devices: none -> 4.57 us  [traded(): out.append((flip, lax.ppermute(block, AXES, hops)))]
  transfers between devices with their start and end apart: 56 -> 56, of which waited for: 25 -> 26; matrix products, arithmetic and copies ran while one was open for 0% -> 0% of each run, Pallas kernels for 6% -> 6%
where the time goes in v6:
time: 133 us; the launch traced here: 131 us
  waiting for transfers between devices  80.8 us (61%)
  starting transfers between devices  33.4 us (25%)
  Pallas kernels  11.7 us (9%)
  local copies, waits for them, and re-layouts  4.7 us (4%)
    ppermute x52, waiting for transfers between devices, move(): return lax.ppermute(block, AXES, hops) if hops else None  65.6 us
    ppermute x52, starting transfers between devices, move(): return lax.ppermute(block, AXES, hops) if hops else None  28.8 us
    ppermute x4, waiting for transfers between devices, traded(): out.append((flip, lax.ppermute(block, AXES, hops)))  15.2 us
    pallas_call x19, Pallas kernels, combine(): pl.pallas_call(functools.partial(combine_kernel, shape, sign, only), out_...  9.97 us
    unnamed x6, local copies, waits for them, and re-layouts  4.68 us
    ppermute x4, starting transfers between devices, traded(): out.append((flip, lax.ppermute(block, AXES, hops)))  4.57 us
  transfers between devices with their start and end apart: 56, of which 26 were waited for; matrix products, arithmetic and copies ran while one was open for 0% of the time, Pallas kernels for 6%

profile of v6, /device:TPU:8, one launch (start us, length us, event | category | flops | bytes accessed | tf_op | source)
XLA Modules:
  0.0 131.1 jit_solution(16368115462912831531)
XLA Ops:
  0.0 1.3 collective-permute-start
  1.3 2.6 %collective-permute-start.6 = (f32[256,256]{1,0:T(8,128)}, f32[256,256]{1,0:T(8,128)S(1)}, u32[]{:S(2)}, u32[]{:S(2)}) collective-permute-start(f32[256,256]{1,0:T(8,128)} %bitcast.7), channel_id=1, source_target_pairs={{0,10},{1,11},{2,8},{3,9},{4,14},{5,15},{6,12},{7,13},{8,18},{9,19... | collective-permute-start | bytes 786440 | tf_op jit(solution)/shard_map/ppermute | solution.py:106
  3.9 2.8 %copy-done = f32[3,1,2,256,1024]{4,3,2,1,0:T(8,128)S(1)} copy-done((f32[3,1,2,256,1024]{4,3,2,1,0:T(8,128)S(1)}, f32[3,1,2,256,1024]{4,3,2,1,0:T(8,128)}, u32[]{:S(2)}) %copy-start) | copy-done | bytes 6291480
  6.7 1.9 %copy-done.1 = f32[1,3,256,1024]{3,2,1,0:T(8,128)S(1)} copy-done((f32[1,3,256,1024]{3,2,1,0:T(8,128)S(1)}, f32[1,3,256,1024]{3,2,1,0:T(8,128)}, u32[]{:S(2)}) %copy-start.1) | copy-done | bytes 3145752
  8.6 1.7 %shard_map.37 = (f32[256,1024]{1,0:T(8,128)S(1)}, f32[256,1024]{1,0:T(8,128)S(1)}, f32[256,1024]{1,0:T(8,128)S(1)}, f32[256,1024]{1,0:T(8,128)S(1)}, f32[256,102...) custom-call(f32[3,2,256,1024]{3,2,1,0:T(8,128)S(1)} %bitcast.4, ...), custom_call_target="tpu_custom_call" | custom-call | tf_op jit(solution)/shard_map/pallas_call | solution.py:87
  10.5 1.3 collective-permute-start.7
  11.8 1.6 %collective-permute-start.4 = (f32[256,256]{1,0:T(8,128)S(1)}, f32[256,256]{1,0:T(8,128)S(1)}, u32[]{:S(2)}, u32[]{:S(2)}) collective-permute-start(f32[256,256]{1,0:T(8,128)S(1)} %collective-permute-done.refs_2_), channel_id=1, source_target_pairs={{0,8},{1,9},{2,10},{3,11},{4,12},{5,13},{6,14},{7,15},{8,16},{9,17... | collective-permute-start | bytes 786440 | tf_op jit(solution)/shard_map/ppermute | solution.py:106
  13.4 1.5 %collective-permute-start.2 = (f32[256,256]{1,0:T(8,128)S(1)}, f32[256,256]{1,0:T(8,128)S(1)}, u32[]{:S(2)}, u32[]{:S(2)}) collective-permute-start(f32[256,256]{1,0:T(8,128)S(1)} %collective-permute-done.refs_2_), channel_id=1, source_target_pairs={{0,2},{1,3},{2,0},{3,1},{4,6},{5,7},{6,4},{7,5},{8,10},{9,11},{10,... | collective-permute-start | bytes 786440 | tf_op jit(solution)/shard_map/ppermute | solution.py:106
  14.9 5.1 %collective-permute-done.7.refs_9_ = f32[256,256]{1,0:T(8,128)S(1)} collective-permute-done((f32[256,256]{1,0:T(8,128)S(1)}, f32[256,256]{1,0:T(8,128)S(1)}, u32[]{:S(2)}, u32[]{:S(2)}) %collective-permute-start.7) | collective-permute-done | bytes 262176 | tf_op jit(solution)/shard_map/ppermute | solution.py:106
  20.7 0.8 collective-permute-done.8.refs_10_
  22.3 1.1 shard_map.38.refs_0_
  23.3 2.2 %collective-permute-start.11 = (f32[256,256]{1,0:T(8,128)S(1)}, f32[256,256]{1,0:T(8,128)S(1)}, u32[]{:S(2)}, u32[]{:S(2)}) collective-permute-start(f32[256,256]{1,0:T(8,128)S(1)} %shard_map.38.refs_0_), channel_id=1, source_target_pairs={{0,1},{1,0},{2,3},{3,2},{4,5},{5,4},{6,7},{7,6},{8,18},{9,19},{10,... | collective-permute-start | bytes 786440 | tf_op jit(solution)/shard_map/ppermute | solution.py:125
  25.5 1.7 %collective-permute-start.9 = (f32[256,256]{1,0:T(8,128)S(1)}, f32[256,256]{1,0:T(8,128)S(1)}, u32[]{:S(2)}, u32[]{:S(2)}) collective-permute-start(f32[256,256]{1,0:T(8,128)S(1)} %shard_map.38.refs_0_), channel_id=1, source_target_pairs={{0,10},{1,11},{2,8},{3,9},{4,5},{5,4},{6,7},{7,6},{8,2},{9,3},{10,... | collective-permute-start | bytes 786440 | tf_op jit(solution)/shard_map/ppermute | solution.py:125
  27.9 8.5 %collective-permute-done.11.refs_5_ = f32[256,256]{1,0:T(8,128)S(1)} collective-permute-done((f32[256,256]{1,0:T(8,128)S(1)}, f32[256,256]{1,0:T(8,128)S(1)}, u32[]{:S(2)}, u32[]{:S(2)}) %collective-permute-start.11) | collective-permute-done | bytes 262176 | tf_op jit(solution)/shard_map/ppermute | solution.py:125
  36.5 2.6 %collective-permute-done.9.refs_2_ = f32[256,256]{1,0:T(8,128)S(1)} collective-permute-done((f32[256,256]{1,0:T(8,128)S(1)}, f32[256,256]{1,0:T(8,128)S(1)}, u32[]{:S(2)}, u32[]{:S(2)}) %collective-permute-start.9) | collective-permute-done | bytes 262176 | tf_op jit(solution)/shard_map/ppermute | solution.py:125
  39.1 1.2 collective-permute-done.15.refs_5_
  40.2 2.9 %collective-permute-done.13.refs_2_ = f32[256,256]{1,0:T(8,128)S(1)} collective-permute-done((f32[256,256]{1,0:T(8,128)S(1)}, f32[256,256]{1,0:T(8,128)S(1)}, u32[]{:S(2)}, u32[]{:S(2)}) %collective-permute-start.13) | collective-permute-done | bytes 262176 | tf_op jit(solution)/shard_map/ppermute | solution.py:125
  43.8 0.9 collective-permute-done.14.refs_3_
  45.3 0.7 collective-permute-start.17
  46.0 0.7 collective-permute-start.19
  46.6 0.7 collective-permute-start.24
  47.3 0.7 collective-permute-start.26
  50.2 1.2 collective-permute-start.22
  52.1 1.0 collective-permute-start.29
  53.6 3.0 %collective-permute-done.22.refs_2_ = f32[256,128]{1,0:T(8,128)S(1)} collective-permute-done((f32[256,128]{1,0:T(8,128)S(1)}, f32[256,128]{1,0:T(8,128)S(1)}, u32[]{:S(2)}, u32[]{:S(2)}) %collective-permute-start.22) | collective-permute-done | bytes 131104 | tf_op jit(solution)/shard_map/ppermute | solution.py:106
  56.6 2.0 %collective-permute-done.29.refs_2_ = f32[256,128]{1,0:T(8,128)S(1)} collective-permute-done((f32[256,128]{1,0:T(8,128)S(1)}, f32[256,128]{1,0:T(8,128)S(1)}, u32[]{:S(2)}, u32[]{:S(2)}) %collective-permute-start.29) | collective-permute-done | bytes 131104 | tf_op jit(solution)/shard_map/ppermute | solution.py:106
  59.7 0.7 collective-permute-start.31
  60.8 0.7 collective-permute-start.35
  61.5 0.7 collective-permute-start.33
  62.2 0.7 collective-permute-start.37
  66.0 1.3 collective-permute-start.41
  67.3 1.3 collective-permute-start.39
  68.6 1.3 collective-permute-start.45
  69.9 1.3 collective-permute-start.43
  71.2 28.0 %collective-permute-done.41.refs_6_ = f32[256,256]{1,0:T(8,128)S(1)} collective-permute-done((f32[256,256]{1,0:T(8,128)S(1)}, f32[256,256]{1,0:T(8,128)S(1)}, u32[]{:S(2)}, u32[]{:S(2)}) %collective-permute-start.41) | collective-permute-done | bytes 262176 | tf_op jit(solution)/shard_map/ppermute | solution.py:106
  99.2 3.5 %collective-permute-done.39.refs_3_ = f32[256,256]{1,0:T(8,128)S(1)} collective-permute-done((f32[256,256]{1,0:T(8,128)S(1)}, f32[256,256]{1,0:T(8,128)S(1)}, u32[]{:S(2)}, u32[]{:S(2)}) %collective-permute-start.39) | collective-permute-done | bytes 262176 | tf_op jit(solution)/shard_map/ppermute | solution.py:106
  103.3 4.2 %collective-permute-done.43.refs_2_ = f32[256,256]{1,0:T(8,128)S(1)} collective-permute-done((f32[256,256]{1,0:T(8,128)S(1)}, f32[256,256]{1,0:T(8,128)S(1)}, u32[]{:S(2)}, u32[]{:S(2)}) %collective-permute-start.43) | collective-permute-done | bytes 262176 | tf_op jit(solution)/shard_map/ppermute | solution.py:106
  107.6 0.7 shard_map.53.refs_0_
  108.2 0.8 collective-permute-done.44.refs_3_
  109.0 0.6 shard_map.54.refs_1_
  109.8 1.3 collective-permute-start.47
  111.1 7.9 %collective-permute-done.49 = f32[256,256]{1,0:T(8,128)S(1)} collective-permute-done((f32[256,256]{1,0:T(8,128)S(1)}, f32[256,256]{1,0:T(8,128)S(1)}, u32[]{:S(2)}, u32[]{:S(2)}) %collective-permute-start.49) | collective-permute-done | bytes 262176 | tf_op jit(solution)/shard_map/ppermute | solution.py:106
  119.0 1.3 collective-permute-start.50
  120.4 1.2 collective-permute-start.52
  121.5 4.0 %collective-permute-done.50.refs_6_ = f32[256,256]{1,0:T(8,128)S(1)} collective-permute-done((f32[256,256]{1,0:T(8,128)S(1)}, f32[256,256]{1,0:T(8,128)S(1)}, u32[]{:S(2)}, u32[]{:S(2)}) %collective-permute-start.50) | collective-permute-done | bytes 262176 | tf_op jit(solution)/shard_map/ppermute | solution.py:106
  125.6 2.3 %collective-permute-done.54.refs_5_ = f32[256,256]{1,0:T(8,128)S(1)} collective-permute-done((f32[256,256]{1,0:T(8,128)S(1)}, f32[256,256]{1,0:T(8,128)S(1)}, u32[]{:S(2)}, u32[]{:S(2)}) %collective-permute-start.54) | collective-permute-done | bytes 262176 | tf_op jit(solution)/shard_map/ppermute | solution.py:106
  128.4 0.6 shard_map.55.refs_0_
  129.8 1.3 %shard_map.56 = f32[256,256]{1,0:T(8,128)} custom-call(f32[256,256]{1,0:T(8,128)S(1)} %shard_map.55.refs_0_, f32[256,1024]{1,0:T(8,128)S(1)} %get-tuple-element.37.refs_1_.refs_5_.refs_4_.refs_2_, f32[256,256]{1,0:T(8,128)S(1)} %collective-permute-done.52.refs_2_, f32[256,256]{1,0:T(8,128)S(1)} %collective-permute-done.53.refs_3_, ...), custom_call_target="tpu_custom_call" | custom-call | flops 402653184 | tf_op jit(solution)/shard_map/pallas_call | solution.py:62
  (93 shorter events, 13.6 us)
Async XLA Ops:
  0.0 10.3 %collective-permute-start = (f32[256,256]{1,0:T(8,128)}, f32[256,256]{1,0:T(8,128)S(1)}, u32[]{:S(2)}, u32[]{:S(2)}) collective-permute-start(f32[256,256]{1,0:T(8,128)} %bitcast.6), channel_id=1, source_target_pairs={{4,0},{5,1},{6,2},{7,3},{12,8},{13,9},{14,10},{15,11},{20,16},{21,... | collective-permute-start | bytes 786440 | tf_op jit(solution)/shard_map/ppermute | solution.py:106
  1.3 9.2 %collective-permute-start.6 = (f32[256,256]{1,0:T(8,128)}, f32[256,256]{1,0:T(8,128)S(1)}, u32[]{:S(2)}, u32[]{:S(2)}) collective-permute-start(f32[256,256]{1,0:T(8,128)} %bitcast.7), channel_id=1, source_target_pairs={{0,10},{1,11},{2,8},{3,9},{4,14},{5,15},{6,12},{7,13},{8,18},{9,19... | collective-permute-start | bytes 786440 | tf_op jit(solution)/shard_map/ppermute | solution.py:106
  10.5 9.5 %collective-permute-start.7 = (f32[256,256]{1,0:T(8,128)S(1)}, f32[256,256]{1,0:T(8,128)S(1)}, u32[]{:S(2)}, u32[]{:S(2)}) collective-permute-start(f32[256,256]{1,0:T(8,128)S(1)} %collective-permute-done.6), channel_id=1, source_target_pairs={{4,0},{5,1},{6,2},{7,3},{12,8},{13,9},{14,10},{15,11},{20,16},{21,... | collective-permute-start | bytes 786440 | tf_op jit(solution)/shard_map/ppermute | solution.py:106
  11.8 8.2 %collective-permute-start.4 = (f32[256,256]{1,0:T(8,128)S(1)}, f32[256,256]{1,0:T(8,128)S(1)}, u32[]{:S(2)}, u32[]{:S(2)}) collective-permute-start(f32[256,256]{1,0:T(8,128)S(1)} %collective-permute-done.refs_2_), channel_id=1, source_target_pairs={{0,8},{1,9},{2,10},{3,11},{4,12},{5,13},{6,14},{7,15},{8,16},{9,17... | collective-permute-start | bytes 786440 | tf_op jit(solution)/shard_map/ppermute | solution.py:106
  13.4 7.3 %collective-permute-start.2 = (f32[256,256]{1,0:T(8,128)S(1)}, f32[256,256]{1,0:T(8,128)S(1)}, u32[]{:S(2)}, u32[]{:S(2)}) collective-permute-start(f32[256,256]{1,0:T(8,128)S(1)} %collective-permute-done.refs_2_), channel_id=1, source_target_pairs={{0,2},{1,3},{2,0},{3,1},{4,6},{5,7},{6,4},{7,5},{8,10},{9,11},{10,... | collective-permute-start | bytes 786440 | tf_op jit(solution)/shard_map/ppermute | solution.py:106
  14.9 5.8 %collective-permute-start.1 = (f32[256,256]{1,0:T(8,128)S(1)}, f32[256,256]{1,0:T(8,128)S(1)}, u32[]{:S(2)}, u32[]{:S(2)}) collective-permute-start(f32[256,256]{1,0:T(8,128)S(1)} %collective-permute-done.refs_2_), channel_id=1, source_target_pairs={{0,1},{1,0},{2,3},{3,2},{4,5},{5,4},{6,7},{7,6},{8,9},{9,8},{10,11... | collective-permute-start | bytes 786440 | tf_op jit(solution)/shard_map/ppermute | solution.py:106
  20.0 1.9 %collective-permute-start.5 = (f32[256,256]{1,0:T(8,128)S(1)}, f32[256,256]{1,0:T(8,128)S(1)}, u32[]{:S(2)}, u32[]{:S(2)}) collective-permute-start(f32[256,256]{1,0:T(8,128)S(1)} %collective-permute-done.4.refs_7_), channel_id=1, source_target_pairs={{0,1},{1,0},{2,3},{3,2},{4,5},{5,4},{6,7},{7,6},{8,9},{9,8},{10,11... | collective-permute-start | bytes 786440 | tf_op jit(solution)/shard_map/ppermute | solution.py:106
  23.3 13.1 %collective-permute-start.11 = (f32[256,256]{1,0:T(8,128)S(1)}, f32[256,256]{1,0:T(8,128)S(1)}, u32[]{:S(2)}, u32[]{:S(2)}) collective-permute-start(f32[256,256]{1,0:T(8,128)S(1)} %shard_map.38.refs_0_), channel_id=1, source_target_pairs={{0,1},{1,0},{2,3},{3,2},{4,5},{5,4},{6,7},{7,6},{8,18},{9,19},{10,... | collective-permute-start | bytes 786440 | tf_op jit(solution)/shard_map/ppermute | solution.py:125
  25.5 13.6 %collective-permute-start.9 = (f32[256,256]{1,0:T(8,128)S(1)}, f32[256,256]{1,0:T(8,128)S(1)}, u32[]{:S(2)}, u32[]{:S(2)}) collective-permute-start(f32[256,256]{1,0:T(8,128)S(1)} %shard_map.38.refs_0_), channel_id=1, source_target_pairs={{0,10},{1,11},{2,8},{3,9},{4,5},{5,4},{6,7},{7,6},{8,2},{9,3},{10,... | collective-permute-start | bytes 786440 | tf_op jit(solution)/shard_map/ppermute | solution.py:125
  27.2 13.0 %collective-permute-start.15 = (f32[256,256]{1,0:T(8,128)S(1)}, f32[256,256]{1,0:T(8,128)S(1)}, u32[]{:S(2)}, u32[]{:S(2)}) collective-permute-start(f32[256,256]{1,0:T(8,128)S(1)} %shard_map.38.refs_0_), channel_id=1, source_target_pairs={{0,1},{1,0},{2,3},{3,2},{4,5},{5,4},{6,7},{7,6},{8,16},{9,17},{10,... | collective-permute-start | bytes 786440 | tf_op jit(solution)/shard_map/ppermute | solution.py:125
  27.7 15.4 %collective-permute-start.13 = (f32[256,256]{1,0:T(8,128)S(1)}, f32[256,256]{1,0:T(8,128)S(1)}, u32[]{:S(2)}, u32[]{:S(2)}) collective-permute-start(f32[256,256]{1,0:T(8,128)S(1)} %shard_map.38.refs_0_), channel_id=1, source_target_pairs={{0,8},{1,9},{2,10},{3,11},{4,5},{5,4},{6,7},{7,6},{8,0},{9,1},{10,... | collective-permute-start | bytes 786440 | tf_op jit(solution)/shard_map/ppermute | solution.py:125
  36.5 6.7 %collective-permute-start.12 = (f32[256,256]{1,0:T(8,128)S(1)}, f32[256,256]{1,0:T(8,128)S(1)}, u32[]{:S(2)}, u32[]{:S(2)}) collective-permute-start(f32[256,256]{1,0:T(8,128)S(1)} %collective-permute-done.11.refs_5_), channel_id=1, source_target_pairs={{0,1},{1,0},{2,3},{3,2},{4,5},{5,4},{6,7},{7,6},{8,9},{9,8},{10,11... | collective-permute-start | bytes 786440 | tf_op jit(solution)/shard_map/ppermute | solution.py:106
  39.1 4.0 %collective-permute-start.10 = (f32[256,256]{1,0:T(8,128)S(1)}, f32[256,256]{1,0:T(8,128)S(1)}, u32[]{:S(2)}, u32[]{:S(2)}) collective-permute-start(f32[256,256]{1,0:T(8,128)S(1)} %collective-permute-done.9.refs_2_), channel_id=1, source_target_pairs={{0,1},{1,0},{2,3},{3,2},{4,5},{5,4},{6,7},{7,6},{8,9},{9,8},{10,11... | collective-permute-start | bytes 786440 | tf_op jit(solution)/shard_map/ppermute | solution.py:106
  40.2 3.5 %collective-permute-start.16 = (f32[256,256]{1,0:T(8,128)S(1)}, f32[256,256]{1,0:T(8,128)S(1)}, u32[]{:S(2)}, u32[]{:S(2)}) collective-permute-start(f32[256,256]{1,0:T(8,128)S(1)} %collective-permute-done.15.refs_5_), channel_id=1, source_target_pairs={{0,1},{1,0},{2,3},{3,2},{4,5},{5,4},{6,7},{7,6},{8,9},{9,8},{10,11... | collective-permute-start | bytes 786440 | tf_op jit(solution)/shard_map/ppermute | solution.py:106
  45.3 2.7 %collective-permute-start.17 = (f32[256,128]{1,0:T(8,128)S(1)}, f32[256,128]{1,0:T(8,128)S(1)}, u32[]{:S(2)}, u32[]{:S(2)}) collective-permute-start(f32[256,128]{1,0:T(8,128)S(1)} %get-tuple-element.39.refs_0_), channel_id=1, source_target_pairs={{16,2},{17,3},{18,0},{19,1}} | collective-permute-start | bytes 393224 | tf_op jit(solution)/shard_map/ppermute | solution.py:106
  46.0 2.2 %collective-permute-start.19 = (f32[256,128]{1,0:T(8,128)S(1)}, f32[256,128]{1,0:T(8,128)S(1)}, u32[]{:S(2)}, u32[]{:S(2)}) collective-permute-start(f32[256,128]{1,0:T(8,128)S(1)} %get-tuple-element.39.refs_0_), channel_id=1, source_target_pairs={{16,0},{17,1},{18,2},{19,3}} | collective-permute-start | bytes 393224 | tf_op jit(solution)/shard_map/ppermute | solution.py:106
  46.6 1.9 %collective-permute-start.24 = (f32[256,128]{1,0:T(8,128)S(1)}, f32[256,128]{1,0:T(8,128)S(1)}, u32[]{:S(2)}, u32[]{:S(2)}) collective-permute-start(f32[256,128]{1,0:T(8,128)S(1)} %get-tuple-element.40.refs_0_), channel_id=1, source_target_pairs={{16,2},{17,3},{18,0},{19,1}} | collective-permute-start | bytes 393224 | tf_op jit(solution)/shard_map/ppermute | solution.py:106
  48.2 1.6 %collective-permute-start.20 = (f32[256,128]{1,0:T(8,128)S(1)}, f32[256,128]{1,0:T(8,128)S(1)}, u32[]{:S(2)}, u32[]{:S(2)}) collective-permute-start(f32[256,128]{1,0:T(8,128)S(1)} %collective-permute-done.19.refs_2_), channel_id=1, source_target_pairs={{0,1},{1,0},{2,3},{3,2},{4,5},{5,4},{6,7},{7,6},{8,9},{9,8},{10,11... | collective-permute-start | bytes 393224 | tf_op jit(solution)/shard_map/ppermute | solution.py:106
  48.6 2.7 %collective-permute-start.25 = (f32[256,128]{1,0:T(8,128)S(1)}, f32[256,128]{1,0:T(8,128)S(1)}, u32[]{:S(2)}, u32[]{:S(2)}) collective-permute-start(f32[256,128]{1,0:T(8,128)S(1)} %collective-permute-done.24.refs_2_), channel_id=1, source_target_pairs={{0,1},{1,0},{2,3},{3,2},{4,5},{5,4},{6,7},{7,6},{8,9},{9,8},{10,11... | collective-permute-start | bytes 393224 | tf_op jit(solution)/shard_map/ppermute | solution.py:106
  48.7 3.0 %collective-permute-start.27 = (f32[256,128]{1,0:T(8,128)S(1)}, f32[256,128]{1,0:T(8,128)S(1)}, u32[]{:S(2)}, u32[]{:S(2)}) collective-permute-start(f32[256,128]{1,0:T(8,128)S(1)} %collective-permute-done.26.refs_2_), channel_id=1, source_target_pairs={{0,1},{1,0},{2,3},{3,2},{4,5},{5,4},{6,7},{7,6},{8,9},{9,8},{10,11... | collective-permute-start | bytes 393224 | tf_op jit(solution)/shard_map/ppermute | solution.py:106
  50.2 6.4 %collective-permute-start.22 = (f32[256,128]{1,0:T(8,128)S(1)}, f32[256,128]{1,0:T(8,128)S(1)}, u32[]{:S(2)}, u32[]{:S(2)}) collective-permute-start(f32[256,128]{1,0:T(8,128)S(1)} %shard_map.42.refs_1_), channel_id=1, source_target_pairs={{0,2},{1,3},{2,0},{3,1},{4,6},{5,7},{6,4},{7,5},{8,10},{9,11},{10,... | collective-permute-start | bytes 393224 | tf_op jit(solution)/shard_map/ppermute | solution.py:106
  52.1 6.5 %collective-permute-start.29 = (f32[256,128]{1,0:T(8,128)S(1)}, f32[256,128]{1,0:T(8,128)S(1)}, u32[]{:S(2)}, u32[]{:S(2)}) collective-permute-start(f32[256,128]{1,0:T(8,128)S(1)} %shard_map.46.refs_1_), channel_id=1, source_target_pairs={{0,2},{1,3},{2,0},{3,1},{4,6},{5,7},{6,4},{7,5},{8,10},{9,11},{10,... | collective-permute-start | bytes 393224 | tf_op jit(solution)/shard_map/ppermute | solution.py:106
  53.1 5.5 %collective-permute-start.21 = (f32[256,128]{1,0:T(8,128)S(1)}, f32[256,128]{1,0:T(8,128)S(1)}, u32[]{:S(2)}, u32[]{:S(2)}) collective-permute-start(f32[256,128]{1,0:T(8,128)S(1)} %shard_map.42.refs_1_), channel_id=1, source_target_pairs={{0,1},{1,0},{2,3},{3,2},{4,5},{5,4},{6,7},{7,6},{8,9},{9,8},{10,11... | collective-permute-start | bytes 393224 | tf_op jit(solution)/shard_map/ppermute | solution.py:106
  53.1 5.9 %collective-permute-start.28 = (f32[256,128]{1,0:T(8,128)S(1)}, f32[256,128]{1,0:T(8,128)S(1)}, u32[]{:S(2)}, u32[]{:S(2)}) collective-permute-start(f32[256,128]{1,0:T(8,128)S(1)} %shard_map.46.refs_1_), channel_id=1, source_target_pairs={{0,1},{1,0},{2,3},{3,2},{4,5},{5,4},{6,7},{7,6},{8,9},{9,8},{10,11... | collective-permute-start | bytes 393224 | tf_op jit(solution)/shard_map/ppermute | solution.py:106
  56.6 2.8 %collective-permute-start.23 = (f32[256,128]{1,0:T(8,128)S(1)}, f32[256,128]{1,0:T(8,128)S(1)}, u32[]{:S(2)}, u32[]{:S(2)}) collective-permute-start(f32[256,128]{1,0:T(8,128)S(1)} %collective-permute-done.22.refs_2_), channel_id=1, source_target_pairs={{0,1},{1,0},{2,3},{3,2},{4,5},{5,4},{6,7},{7,6},{8,9},{9,8},{10,11... | collective-permute-start | bytes 393224 | tf_op jit(solution)/shard_map/ppermute | solution.py:106
  58.6 1.8 %collective-permute-start.30 = (f32[256,128]{1,0:T(8,128)S(1)}, f32[256,128]{1,0:T(8,128)S(1)}, u32[]{:S(2)}, u32[]{:S(2)}) collective-permute-start(f32[256,128]{1,0:T(8,128)S(1)} %collective-permute-done.29.refs_2_), channel_id=1, source_target_pairs={{0,1},{1,0},{2,3},{3,2},{4,5},{5,4},{6,7},{7,6},{8,9},{9,8},{10,11... | collective-permute-start | bytes 393224 | tf_op jit(solution)/shard_map/ppermute | solution.py:106
  59.7 3.1 %collective-permute-start.31 = (f32[256,128]{1,0:T(8,128)S(1)}, f32[256,128]{1,0:T(8,128)S(1)}, u32[]{:S(2)}, u32[]{:S(2)}) collective-permute-start(f32[256,128]{1,0:T(8,128)S(1)} %shard_map.44.refs_0_), channel_id=1, source_target_pairs={{0,18},{1,19},{2,16},{3,17}} | collective-permute-start | bytes 393224 | tf_op jit(solution)/shard_map/ppermute | solution.py:106
  60.8 2.6 %collective-permute-start.35 = (f32[256,128]{1,0:T(8,128)S(1)}, f32[256,128]{1,0:T(8,128)S(1)}, u32[]{:S(2)}, u32[]{:S(2)}) collective-permute-start(f32[256,128]{1,0:T(8,128)S(1)} %shard_map.48.refs_0_), channel_id=1, source_target_pairs={{0,18},{1,19},{2,16},{3,17}} | collective-permute-start | bytes 393224 | tf_op jit(solution)/shard_map/ppermute | solution.py:106
  61.5 2.1 %collective-permute-start.33 = (f32[256,128]{1,0:T(8,128)S(1)}, f32[256,128]{1,0:T(8,128)S(1)}, u32[]{:S(2)}, u32[]{:S(2)}) collective-permute-start(f32[256,128]{1,0:T(8,128)S(1)} %shard_map.44.refs_0_), channel_id=1, source_target_pairs={{0,16},{1,17},{2,18},{3,19}} | collective-permute-start | bytes 393224 | tf_op jit(solution)/shard_map/ppermute | solution.py:106
  62.2 1.8 %collective-permute-start.37 = (f32[256,128]{1,0:T(8,128)S(1)}, f32[256,128]{1,0:T(8,128)S(1)}, u32[]{:S(2)}, u32[]{:S(2)}) collective-permute-start(f32[256,128]{1,0:T(8,128)S(1)} %shard_map.48.refs_0_), channel_id=1, source_target_pairs={{0,16},{1,17},{2,18},{3,19}} | collective-permute-start | bytes 393224 | tf_op jit(solution)/shard_map/ppermute | solution.py:106
  62.9 1.6 %collective-permute-start.32 = (f32[256,128]{1,0:T(8,128)S(1)}, f32[256,128]{1,0:T(8,128)S(1)}, u32[]{:S(2)}, u32[]{:S(2)}) collective-permute-start(f32[256,128]{1,0:T(8,128)S(1)} %collective-permute-done.31.refs_2_), channel_id=1, source_target_pairs={{0,1},{1,0},{2,3},{3,2},{4,5},{5,4},{6,7},{7,6},{8,9},{9,8},{10,11... | collective-permute-start | bytes 393224 | tf_op jit(solution)/shard_map/ppermute | solution.py:106
  63.5 1.7 %collective-permute-start.34 = (f32[256,128]{1,0:T(8,128)S(1)}, f32[256,128]{1,0:T(8,128)S(1)}, u32[]{:S(2)}, u32[]{:S(2)}) collective-permute-start(f32[256,128]{1,0:T(8,128)S(1)} %collective-permute-done.33.refs_2_), channel_id=1, source_target_pairs={{0,1},{1,0},{2,3},{3,2},{4,5},{5,4},{6,7},{7,6},{8,9},{9,8},{10,11... | collective-permute-start | bytes 393224 | tf_op jit(solution)/shard_map/ppermute | solution.py:106
  64.0 1.6 %collective-permute-start.38 = (f32[256,128]{1,0:T(8,128)S(1)}, f32[256,128]{1,0:T(8,128)S(1)}, u32[]{:S(2)}, u32[]{:S(2)}) collective-permute-start(f32[256,128]{1,0:T(8,128)S(1)} %collective-permute-done.37.refs_2_), channel_id=1, source_target_pairs={{0,1},{1,0},{2,3},{3,2},{4,5},{5,4},{6,7},{7,6},{8,9},{9,8},{10,11... | collective-permute-start | bytes 393224 | tf_op jit(solution)/shard_map/ppermute | solution.py:106
  66.0 33.2 %collective-permute-start.41 = (f32[256,256]{1,0:T(8,128)S(1)}, f32[256,256]{1,0:T(8,128)S(1)}, u32[]{:S(2)}, u32[]{:S(2)}) collective-permute-start(f32[256,256]{1,0:T(8,128)S(1)} %pad_maximum_fusion.1.refs_1_), channel_id=1, source_target_pairs={{0,10},{1,11},{2,8},{3,9},{16,26},{17,27},{18,24},{19,25}} | collective-permute-start | bytes 786440 | tf_op jit(solution)/shard_map/ppermute | solution.py:106
  67.3 35.5 %collective-permute-start.39 = (f32[256,256]{1,0:T(8,128)S(1)}, f32[256,256]{1,0:T(8,128)S(1)}, u32[]{:S(2)}, u32[]{:S(2)}) collective-permute-start(f32[256,256]{1,0:T(8,128)S(1)} %pad_maximum_fusion.1.refs_1_), channel_id=1, source_target_pairs={{16,10},{17,11},{18,8},{19,9}} | collective-permute-start | bytes 786440 | tf_op jit(solution)/shard_map/ppermute | solution.py:106
  68.6 34.5 %collective-permute-start.45 = (f32[256,256]{1,0:T(8,128)S(1)}, f32[256,256]{1,0:T(8,128)S(1)}, u32[]{:S(2)}, u32[]{:S(2)}) collective-permute-start(f32[256,256]{1,0:T(8,128)S(1)} %pad_maximum_fusion.1.refs_1_), channel_id=1, source_target_pairs={{0,8},{1,9},{2,10},{3,11},{16,24},{17,25},{18,26},{19,27}} | collective-permute-start | bytes 786440 | tf_op jit(solution)/shard_map/ppermute | solution.py:106
  69.9 37.6 %collective-permute-start.43 = (f32[256,256]{1,0:T(8,128)S(1)}, f32[256,256]{1,0:T(8,128)S(1)}, u32[]{:S(2)}, u32[]{:S(2)}) collective-permute-start(f32[256,256]{1,0:T(8,128)S(1)} %pad_maximum_fusion.1.refs_1_), channel_id=1, source_target_pairs={{16,8},{17,9},{18,10},{19,11}} | collective-permute-start | bytes 786440 | tf_op jit(solution)/shard_map/ppermute | solution.py:106
  99.2 8.3 %collective-permute-start.42 = (f32[256,256]{1,0:T(8,128)S(1)}, f32[256,256]{1,0:T(8,128)S(1)}, u32[]{:S(2)}, u32[]{:S(2)}) collective-permute-start(f32[256,256]{1,0:T(8,128)S(1)} %collective-permute-done.41.refs_6_), channel_id=1, source_target_pairs={{0,1},{1,0},{2,3},{3,2},{4,5},{5,4},{6,7},{7,6},{8,9},{9,8},{10,11... | collective-permute-start | bytes 786440 | tf_op jit(solution)/shard_map/ppermute | solution.py:106
  102.8 4.8 %collective-permute-start.40 = (f32[256,256]{1,0:T(8,128)S(1)}, f32[256,256]{1,0:T(8,128)S(1)}, u32[]{:S(2)}, u32[]{:S(2)}) collective-permute-start(f32[256,256]{1,0:T(8,128)S(1)} %collective-permute-done.39.refs_3_), channel_id=1, source_target_pairs={{0,1},{1,0},{2,3},{3,2},{4,5},{5,4},{6,7},{7,6},{8,9},{9,8},{10,11... | collective-permute-start | bytes 786440 | tf_op jit(solution)/shard_map/ppermute | solution.py:106
  103.1 5.2 %collective-permute-start.46 = (f32[256,256]{1,0:T(8,128)S(1)}, f32[256,256]{1,0:T(8,128)S(1)}, u32[]{:S(2)}, u32[]{:S(2)}) collective-permute-start(f32[256,256]{1,0:T(8,128)S(1)} %collective-permute-done.45.refs_5_), channel_id=1, source_target_pairs={{0,1},{1,0},{2,3},{3,2},{4,5},{5,4},{6,7},{7,6},{8,9},{9,8},{10,11... | collective-permute-start | bytes 786440 | tf_op jit(solution)/shard_map/ppermute | solution.py:106
  109.7 9.3 %collective-permute-start.49 = (f32[256,256]{1,0:T(8,128)S(1)}, f32[256,256]{1,0:T(8,128)S(1)}, u32[]{:S(2)}, u32[]{:S(2)}) collective-permute-start(f32[256,256]{1,0:T(8,128)S(1)} %shard_map.54.refs_1_), channel_id=1, source_target_pairs={{0,26},{1,27},{2,24},{3,25},{4,30},{5,31},{6,28},{7,29},{8,2},{9,3... | collective-permute-start | bytes 786440 | tf_op jit(solution)/shard_map/ppermute | solution.py:106
  109.8 10.5 %collective-permute-start.47 = (f32[256,256]{1,0:T(8,128)S(1)}, f32[256,256]{1,0:T(8,128)S(1)}, u32[]{:S(2)}, u32[]{:S(2)}) collective-permute-start(f32[256,256]{1,0:T(8,128)S(1)} %shard_map.54.refs_1_), channel_id=1, source_target_pairs={{0,4},{1,5},{2,6},{3,7},{8,12},{9,13},{10,14},{11,15},{16,20},{17,... | collective-permute-start | bytes 786440 | tf_op jit(solution)/shard_map/ppermute | solution.py:106
  119.0 6.6 %collective-permute-start.50 = (f32[256,256]{1,0:T(8,128)S(1)}, f32[256,256]{1,0:T(8,128)S(1)}, u32[]{:S(2)}, u32[]{:S(2)}) collective-permute-start(f32[256,256]{1,0:T(8,128)S(1)} %collective-permute-done.49), channel_id=1, source_target_pairs={{0,4},{1,5},{2,6},{3,7},{8,12},{9,13},{10,14},{11,15},{16,20},{17,... | collective-permute-start | bytes 786440 | tf_op jit(solution)/shard_map/ppermute | solution.py:106
  120.3 7.6 %collective-permute-start.54 = (f32[256,256]{1,0:T(8,128)S(1)}, f32[256,256]{1,0:T(8,128)S(1)}, u32[]{:S(2)}, u32[]{:S(2)}) collective-permute-start(f32[256,256]{1,0:T(8,128)S(1)} %collective-permute-done.47.refs_3_), channel_id=1, source_target_pairs={{0,24},{1,25},{2,26},{3,27},{4,28},{5,29},{6,30},{7,31},{8,0},{9,1... | collective-permute-start | bytes 786440 | tf_op jit(solution)/shard_map/ppermute | solution.py:106
  120.4 7.6 %collective-permute-start.52 = (f32[256,256]{1,0:T(8,128)S(1)}, f32[256,256]{1,0:T(8,128)S(1)}, u32[]{:S(2)}, u32[]{:S(2)}) collective-permute-start(f32[256,256]{1,0:T(8,128)S(1)} %collective-permute-done.47.refs_3_), channel_id=1, source_target_pairs={{0,2},{1,3},{2,0},{3,1},{4,6},{5,7},{6,4},{7,5},{8,10},{9,11},{10,... | collective-permute-start | bytes 786440 | tf_op jit(solution)/shard_map/ppermute | solution.py:106
  121.5 6.8 %collective-permute-start.48 = (f32[256,256]{1,0:T(8,128)S(1)}, f32[256,256]{1,0:T(8,128)S(1)}, u32[]{:S(2)}, u32[]{:S(2)}) collective-permute-start(f32[256,256]{1,0:T(8,128)S(1)} %collective-permute-done.47.refs_3_), channel_id=1, source_target_pairs={{0,1},{1,0},{2,3},{3,2},{4,5},{5,4},{6,7},{7,6},{8,9},{9,8},{10,11... | collective-permute-start | bytes 786440 | tf_op jit(solution)/shard_map/ppermute | solution.py:106
  125.6 2.8 %collective-permute-start.51 = (f32[256,256]{1,0:T(8,128)S(1)}, f32[256,256]{1,0:T(8,128)S(1)}, u32[]{:S(2)}, u32[]{:S(2)}) collective-permute-start(f32[256,256]{1,0:T(8,128)S(1)} %collective-permute-done.50.refs_6_), channel_id=1, source_target_pairs={{0,1},{1,0},{2,3},{3,2},{4,5},{5,4},{6,7},{7,6},{8,9},{9,8},{10,11... | collective-permute-start | bytes 786440 | tf_op jit(solution)/shard_map/ppermute | solution.py:106
  127.9 1.8 %collective-permute-start.53 = (f32[256,256]{1,0:T(8,128)S(1)}, f32[256,256]{1,0:T(8,128)S(1)}, u32[]{:S(2)}, u32[]{:S(2)}) collective-permute-start(f32[256,256]{1,0:T(8,128)S(1)} %collective-permute-done.52.refs_2_), channel_id=1, source_target_pairs={{0,1},{1,0},{2,3},{3,2},{4,5},{5,4},{6,7},{7,6},{8,9},{9,8},{10,11... | collective-permute-start | bytes 786440 | tf_op jit(solution)/shard_map/ppermute | solution.py:106
  (11 other events, 30.3 us)

commit v7 on v6

--- a/solution.py
+++ b/solution.py
@@ -143,7 +143,7 @@
     current = right_side[0]
 
     def hop(block, by):
-        return move(block, [(i, i - by) for i in range(1 if by > 0 else 0, layers, 2)])
+        return move(block, [(i, i ^ 1) for i in range(layers)])
 
     def near_shards(near):
         return within(near)

time: 133 us -> 130 us (0.977)
  starting transfers between devices: 33.4 us -> 29.8 us
    ppermute x52, starting transfers between devices: 28.8 us -> 25.8 us  [move(): return lax.ppermute(block, AXES, hops) if hops else None]
  transfers between devices with their start and end apart: 56 -> 56, of which waited for: 26 -> 22; matrix products, arithmetic and copies ran while one was open for 0% -> 0% of each run, Pallas kernels for 6% -> 6%
where the time goes in v7:
time: 130 us; the launch traced here: 128 us
  waiting for transfers between devices  81.7 us (63%)
  starting transfers between devices  29.8 us (23%)
  Pallas kernels  11.7 us (9%)
  local copies, waits for them, and re-layouts  4.7 us (4%)
    ppermute x52, waiting for transfers between devices, move(): return lax.ppermute(block, AXES, hops) if hops else None  66.7 us
    ppermute x52, starting transfers between devices, move(): return lax.ppermute(block, AXES, hops) if hops else None  25.8 us
    ppermute x4, waiting for transfers between devices, traded(): out.append((flip, lax.ppermute(block, AXES, hops)))  15 us
    pallas_call x19, Pallas kernels, combine(): pl.pallas_call(functools.partial(combine_kernel, shape, sign, only), out_...  9.96 us
    unnamed x6, local copies, waits for them, and re-layouts  4.68 us
    ppermute x4, starting transfers between devices, traded(): out.append((flip, lax.ppermute(block, AXES, hops)))  4.05 us
  transfers between devices with their start and end apart: 56, of which 22 were waited for; matrix products, arithmetic and copies ran while one was open for 0% of the time, Pallas kernels for 6%

profile of v7, /device:TPU:8, one launch (start us, length us, event | category | flops | bytes accessed | tf_op | source)
XLA Modules:
  0.0 128.4 jit_solution(18218866401079254876)
XLA Ops:
  0.0 1.5 %collective-permute-start = (f32[256,256]{1,0:T(8,128)}, f32[256,256]{1,0:T(8,128)S(1)}, u32[]{:S(2)}, u32[]{:S(2)}) collective-permute-start(f32[256,256]{1,0:T(8,128)} %bitcast.6), channel_id=1, source_target_pairs={{0,4},{1,5},{2,6},{3,7},{4,0},{5,1},{6,2},{7,3},{8,12},{9,13},{10,... | collective-permute-start | bytes 786440 | tf_op jit(solution)/shard_map/ppermute | solution.py:106
  1.5 2.5 %collective-permute-start.6 = (f32[256,256]{1,0:T(8,128)}, f32[256,256]{1,0:T(8,128)S(1)}, u32[]{:S(2)}, u32[]{:S(2)}) collective-permute-start(f32[256,256]{1,0:T(8,128)} %bitcast.7), channel_id=1, source_target_pairs={{0,10},{1,11},{2,8},{3,9},{4,14},{5,15},{6,12},{7,13},{8,18},{9,19... | collective-permute-start | bytes 786440 | tf_op jit(solution)/shard_map/ppermute | solution.py:106
  4.0 2.8 %copy-done = f32[3,1,2,256,1024]{4,3,2,1,0:T(8,128)S(1)} copy-done((f32[3,1,2,256,1024]{4,3,2,1,0:T(8,128)S(1)}, f32[3,1,2,256,1024]{4,3,2,1,0:T(8,128)}, u32[]{:S(2)}) %copy-start) | copy-done | bytes 6291480
  6.8 1.9 %copy-done.1 = f32[1,3,256,1024]{3,2,1,0:T(8,128)S(1)} copy-done((f32[1,3,256,1024]{3,2,1,0:T(8,128)S(1)}, f32[1,3,256,1024]{3,2,1,0:T(8,128)}, u32[]{:S(2)}) %copy-start.1) | copy-done | bytes 3145752
  8.7 1.7 %shard_map.37 = (f32[256,1024]{1,0:T(8,128)S(1)}, f32[256,1024]{1,0:T(8,128)S(1)}, f32[256,1024]{1,0:T(8,128)S(1)}, f32[256,1024]{1,0:T(8,128)S(1)}, f32[256,102...) custom-call(f32[3,2,256,1024]{3,2,1,0:T(8,128)S(1)} %bitcast.4, ...), custom_call_target="tpu_custom_call" | custom-call | tf_op jit(solution)/shard_map/pallas_call | solution.py:87
  10.5 0.6 collective-permute-start.7
  11.1 1.6 %collective-permute-start.4 = (f32[256,256]{1,0:T(8,128)S(1)}, f32[256,256]{1,0:T(8,128)S(1)}, u32[]{:S(2)}, u32[]{:S(2)}) collective-permute-start(f32[256,256]{1,0:T(8,128)S(1)} %collective-permute-done.refs_2_), channel_id=1, source_target_pairs={{0,8},{1,9},{2,10},{3,11},{4,12},{5,13},{6,14},{7,15},{8,16},{9,17... | collective-permute-start | bytes 786440 | tf_op jit(solution)/shard_map/ppermute | solution.py:106
  12.6 1.4 %collective-permute-start.2 = (f32[256,256]{1,0:T(8,128)S(1)}, f32[256,256]{1,0:T(8,128)S(1)}, u32[]{:S(2)}, u32[]{:S(2)}) collective-permute-start(f32[256,256]{1,0:T(8,128)S(1)} %collective-permute-done.refs_2_), channel_id=1, source_target_pairs={{0,2},{1,3},{2,0},{3,1},{4,6},{5,7},{6,4},{7,5},{8,10},{9,11},{10,... | collective-permute-start | bytes 786440 | tf_op jit(solution)/shard_map/ppermute | solution.py:106
  14.0 4.0 %collective-permute-done.7.refs_9_ = f32[256,256]{1,0:T(8,128)S(1)} collective-permute-done((f32[256,256]{1,0:T(8,128)S(1)}, f32[256,256]{1,0:T(8,128)S(1)}, u32[]{:S(2)}, u32[]{:S(2)}) %collective-permute-start.7) | collective-permute-done | bytes 262176 | tf_op jit(solution)/shard_map/ppermute | solution.py:106
  18.5 1.0 collective-permute-done.2.refs_4_
  20.0 1.1 collective-permute-done.3.refs_5_
  21.1 1.1 shard_map.38.refs_0_
  22.2 1.9 %collective-permute-start.11 = (f32[256,256]{1,0:T(8,128)S(1)}, f32[256,256]{1,0:T(8,128)S(1)}, u32[]{:S(2)}, u32[]{:S(2)}) collective-permute-start(f32[256,256]{1,0:T(8,128)S(1)} %shard_map.38.refs_0_), channel_id=1, source_target_pairs={{0,1},{1,0},{2,3},{3,2},{4,5},{5,4},{6,7},{7,6},{8,18},{9,19},{10,... | collective-permute-start | bytes 786440 | tf_op jit(solution)/shard_map/ppermute | solution.py:125
  24.1 1.6 %collective-permute-start.9 = (f32[256,256]{1,0:T(8,128)S(1)}, f32[256,256]{1,0:T(8,128)S(1)}, u32[]{:S(2)}, u32[]{:S(2)}) collective-permute-start(f32[256,256]{1,0:T(8,128)S(1)} %shard_map.38.refs_0_), channel_id=1, source_target_pairs={{0,10},{1,11},{2,8},{3,9},{4,5},{5,4},{6,7},{7,6},{8,2},{9,3},{10,... | collective-permute-start | bytes 786440 | tf_op jit(solution)/shard_map/ppermute | solution.py:125
  26.2 9.3 %collective-permute-done.11.refs_5_ = f32[256,256]{1,0:T(8,128)S(1)} collective-permute-done((f32[256,256]{1,0:T(8,128)S(1)}, f32[256,256]{1,0:T(8,128)S(1)}, u32[]{:S(2)}, u32[]{:S(2)}) %collective-permute-start.11) | collective-permute-done | bytes 262176 | tf_op jit(solution)/shard_map/ppermute | solution.py:125
  35.6 2.1 %collective-permute-done.9.refs_2_ = f32[256,256]{1,0:T(8,128)S(1)} collective-permute-done((f32[256,256]{1,0:T(8,128)S(1)}, f32[256,256]{1,0:T(8,128)S(1)}, u32[]{:S(2)}, u32[]{:S(2)}) %collective-permute-start.9) | collective-permute-done | bytes 262176 | tf_op jit(solution)/shard_map/ppermute | solution.py:125
  37.6 1.4 %collective-permute-done.15.refs_5_ = f32[256,256]{1,0:T(8,128)S(1)} collective-permute-done((f32[256,256]{1,0:T(8,128)S(1)}, f32[256,256]{1,0:T(8,128)S(1)}, u32[]{:S(2)}, u32[]{:S(2)}) %collective-permute-start.15) | collective-permute-done | bytes 262176 | tf_op jit(solution)/shard_map/ppermute | solution.py:125
  39.0 2.2 %collective-permute-done.13.refs_2_ = f32[256,256]{1,0:T(8,128)S(1)} collective-permute-done((f32[256,256]{1,0:T(8,128)S(1)}, f32[256,256]{1,0:T(8,128)S(1)}, u32[]{:S(2)}, u32[]{:S(2)}) %collective-permute-start.13) | collective-permute-done | bytes 262176 | tf_op jit(solution)/shard_map/ppermute | solution.py:125
  41.2 0.6 shard_map.39.refs_0_
  41.9 0.9 collective-permute-done.14.refs_3_
  42.7 0.6 shard_map.40
  43.4 0.7 collective-permute-start.17
  44.1 0.7 collective-permute-start.19
  44.8 0.7 collective-permute-start.24
  45.4 0.7 collective-permute-start.26
  48.3 1.6 %collective-permute-start.22 = (f32[256,128]{1,0:T(8,128)S(1)}, f32[256,128]{1,0:T(8,128)S(1)}, u32[]{:S(2)}, u32[]{:S(2)}) collective-permute-start(f32[256,128]{1,0:T(8,128)S(1)} %shard_map.42.refs_1_), channel_id=1, source_target_pairs={{0,2},{1,3},{2,0},{3,1},{4,6},{5,7},{6,4},{7,5},{8,10},{9,11},{10,... | collective-permute-start | bytes 393224 | tf_op jit(solution)/shard_map/ppermute | solution.py:106
  51.7 2.9 %collective-permute-done.22.refs_2_ = f32[256,128]{1,0:T(8,128)S(1)} collective-permute-done((f32[256,128]{1,0:T(8,128)S(1)}, f32[256,128]{1,0:T(8,128)S(1)}, u32[]{:S(2)}, u32[]{:S(2)}) %collective-permute-start.22) | collective-permute-done | bytes 131104 | tf_op jit(solution)/shard_map/ppermute | solution.py:106
  54.6 2.1 %collective-permute-done.29.refs_2_ = f32[256,128]{1,0:T(8,128)S(1)} collective-permute-done((f32[256,128]{1,0:T(8,128)S(1)}, f32[256,128]{1,0:T(8,128)S(1)}, u32[]{:S(2)}, u32[]{:S(2)}) %collective-permute-start.29) | collective-permute-done | bytes 131104 | tf_op jit(solution)/shard_map/ppermute | solution.py:106
  57.9 0.7 collective-permute-start.31
  58.9 0.7 collective-permute-start.35
  59.6 0.7 collective-permute-start.33
  60.3 0.7 collective-permute-start.37
  64.1 1.3 %collective-permute-start.41 = (f32[256,256]{1,0:T(8,128)S(1)}, f32[256,256]{1,0:T(8,128)S(1)}, u32[]{:S(2)}, u32[]{:S(2)}) collective-permute-start(f32[256,256]{1,0:T(8,128)S(1)} %pad_maximum_fusion.1.refs_1_), channel_id=1, source_target_pairs={{0,10},{1,11},{2,8},{3,9},{16,26},{17,27},{18,24},{19,25}} | collective-permute-start | bytes 786440 | tf_op jit(solution)/shard_map/ppermute | solution.py:106
  65.4 1.3 %collective-permute-start.39 = (f32[256,256]{1,0:T(8,128)S(1)}, f32[256,256]{1,0:T(8,128)S(1)}, u32[]{:S(2)}, u32[]{:S(2)}) collective-permute-start(f32[256,256]{1,0:T(8,128)S(1)} %pad_maximum_fusion.1.refs_1_), channel_id=1, source_target_pairs={{16,10},{17,11},{18,8},{19,9}} | collective-permute-start | bytes 786440 | tf_op jit(solution)/shard_map/ppermute | solution.py:106
  66.7 1.3 %collective-permute-start.45 = (f32[256,256]{1,0:T(8,128)S(1)}, f32[256,256]{1,0:T(8,128)S(1)}, u32[]{:S(2)}, u32[]{:S(2)}) collective-permute-start(f32[256,256]{1,0:T(8,128)S(1)} %pad_maximum_fusion.1.refs_1_), channel_id=1, source_target_pairs={{0,8},{1,9},{2,10},{3,11},{16,24},{17,25},{18,26},{19,27}} | collective-permute-start | bytes 786440 | tf_op jit(solution)/shard_map/ppermute | solution.py:106
  68.0 1.3 %collective-permute-start.43 = (f32[256,256]{1,0:T(8,128)S(1)}, f32[256,256]{1,0:T(8,128)S(1)}, u32[]{:S(2)}, u32[]{:S(2)}) collective-permute-start(f32[256,256]{1,0:T(8,128)S(1)} %pad_maximum_fusion.1.refs_1_), channel_id=1, source_target_pairs={{16,8},{17,9},{18,10},{19,11}} | collective-permute-start | bytes 786440 | tf_op jit(solution)/shard_map/ppermute | solution.py:106
  69.3 28.5 %collective-permute-done.41.refs_6_ = f32[256,256]{1,0:T(8,128)S(1)} collective-permute-done((f32[256,256]{1,0:T(8,128)S(1)}, f32[256,256]{1,0:T(8,128)S(1)}, u32[]{:S(2)}, u32[]{:S(2)}) %collective-permute-start.41) | collective-permute-done | bytes 262176 | tf_op jit(solution)/shard_map/ppermute | solution.py:106
  97.8 3.5 %collective-permute-done.39.refs_3_ = f32[256,256]{1,0:T(8,128)S(1)} collective-permute-done((f32[256,256]{1,0:T(8,128)S(1)}, f32[256,256]{1,0:T(8,128)S(1)}, u32[]{:S(2)}, u32[]{:S(2)}) %collective-permute-start.39) | collective-permute-done | bytes 262176 | tf_op jit(solution)/shard_map/ppermute | solution.py:106
  101.8 4.0 %collective-permute-done.43.refs_2_ = f32[256,256]{1,0:T(8,128)S(1)} collective-permute-done((f32[256,256]{1,0:T(8,128)S(1)}, f32[256,256]{1,0:T(8,128)S(1)}, u32[]{:S(2)}, u32[]{:S(2)}) %collective-permute-start.43) | collective-permute-done | bytes 262176 | tf_op jit(solution)/shard_map/ppermute | solution.py:106
  105.8 0.7 shard_map.53.refs_0_
  106.5 0.8 collective-permute-done.44.refs_3_
  107.3 0.6 shard_map.54.refs_1_
  108.1 9.1 %collective-permute-done.49 = f32[256,256]{1,0:T(8,128)S(1)} collective-permute-done((f32[256,256]{1,0:T(8,128)S(1)}, f32[256,256]{1,0:T(8,128)S(1)}, u32[]{:S(2)}, u32[]{:S(2)}) %collective-permute-start.49) | collective-permute-done | bytes 262176 | tf_op jit(solution)/shard_map/ppermute | solution.py:106
  117.4 1.2 collective-permute-start.52
  118.7 6.1 %collective-permute-done.50.refs_6_ = f32[256,256]{1,0:T(8,128)S(1)} collective-permute-done((f32[256,256]{1,0:T(8,128)S(1)}, f32[256,256]{1,0:T(8,128)S(1)}, u32[]{:S(2)}, u32[]{:S(2)}) %collective-permute-start.50) | collective-permute-done | bytes 262176 | tf_op jit(solution)/shard_map/ppermute | solution.py:106
  125.4 0.9 collective-permute-done.51.refs_7_
  126.3 0.6 shard_map.55.refs_0_
  127.1 1.3 %shard_map.56 = f32[256,256]{1,0:T(8,128)} custom-call(f32[256,256]{1,0:T(8,128)S(1)} %shard_map.55.refs_0_, f32[256,1024]{1,0:T(8,128)S(1)} %get-tuple-element.37.refs_1_.refs_5_.refs_4_.refs_2_, f32[256,256]{1,0:T(8,128)S(1)} %collective-permute-done.52.refs_2_, f32[256,256]{1,0:T(8,128)S(1)} %collective-permute-done.53.refs_3_, ...), custom_call_target="tpu_custom_call" | custom-call | flops 402653184 | tf_op jit(solution)/shard_map/pallas_call | solution.py:62
  (93 shorter events, 11.6 us)
Async XLA Ops:
  0.0 10.4 %collective-permute-start = (f32[256,256]{1,0:T(8,128)}, f32[256,256]{1,0:T(8,128)S(1)}, u32[]{:S(2)}, u32[]{:S(2)}) collective-permute-start(f32[256,256]{1,0:T(8,128)} %bitcast.6), channel_id=1, source_target_pairs={{0,4},{1,5},{2,6},{3,7},{4,0},{5,1},{6,2},{7,3},{8,12},{9,13},{10,... | collective-permute-start | bytes 786440 | tf_op jit(solution)/shard_map/ppermute | solution.py:106
  1.5 9.0 %collective-permute-start.6 = (f32[256,256]{1,0:T(8,128)}, f32[256,256]{1,0:T(8,128)S(1)}, u32[]{:S(2)}, u32[]{:S(2)}) collective-permute-start(f32[256,256]{1,0:T(8,128)} %bitcast.7), channel_id=1, source_target_pairs={{0,10},{1,11},{2,8},{3,9},{4,14},{5,15},{6,12},{7,13},{8,18},{9,19... | collective-permute-start | bytes 786440 | tf_op jit(solution)/shard_map/ppermute | solution.py:106
  10.5 7.6 %collective-permute-start.7 = (f32[256,256]{1,0:T(8,128)S(1)}, f32[256,256]{1,0:T(8,128)S(1)}, u32[]{:S(2)}, u32[]{:S(2)}) collective-permute-start(f32[256,256]{1,0:T(8,128)S(1)} %collective-permute-done.6), channel_id=1, source_target_pairs={{0,4},{1,5},{2,6},{3,7},{4,0},{5,1},{6,2},{7,3},{8,12},{9,13},{10,... | collective-permute-start | bytes 786440 | tf_op jit(solution)/shard_map/ppermute | solution.py:106
  11.1 7.4 %collective-permute-start.4 = (f32[256,256]{1,0:T(8,128)S(1)}, f32[256,256]{1,0:T(8,128)S(1)}, u32[]{:S(2)}, u32[]{:S(2)}) collective-permute-start(f32[256,256]{1,0:T(8,128)S(1)} %collective-permute-done.refs_2_), channel_id=1, source_target_pairs={{0,8},{1,9},{2,10},{3,11},{4,12},{5,13},{6,14},{7,15},{8,16},{9,17... | collective-permute-start | bytes 786440 | tf_op jit(solution)/shard_map/ppermute | solution.py:106
  12.6 6.9 %collective-permute-start.2 = (f32[256,256]{1,0:T(8,128)S(1)}, f32[256,256]{1,0:T(8,128)S(1)}, u32[]{:S(2)}, u32[]{:S(2)}) collective-permute-start(f32[256,256]{1,0:T(8,128)S(1)} %collective-permute-done.refs_2_), channel_id=1, source_target_pairs={{0,2},{1,3},{2,0},{3,1},{4,6},{5,7},{6,4},{7,5},{8,10},{9,11},{10,... | collective-permute-start | bytes 786440 | tf_op jit(solution)/shard_map/ppermute | solution.py:106
  14.0 5.6 %collective-permute-start.1 = (f32[256,256]{1,0:T(8,128)S(1)}, f32[256,256]{1,0:T(8,128)S(1)}, u32[]{:S(2)}, u32[]{:S(2)}) collective-permute-start(f32[256,256]{1,0:T(8,128)S(1)} %collective-permute-done.refs_2_), channel_id=1, source_target_pairs={{0,1},{1,0},{2,3},{3,2},{4,5},{5,4},{6,7},{7,6},{8,9},{9,8},{10,11... | collective-permute-start | bytes 786440 | tf_op jit(solution)/shard_map/ppermute | solution.py:106
  18.0 1.6 %collective-permute-start.8 = (f32[256,256]{1,0:T(8,128)S(1)}, f32[256,256]{1,0:T(8,128)S(1)}, u32[]{:S(2)}, u32[]{:S(2)}) collective-permute-start(f32[256,256]{1,0:T(8,128)S(1)} %collective-permute-done.7.refs_9_), channel_id=1, source_target_pairs={{0,1},{1,0},{2,3},{3,2},{4,5},{5,4},{6,7},{7,6},{8,9},{9,8},{10,11... | collective-permute-start | bytes 786440 | tf_op jit(solution)/shard_map/ppermute | solution.py:106
  22.2 13.4 %collective-permute-start.11 = (f32[256,256]{1,0:T(8,128)S(1)}, f32[256,256]{1,0:T(8,128)S(1)}, u32[]{:S(2)}, u32[]{:S(2)}) collective-permute-start(f32[256,256]{1,0:T(8,128)S(1)} %shard_map.38.refs_0_), channel_id=1, source_target_pairs={{0,1},{1,0},{2,3},{3,2},{4,5},{5,4},{6,7},{7,6},{8,18},{9,19},{10,... | collective-permute-start | bytes 786440 | tf_op jit(solution)/shard_map/ppermute | solution.py:125
  24.1 13.6 %collective-permute-start.9 = (f32[256,256]{1,0:T(8,128)S(1)}, f32[256,256]{1,0:T(8,128)S(1)}, u32[]{:S(2)}, u32[]{:S(2)}) collective-permute-start(f32[256,256]{1,0:T(8,128)S(1)} %shard_map.38.refs_0_), channel_id=1, source_target_pairs={{0,10},{1,11},{2,8},{3,9},{4,5},{5,4},{6,7},{7,6},{8,2},{9,3},{10,... | collective-permute-start | bytes 786440 | tf_op jit(solution)/shard_map/ppermute | solution.py:125
  25.7 13.3 %collective-permute-start.15 = (f32[256,256]{1,0:T(8,128)S(1)}, f32[256,256]{1,0:T(8,128)S(1)}, u32[]{:S(2)}, u32[]{:S(2)}) collective-permute-start(f32[256,256]{1,0:T(8,128)S(1)} %shard_map.38.refs_0_), channel_id=1, source_target_pairs={{0,1},{1,0},{2,3},{3,2},{4,5},{5,4},{6,7},{7,6},{8,16},{9,17},{10,... | collective-permute-start | bytes 786440 | tf_op jit(solution)/shard_map/ppermute | solution.py:125
  26.2 15.0 %collective-permute-start.13 = (f32[256,256]{1,0:T(8,128)S(1)}, f32[256,256]{1,0:T(8,128)S(1)}, u32[]{:S(2)}, u32[]{:S(2)}) collective-permute-start(f32[256,256]{1,0:T(8,128)S(1)} %shard_map.38.refs_0_), channel_id=1, source_target_pairs={{0,8},{1,9},{2,10},{3,11},{4,5},{5,4},{6,7},{7,6},{8,0},{9,1},{10,... | collective-permute-start | bytes 786440 | tf_op jit(solution)/shard_map/ppermute | solution.py:125
  35.6 5.7 %collective-permute-start.12 = (f32[256,256]{1,0:T(8,128)S(1)}, f32[256,256]{1,0:T(8,128)S(1)}, u32[]{:S(2)}, u32[]{:S(2)}) collective-permute-start(f32[256,256]{1,0:T(8,128)S(1)} %collective-permute-done.11.refs_5_), channel_id=1, source_target_pairs={{0,1},{1,0},{2,3},{3,2},{4,5},{5,4},{6,7},{7,6},{8,9},{9,8},{10,11... | collective-permute-start | bytes 786440 | tf_op jit(solution)/shard_map/ppermute | solution.py:106
  37.6 3.6 %collective-permute-start.10 = (f32[256,256]{1,0:T(8,128)S(1)}, f32[256,256]{1,0:T(8,128)S(1)}, u32[]{:S(2)}, u32[]{:S(2)}) collective-permute-start(f32[256,256]{1,0:T(8,128)S(1)} %collective-permute-done.9.refs_2_), channel_id=1, source_target_pairs={{0,1},{1,0},{2,3},{3,2},{4,5},{5,4},{6,7},{7,6},{8,9},{9,8},{10,11... | collective-permute-start | bytes 786440 | tf_op jit(solution)/shard_map/ppermute | solution.py:106
  39.0 2.9 %collective-permute-start.16 = (f32[256,256]{1,0:T(8,128)S(1)}, f32[256,256]{1,0:T(8,128)S(1)}, u32[]{:S(2)}, u32[]{:S(2)}) collective-permute-start(f32[256,256]{1,0:T(8,128)S(1)} %collective-permute-done.15.refs_5_), channel_id=1, source_target_pairs={{0,1},{1,0},{2,3},{3,2},{4,5},{5,4},{6,7},{7,6},{8,9},{9,8},{10,11... | collective-permute-start | bytes 786440 | tf_op jit(solution)/shard_map/ppermute | solution.py:106
  43.4 2.7 %collective-permute-start.17 = (f32[256,128]{1,0:T(8,128)S(1)}, f32[256,128]{1,0:T(8,128)S(1)}, u32[]{:S(2)}, u32[]{:S(2)}) collective-permute-start(f32[256,128]{1,0:T(8,128)S(1)} %get-tuple-element.39.refs_0_), channel_id=1, source_target_pairs={{16,2},{17,3},{18,0},{19,1}} | collective-permute-start | bytes 393224 | tf_op jit(solution)/shard_map/ppermute | solution.py:106
  44.1 2.2 %collective-permute-start.19 = (f32[256,128]{1,0:T(8,128)S(1)}, f32[256,128]{1,0:T(8,128)S(1)}, u32[]{:S(2)}, u32[]{:S(2)}) collective-permute-start(f32[256,128]{1,0:T(8,128)S(1)} %get-tuple-element.39.refs_0_), channel_id=1, source_target_pairs={{16,0},{17,1},{18,2},{19,3}} | collective-permute-start | bytes 393224 | tf_op jit(solution)/shard_map/ppermute | solution.py:106
  44.8 1.9 %collective-permute-start.24 = (f32[256,128]{1,0:T(8,128)S(1)}, f32[256,128]{1,0:T(8,128)S(1)}, u32[]{:S(2)}, u32[]{:S(2)}) collective-permute-start(f32[256,128]{1,0:T(8,128)S(1)} %get-tuple-element.40.refs_0_), channel_id=1, source_target_pairs={{16,2},{17,3},{18,0},{19,1}} | collective-permute-start | bytes 393224 | tf_op jit(solution)/shard_map/ppermute | solution.py:106
  46.3 1.6 %collective-permute-start.20 = (f32[256,128]{1,0:T(8,128)S(1)}, f32[256,128]{1,0:T(8,128)S(1)}, u32[]{:S(2)}, u32[]{:S(2)}) collective-permute-start(f32[256,128]{1,0:T(8,128)S(1)} %collective-permute-done.19.refs_2_), channel_id=1, source_target_pairs={{0,1},{1,0},{2,3},{3,2},{4,5},{5,4},{6,7},{7,6},{8,9},{9,8},{10,11... | collective-permute-start | bytes 393224 | tf_op jit(solution)/shard_map/ppermute | solution.py:106
  46.7 3.2 %collective-permute-start.25 = (f32[256,128]{1,0:T(8,128)S(1)}, f32[256,128]{1,0:T(8,128)S(1)}, u32[]{:S(2)}, u32[]{:S(2)}) collective-permute-start(f32[256,128]{1,0:T(8,128)S(1)} %collective-permute-done.24.refs_2_), channel_id=1, source_target_pairs={{0,1},{1,0},{2,3},{3,2},{4,5},{5,4},{6,7},{7,6},{8,9},{9,8},{10,11... | collective-permute-start | bytes 393224 | tf_op jit(solution)/shard_map/ppermute | solution.py:106
  46.8 3.4 %collective-permute-start.27 = (f32[256,128]{1,0:T(8,128)S(1)}, f32[256,128]{1,0:T(8,128)S(1)}, u32[]{:S(2)}, u32[]{:S(2)}) collective-permute-start(f32[256,128]{1,0:T(8,128)S(1)} %collective-permute-done.26.refs_2_), channel_id=1, source_target_pairs={{0,1},{1,0},{2,3},{3,2},{4,5},{5,4},{6,7},{7,6},{8,9},{9,8},{10,11... | collective-permute-start | bytes 393224 | tf_op jit(solution)/shard_map/ppermute | solution.py:106
  48.3 6.3 %collective-permute-start.22 = (f32[256,128]{1,0:T(8,128)S(1)}, f32[256,128]{1,0:T(8,128)S(1)}, u32[]{:S(2)}, u32[]{:S(2)}) collective-permute-start(f32[256,128]{1,0:T(8,128)S(1)} %shard_map.42.refs_1_), channel_id=1, source_target_pairs={{0,2},{1,3},{2,0},{3,1},{4,6},{5,7},{6,4},{7,5},{8,10},{9,11},{10,... | collective-permute-start | bytes 393224 | tf_op jit(solution)/shard_map/ppermute | solution.py:106
  50.6 6.1 %collective-permute-start.29 = (f32[256,128]{1,0:T(8,128)S(1)}, f32[256,128]{1,0:T(8,128)S(1)}, u32[]{:S(2)}, u32[]{:S(2)}) collective-permute-start(f32[256,128]{1,0:T(8,128)S(1)} %shard_map.46.refs_1_), channel_id=1, source_target_pairs={{0,2},{1,3},{2,0},{3,1},{4,6},{5,7},{6,4},{7,5},{8,10},{9,11},{10,... | collective-permute-start | bytes 393224 | tf_op jit(solution)/shard_map/ppermute | solution.py:106
  51.2 5.5 %collective-permute-start.21 = (f32[256,128]{1,0:T(8,128)S(1)}, f32[256,128]{1,0:T(8,128)S(1)}, u32[]{:S(2)}, u32[]{:S(2)}) collective-permute-start(f32[256,128]{1,0:T(8,128)S(1)} %shard_map.42.refs_1_), channel_id=1, source_target_pairs={{0,1},{1,0},{2,3},{3,2},{4,5},{5,4},{6,7},{7,6},{8,9},{9,8},{10,11... | collective-permute-start | bytes 393224 | tf_op jit(solution)/shard_map/ppermute | solution.py:106
  51.2 5.9 %collective-permute-start.28 = (f32[256,128]{1,0:T(8,128)S(1)}, f32[256,128]{1,0:T(8,128)S(1)}, u32[]{:S(2)}, u32[]{:S(2)}) collective-permute-start(f32[256,128]{1,0:T(8,128)S(1)} %shard_map.46.refs_1_), channel_id=1, source_target_pairs={{0,1},{1,0},{2,3},{3,2},{4,5},{5,4},{6,7},{7,6},{8,9},{9,8},{10,11... | collective-permute-start | bytes 393224 | tf_op jit(solution)/shard_map/ppermute | solution.py:106
  54.6 2.9 %collective-permute-start.23 = (f32[256,128]{1,0:T(8,128)S(1)}, f32[256,128]{1,0:T(8,128)S(1)}, u32[]{:S(2)}, u32[]{:S(2)}) collective-permute-start(f32[256,128]{1,0:T(8,128)S(1)} %collective-permute-done.22.refs_2_), channel_id=1, source_target_pairs={{0,1},{1,0},{2,3},{3,2},{4,5},{5,4},{6,7},{7,6},{8,9},{9,8},{10,11... | collective-permute-start | bytes 393224 | tf_op jit(solution)/shard_map/ppermute | solution.py:106
  56.7 1.8 %collective-permute-start.30 = (f32[256,128]{1,0:T(8,128)S(1)}, f32[256,128]{1,0:T(8,128)S(1)}, u32[]{:S(2)}, u32[]{:S(2)}) collective-permute-start(f32[256,128]{1,0:T(8,128)S(1)} %collective-permute-done.29.refs_2_), channel_id=1, source_target_pairs={{0,1},{1,0},{2,3},{3,2},{4,5},{5,4},{6,7},{7,6},{8,9},{9,8},{10,11... | collective-permute-start | bytes 393224 | tf_op jit(solution)/shard_map/ppermute | solution.py:106
  57.9 3.1 %collective-permute-start.31 = (f32[256,128]{1,0:T(8,128)S(1)}, f32[256,128]{1,0:T(8,128)S(1)}, u32[]{:S(2)}, u32[]{:S(2)}) collective-permute-start(f32[256,128]{1,0:T(8,128)S(1)} %shard_map.44.refs_0_), channel_id=1, source_target_pairs={{0,18},{1,19},{2,16},{3,17}} | collective-permute-start | bytes 393224 | tf_op jit(solution)/shard_map/ppermute | solution.py:106
  58.9 2.6 %collective-permute-start.35 = (f32[256,128]{1,0:T(8,128)S(1)}, f32[256,128]{1,0:T(8,128)S(1)}, u32[]{:S(2)}, u32[]{:S(2)}) collective-permute-start(f32[256,128]{1,0:T(8,128)S(1)} %shard_map.48.refs_0_), channel_id=1, source_target_pairs={{0,18},{1,19},{2,16},{3,17}} | collective-permute-start | bytes 393224 | tf_op jit(solution)/shard_map/ppermute | solution.py:106
  59.6 2.1 %collective-permute-start.33 = (f32[256,128]{1,0:T(8,128)S(1)}, f32[256,128]{1,0:T(8,128)S(1)}, u32[]{:S(2)}, u32[]{:S(2)}) collective-permute-start(f32[256,128]{1,0:T(8,128)S(1)} %shard_map.44.refs_0_), channel_id=1, source_target_pairs={{0,16},{1,17},{2,18},{3,19}} | collective-permute-start | bytes 393224 | tf_op jit(solution)/shard_map/ppermute | solution.py:106
  60.3 1.8 %collective-permute-start.37 = (f32[256,128]{1,0:T(8,128)S(1)}, f32[256,128]{1,0:T(8,128)S(1)}, u32[]{:S(2)}, u32[]{:S(2)}) collective-permute-start(f32[256,128]{1,0:T(8,128)S(1)} %shard_map.48.refs_0_), channel_id=1, source_target_pairs={{0,16},{1,17},{2,18},{3,19}} | collective-permute-start | bytes 393224 | tf_op jit(solution)/shard_map/ppermute | solution.py:106
  61.0 1.6 %collective-permute-start.32 = (f32[256,128]{1,0:T(8,128)S(1)}, f32[256,128]{1,0:T(8,128)S(1)}, u32[]{:S(2)}, u32[]{:S(2)}) collective-permute-start(f32[256,128]{1,0:T(8,128)S(1)} %collective-permute-done.31.refs_2_), channel_id=1, source_target_pairs={{0,1},{1,0},{2,3},{3,2},{4,5},{5,4},{6,7},{7,6},{8,9},{9,8},{10,11... | collective-permute-start | bytes 393224 | tf_op jit(solution)/shard_map/ppermute | solution.py:106
  61.6 1.7 %collective-permute-start.34 = (f32[256,128]{1,0:T(8,128)S(1)}, f32[256,128]{1,0:T(8,128)S(1)}, u32[]{:S(2)}, u32[]{:S(2)}) collective-permute-start(f32[256,128]{1,0:T(8,128)S(1)} %collective-permute-done.33.refs_2_), channel_id=1, source_target_pairs={{0,1},{1,0},{2,3},{3,2},{4,5},{5,4},{6,7},{7,6},{8,9},{9,8},{10,11... | collective-permute-start | bytes 393224 | tf_op jit(solution)/shard_map/ppermute | solution.py:106
  62.1 1.6 %collective-permute-start.38 = (f32[256,128]{1,0:T(8,128)S(1)}, f32[256,128]{1,0:T(8,128)S(1)}, u32[]{:S(2)}, u32[]{:S(2)}) collective-permute-start(f32[256,128]{1,0:T(8,128)S(1)} %collective-permute-done.37.refs_2_), channel_id=1, source_target_pairs={{0,1},{1,0},{2,3},{3,2},{4,5},{5,4},{6,7},{7,6},{8,9},{9,8},{10,11... | collective-permute-start | bytes 393224 | tf_op jit(solution)/shard_map/ppermute | solution.py:106
  64.1 33.7 %collective-permute-start.41 = (f32[256,256]{1,0:T(8,128)S(1)}, f32[256,256]{1,0:T(8,128)S(1)}, u32[]{:S(2)}, u32[]{:S(2)}) collective-permute-start(f32[256,256]{1,0:T(8,128)S(1)} %pad_maximum_fusion.1.refs_1_), channel_id=1, source_target_pairs={{0,10},{1,11},{2,8},{3,9},{16,26},{17,27},{18,24},{19,25}} | collective-permute-start | bytes 786440 | tf_op jit(solution)/shard_map/ppermute | solution.py:106
  65.4 35.9 %collective-permute-start.39 = (f32[256,256]{1,0:T(8,128)S(1)}, f32[256,256]{1,0:T(8,128)S(1)}, u32[]{:S(2)}, u32[]{:S(2)}) collective-permute-start(f32[256,256]{1,0:T(8,128)S(1)} %pad_maximum_fusion.1.refs_1_), channel_id=1, source_target_pairs={{16,10},{17,11},{18,8},{19,9}} | collective-permute-start | bytes 786440 | tf_op jit(solution)/shard_map/ppermute | solution.py:106
  66.7 34.6 %collective-permute-start.45 = (f32[256,256]{1,0:T(8,128)S(1)}, f32[256,256]{1,0:T(8,128)S(1)}, u32[]{:S(2)}, u32[]{:S(2)}) collective-permute-start(f32[256,256]{1,0:T(8,128)S(1)} %pad_maximum_fusion.1.refs_1_), channel_id=1, source_target_pairs={{0,8},{1,9},{2,10},{3,11},{16,24},{17,25},{18,26},{19,27}} | collective-permute-start | bytes 786440 | tf_op jit(solution)/shard_map/ppermute | solution.py:106
  68.0 37.8 %collective-permute-start.43 = (f32[256,256]{1,0:T(8,128)S(1)}, f32[256,256]{1,0:T(8,128)S(1)}, u32[]{:S(2)}, u32[]{:S(2)}) collective-permute-start(f32[256,256]{1,0:T(8,128)S(1)} %pad_maximum_fusion.1.refs_1_), channel_id=1, source_target_pairs={{16,8},{17,9},{18,10},{19,11}} | collective-permute-start | bytes 786440 | tf_op jit(solution)/shard_map/ppermute | solution.py:106
  97.8 8.0 %collective-permute-start.42 = (f32[256,256]{1,0:T(8,128)S(1)}, f32[256,256]{1,0:T(8,128)S(1)}, u32[]{:S(2)}, u32[]{:S(2)}) collective-permute-start(f32[256,256]{1,0:T(8,128)S(1)} %collective-permute-done.41.refs_6_), channel_id=1, source_target_pairs={{0,1},{1,0},{2,3},{3,2},{4,5},{5,4},{6,7},{7,6},{8,9},{9,8},{10,11... | collective-permute-start | bytes 786440 | tf_op jit(solution)/shard_map/ppermute | solution.py:106
  101.3 4.5 %collective-permute-start.40 = (f32[256,256]{1,0:T(8,128)S(1)}, f32[256,256]{1,0:T(8,128)S(1)}, u32[]{:S(2)}, u32[]{:S(2)}) collective-permute-start(f32[256,256]{1,0:T(8,128)S(1)} %collective-permute-done.39.refs_3_), channel_id=1, source_target_pairs={{0,1},{1,0},{2,3},{3,2},{4,5},{5,4},{6,7},{7,6},{8,9},{9,8},{10,11... | collective-permute-start | bytes 786440 | tf_op jit(solution)/shard_map/ppermute | solution.py:106
  101.3 5.2 %collective-permute-start.46 = (f32[256,256]{1,0:T(8,128)S(1)}, f32[256,256]{1,0:T(8,128)S(1)}, u32[]{:S(2)}, u32[]{:S(2)}) collective-permute-start(f32[256,256]{1,0:T(8,128)S(1)} %collective-permute-done.45.refs_5_), channel_id=1, source_target_pairs={{0,1},{1,0},{2,3},{3,2},{4,5},{5,4},{6,7},{7,6},{8,9},{9,8},{10,11... | collective-permute-start | bytes 786440 | tf_op jit(solution)/shard_map/ppermute | solution.py:106
  108.0 9.3 %collective-permute-start.49 = (f32[256,256]{1,0:T(8,128)S(1)}, f32[256,256]{1,0:T(8,128)S(1)}, u32[]{:S(2)}, u32[]{:S(2)}) collective-permute-start(f32[256,256]{1,0:T(8,128)S(1)} %shard_map.54.refs_1_), channel_id=1, source_target_pairs={{0,26},{1,27},{2,24},{3,25},{4,30},{5,31},{6,28},{7,29},{8,2},{9,3... | collective-permute-start | bytes 786440 | tf_op jit(solution)/shard_map/ppermute | solution.py:106
  108.0 9.2 %collective-permute-start.47 = (f32[256,256]{1,0:T(8,128)S(1)}, f32[256,256]{1,0:T(8,128)S(1)}, u32[]{:S(2)}, u32[]{:S(2)}) collective-permute-start(f32[256,256]{1,0:T(8,128)S(1)} %shard_map.54.refs_1_), channel_id=1, source_target_pairs={{0,4},{1,5},{2,6},{3,7},{4,0},{5,1},{6,2},{7,3},{8,12},{9,13},{10,... | collective-permute-start | bytes 786440 | tf_op jit(solution)/shard_map/ppermute | solution.py:106
  117.3 7.5 %collective-permute-start.50 = (f32[256,256]{1,0:T(8,128)S(1)}, f32[256,256]{1,0:T(8,128)S(1)}, u32[]{:S(2)}, u32[]{:S(2)}) collective-permute-start(f32[256,256]{1,0:T(8,128)S(1)} %collective-permute-done.49), channel_id=1, source_target_pairs={{0,4},{1,5},{2,6},{3,7},{4,0},{5,1},{6,2},{7,3},{8,12},{9,13},{10,... | collective-permute-start | bytes 786440 | tf_op jit(solution)/shard_map/ppermute | solution.py:106
  117.3 7.5 %collective-permute-start.54 = (f32[256,256]{1,0:T(8,128)S(1)}, f32[256,256]{1,0:T(8,128)S(1)}, u32[]{:S(2)}, u32[]{:S(2)}) collective-permute-start(f32[256,256]{1,0:T(8,128)S(1)} %collective-permute-done.47.refs_3_), channel_id=1, source_target_pairs={{0,24},{1,25},{2,26},{3,27},{4,28},{5,29},{6,30},{7,31},{8,0},{9,1... | collective-permute-start | bytes 786440 | tf_op jit(solution)/shard_map/ppermute | solution.py:106
  117.4 7.8 %collective-permute-start.52 = (f32[256,256]{1,0:T(8,128)S(1)}, f32[256,256]{1,0:T(8,128)S(1)}, u32[]{:S(2)}, u32[]{:S(2)}) collective-permute-start(f32[256,256]{1,0:T(8,128)S(1)} %collective-permute-done.47.refs_3_), channel_id=1, source_target_pairs={{0,2},{1,3},{2,0},{3,1},{4,6},{5,7},{6,4},{7,5},{8,10},{9,11},{10,... | collective-permute-start | bytes 786440 | tf_op jit(solution)/shard_map/ppermute | solution.py:106
  118.7 6.7 %collective-permute-start.48 = (f32[256,256]{1,0:T(8,128)S(1)}, f32[256,256]{1,0:T(8,128)S(1)}, u32[]{:S(2)}, u32[]{:S(2)}) collective-permute-start(f32[256,256]{1,0:T(8,128)S(1)} %collective-permute-done.47.refs_3_), channel_id=1, source_target_pairs={{0,1},{1,0},{2,3},{3,2},{4,5},{5,4},{6,7},{7,6},{8,9},{9,8},{10,11... | collective-permute-start | bytes 786440 | tf_op jit(solution)/shard_map/ppermute | solution.py:106
  124.8 2.2 %collective-permute-start.55 = (f32[256,256]{1,0:T(8,128)S(1)}, f32[256,256]{1,0:T(8,128)S(1)}, u32[]{:S(2)}, u32[]{:S(2)}) collective-permute-start(f32[256,256]{1,0:T(8,128)S(1)} %collective-permute-done.54.refs_5_), channel_id=1, source_target_pairs={{0,1},{1,0},{2,3},{3,2},{4,5},{5,4},{6,7},{7,6},{8,9},{9,8},{10,11... | collective-permute-start | bytes 786440 | tf_op jit(solution)/shard_map/ppermute | solution.py:106
  125.3 1.8 %collective-permute-start.53 = (f32[256,256]{1,0:T(8,128)S(1)}, f32[256,256]{1,0:T(8,128)S(1)}, u32[]{:S(2)}, u32[]{:S(2)}) collective-permute-start(f32[256,256]{1,0:T(8,128)S(1)} %collective-permute-done.52.refs_2_), channel_id=1, source_target_pairs={{0,1},{1,0},{2,3},{3,2},{4,5},{5,4},{6,7},{7,6},{8,9},{9,8},{10,11... | collective-permute-start | bytes 786440 | tf_op jit(solution)/shard_map/ppermute | solution.py:106
  (11 other events, 28.9 us)

commit v8 on v7

--- a/solution.py
+++ b/solution.py
@@ -189,7 +189,7 @@
         only = (2 * stride, stride)
         senders = range(0, layers, 2 * stride)
         if k > 0:
-            lower = swapped(direct(result, [(j, j + stride) for j in senders]))
+            lower = swapped(traded(result, [(j, j + stride) for j in senders]))
             upper = swapped(direct(result, [(j, j - stride) for j in senders]))
             result = apply([base, result], -1, (east, upper), (west, lower), only=only, far_first=True)
         else:

time: 130 us -> 129 us (level)
  waiting for transfers between devices: 81.7 us -> 59.7 us
  starting transfers between devices: 29.8 us -> 50.6 us
    ppermute x52 -> x50, waiting for transfers between devices: 66.7 us -> 39.3 us  [move(): return lax.ppermute(block, AXES, hops) if hops else None]
    ppermute x4 -> x6, starting transfers between devices: 4.05 us -> 27.4 us  [traded(): out.append((flip, lax.ppermute(block, AXES, hops)))]
    ppermute x4 -> x6, waiting for transfers between devices: 15 us -> 20.5 us  [traded(): out.append((flip, lax.ppermute(block, AXES, hops)))]
    ppermute x52 -> x50, starting transfers between devices: 25.8 us -> 23.2 us  [move(): return lax.ppermute(block, AXES, hops) if hops else None]
where the time goes in v8:
time: 129 us; the launch traced here: 127 us
  waiting for transfers between devices  59.7 us (46%)
  starting transfers between devices  50.6 us (39%)
  Pallas kernels  11.7 us (9%)
  local copies, waits for them, and re-layouts  4.7 us (4%)
    ppermute x50, waiting for transfers between devices, move(): return lax.ppermute(block, AXES, hops) if hops else None  39.3 us
    ppermute x6, starting transfers between devices, traded(): out.append((flip, lax.ppermute(block, AXES, hops)))  27.4 us
    ppermute x50, starting transfers between devices, move(): return lax.ppermute(block, AXES, hops) if hops else None  23.2 us
    ppermute x6, waiting for transfers between devices, traded(): out.append((flip, lax.ppermute(block, AXES, hops)))  20.5 us
    pallas_call x19, Pallas kernels, combine(): pl.pallas_call(functools.partial(combine_kernel, shape, sign, only), out_...  9.97 us
    unnamed x6, local copies, waits for them, and re-layouts  4.68 us
  transfers between devices with their start and end apart: 56, of which 22 were waited for; matrix products, arithmetic and copies ran while one was open for 0% of the time, Pallas kernels for 6%

profile of v8, /device:TPU:8, one launch (start us, length us, event | category | flops | bytes accessed | tf_op | source)
XLA Modules:
  0.0 127.2 jit_solution(17342328971237257460)
XLA Ops:
  0.0 1.5 %collective-permute-start = (f32[256,256]{1,0:T(8,128)}, f32[256,256]{1,0:T(8,128)S(1)}, u32[]{:S(2)}, u32[]{:S(2)}) collective-permute-start(f32[256,256]{1,0:T(8,128)} %bitcast.6), channel_id=1, source_target_pairs={{0,4},{1,5},{2,6},{3,7},{4,0},{5,1},{6,2},{7,3},{8,12},{9,13},{10,... | collective-permute-start | bytes 786440 | tf_op jit(solution)/shard_map/ppermute | solution.py:106
  1.5 2.5 %collective-permute-start.6 = (f32[256,256]{1,0:T(8,128)}, f32[256,256]{1,0:T(8,128)S(1)}, u32[]{:S(2)}, u32[]{:S(2)}) collective-permute-start(f32[256,256]{1,0:T(8,128)} %bitcast.7), channel_id=1, source_target_pairs={{0,10},{1,11},{2,8},{3,9},{4,14},{5,15},{6,12},{7,13},{8,18},{9,19... | collective-permute-start | bytes 786440 | tf_op jit(solution)/shard_map/ppermute | solution.py:106
  4.0 2.8 %copy-done = f32[3,1,2,256,1024]{4,3,2,1,0:T(8,128)S(1)} copy-done((f32[3,1,2,256,1024]{4,3,2,1,0:T(8,128)S(1)}, f32[3,1,2,256,1024]{4,3,2,1,0:T(8,128)}, u32[]{:S(2)}) %copy-start) | copy-done | bytes 6291480
  6.8 1.9 %copy-done.1 = f32[1,3,256,1024]{3,2,1,0:T(8,128)S(1)} copy-done((f32[1,3,256,1024]{3,2,1,0:T(8,128)S(1)}, f32[1,3,256,1024]{3,2,1,0:T(8,128)}, u32[]{:S(2)}) %copy-start.1) | copy-done | bytes 3145752
  8.7 1.7 %shard_map.37 = (f32[256,1024]{1,0:T(8,128)S(1)}, f32[256,1024]{1,0:T(8,128)S(1)}, f32[256,1024]{1,0:T(8,128)S(1)}, f32[256,1024]{1,0:T(8,128)S(1)}, f32[256,102...) custom-call(f32[3,2,256,1024]{3,2,1,0:T(8,128)S(1)} %bitcast.4, ...), custom_call_target="tpu_custom_call" | custom-call | tf_op jit(solution)/shard_map/pallas_call | solution.py:87
  10.5 0.6 collective-permute-start.7
  11.1 1.6 %collective-permute-start.4 = (f32[256,256]{1,0:T(8,128)S(1)}, f32[256,256]{1,0:T(8,128)S(1)}, u32[]{:S(2)}, u32[]{:S(2)}) collective-permute-start(f32[256,256]{1,0:T(8,128)S(1)} %collective-permute-done.refs_2_), channel_id=1, source_target_pairs={{0,8},{1,9},{2,10},{3,11},{4,12},{5,13},{6,14},{7,15},{8,16},{9,17... | collective-permute-start | bytes 786440 | tf_op jit(solution)/shard_map/ppermute | solution.py:106
  12.6 1.4 %collective-permute-start.2 = (f32[256,256]{1,0:T(8,128)S(1)}, f32[256,256]{1,0:T(8,128)S(1)}, u32[]{:S(2)}, u32[]{:S(2)}) collective-permute-start(f32[256,256]{1,0:T(8,128)S(1)} %collective-permute-done.refs_2_), channel_id=1, source_target_pairs={{0,2},{1,3},{2,0},{3,1},{4,6},{5,7},{6,4},{7,5},{8,10},{9,11},{10,... | collective-permute-start | bytes 786440 | tf_op jit(solution)/shard_map/ppermute | solution.py:106
  14.0 4.0 %collective-permute-done.7.refs_9_ = f32[256,256]{1,0:T(8,128)S(1)} collective-permute-done((f32[256,256]{1,0:T(8,128)S(1)}, f32[256,256]{1,0:T(8,128)S(1)}, u32[]{:S(2)}, u32[]{:S(2)}) %collective-permute-start.7) | collective-permute-done | bytes 262176 | tf_op jit(solution)/shard_map/ppermute | solution.py:106
  18.5 1.0 collective-permute-done.2.refs_4_
  20.0 1.1 collective-permute-done.3.refs_5_
  21.1 1.1 shard_map.38.refs_0_
  22.2 1.9 %collective-permute-start.11 = (f32[256,256]{1,0:T(8,128)S(1)}, f32[256,256]{1,0:T(8,128)S(1)}, u32[]{:S(2)}, u32[]{:S(2)}) collective-permute-start(f32[256,256]{1,0:T(8,128)S(1)} %shard_map.38.refs_0_), channel_id=1, source_target_pairs={{0,1},{1,0},{2,3},{3,2},{4,5},{5,4},{6,7},{7,6},{8,18},{9,19},{10,... | collective-permute-start | bytes 786440 | tf_op jit(solution)/shard_map/ppermute | solution.py:125
  24.1 1.6 %collective-permute-start.9 = (f32[256,256]{1,0:T(8,128)S(1)}, f32[256,256]{1,0:T(8,128)S(1)}, u32[]{:S(2)}, u32[]{:S(2)}) collective-permute-start(f32[256,256]{1,0:T(8,128)S(1)} %shard_map.38.refs_0_), channel_id=1, source_target_pairs={{0,10},{1,11},{2,8},{3,9},{4,5},{5,4},{6,7},{7,6},{8,2},{9,3},{10,... | collective-permute-start | bytes 786440 | tf_op jit(solution)/shard_map/ppermute | solution.py:125
  26.2 9.3 %collective-permute-done.11.refs_5_ = f32[256,256]{1,0:T(8,128)S(1)} collective-permute-done((f32[256,256]{1,0:T(8,128)S(1)}, f32[256,256]{1,0:T(8,128)S(1)}, u32[]{:S(2)}, u32[]{:S(2)}) %collective-permute-start.11) | collective-permute-done | bytes 262176 | tf_op jit(solution)/shard_map/ppermute | solution.py:125
  35.6 2.1 %collective-permute-done.9.refs_2_ = f32[256,256]{1,0:T(8,128)S(1)} collective-permute-done((f32[256,256]{1,0:T(8,128)S(1)}, f32[256,256]{1,0:T(8,128)S(1)}, u32[]{:S(2)}, u32[]{:S(2)}) %collective-permute-start.9) | collective-permute-done | bytes 262176 | tf_op jit(solution)/shard_map/ppermute | solution.py:125
  37.6 1.4 %collective-permute-done.15.refs_5_ = f32[256,256]{1,0:T(8,128)S(1)} collective-permute-done((f32[256,256]{1,0:T(8,128)S(1)}, f32[256,256]{1,0:T(8,128)S(1)}, u32[]{:S(2)}, u32[]{:S(2)}) %collective-permute-start.15) | collective-permute-done | bytes 262176 | tf_op jit(solution)/shard_map/ppermute | solution.py:125
  39.0 2.2 %collective-permute-done.13.refs_2_ = f32[256,256]{1,0:T(8,128)S(1)} collective-permute-done((f32[256,256]{1,0:T(8,128)S(1)}, f32[256,256]{1,0:T(8,128)S(1)}, u32[]{:S(2)}, u32[]{:S(2)}) %collective-permute-start.13) | collective-permute-done | bytes 262176 | tf_op jit(solution)/shard_map/ppermute | solution.py:125
  41.2 0.6 shard_map.39.refs_0_
  41.9 0.9 collective-permute-done.14.refs_3_
  42.7 0.6 shard_map.40
  43.4 0.7 collective-permute-start.17
  44.1 0.7 collective-permute-start.19
  44.8 0.7 collective-permute-start.24
  45.4 0.7 collective-permute-start.26
  48.3 1.6 %collective-permute-start.22 = (f32[256,128]{1,0:T(8,128)S(1)}, f32[256,128]{1,0:T(8,128)S(1)}, u32[]{:S(2)}, u32[]{:S(2)}) collective-permute-start(f32[256,128]{1,0:T(8,128)S(1)} %shard_map.42.refs_1_), channel_id=1, source_target_pairs={{0,2},{1,3},{2,0},{3,1},{4,6},{5,7},{6,4},{7,5},{8,10},{9,11},{10,... | collective-permute-start | bytes 393224 | tf_op jit(solution)/shard_map/ppermute | solution.py:106
  51.7 2.9 %collective-permute-done.22.refs_2_ = f32[256,128]{1,0:T(8,128)S(1)} collective-permute-done((f32[256,128]{1,0:T(8,128)S(1)}, f32[256,128]{1,0:T(8,128)S(1)}, u32[]{:S(2)}, u32[]{:S(2)}) %collective-permute-start.22) | collective-permute-done | bytes 131104 | tf_op jit(solution)/shard_map/ppermute | solution.py:106
  54.6 2.1 %collective-permute-done.29.refs_2_ = f32[256,128]{1,0:T(8,128)S(1)} collective-permute-done((f32[256,128]{1,0:T(8,128)S(1)}, f32[256,128]{1,0:T(8,128)S(1)}, u32[]{:S(2)}, u32[]{:S(2)}) %collective-permute-start.29) | collective-permute-done | bytes 131104 | tf_op jit(solution)/shard_map/ppermute | solution.py:106
  57.9 0.7 collective-permute-start.31
  58.9 0.7 collective-permute-start.35
  59.6 0.7 collective-permute-start.33
  60.3 0.7 collective-permute-start.37
  61.0 0.6 collective-permute-start.32
  64.1 23.3 %collective-permute-start.41 = (f32[256,256]{1,0:T(8,128)S(1)}, f32[256,256]{1,0:T(8,128)S(1)}, u32[]{:S(2)}, u32[]{:S(2)}) collective-permute-start(f32[256,256]{1,0:T(8,128)S(1)} %pad_maximum_fusion.1.refs_1_), channel_id=1, source_target_pairs={{0,10},{1,11},{2,8},{3,9},{4,5},{5,4},{6,7},{7,6},{8,2},{9,3},{10,... | collective-permute-start | bytes 786440 | tf_op jit(solution)/shard_map/ppermute | solution.py:125
  87.4 1.3 %collective-permute-start.39 = (f32[256,256]{1,0:T(8,128)S(1)}, f32[256,256]{1,0:T(8,128)S(1)}, u32[]{:S(2)}, u32[]{:S(2)}) collective-permute-start(f32[256,256]{1,0:T(8,128)S(1)} %pad_maximum_fusion.1.refs_1_), channel_id=1, source_target_pairs={{16,10},{17,11},{18,8},{19,9}} | collective-permute-start | bytes 786440 | tf_op jit(solution)/shard_map/ppermute | solution.py:106
  88.7 1.3 %collective-permute-start.43 = (f32[256,256]{1,0:T(8,128)S(1)}, f32[256,256]{1,0:T(8,128)S(1)}, u32[]{:S(2)}, u32[]{:S(2)}) collective-permute-start(f32[256,256]{1,0:T(8,128)S(1)} %pad_maximum_fusion.1.refs_1_), channel_id=1, source_target_pairs={{16,8},{17,9},{18,10},{19,11}} | collective-permute-start | bytes 786440 | tf_op jit(solution)/shard_map/ppermute | solution.py:106
  90.0 5.5 %collective-permute-done.41.refs_6_ = f32[256,256]{1,0:T(8,128)S(1)} collective-permute-done((f32[256,256]{1,0:T(8,128)S(1)}, f32[256,256]{1,0:T(8,128)S(1)}, u32[]{:S(2)}, u32[]{:S(2)}) %collective-permute-start.41) | collective-permute-done | bytes 262176 | tf_op jit(solution)/shard_map/ppermute | solution.py:125
  95.6 5.1 %collective-permute-done.39.refs_3_ = f32[256,256]{1,0:T(8,128)S(1)} collective-permute-done((f32[256,256]{1,0:T(8,128)S(1)}, f32[256,256]{1,0:T(8,128)S(1)}, u32[]{:S(2)}, u32[]{:S(2)}) %collective-permute-start.39) | collective-permute-done | bytes 262176 | tf_op jit(solution)/shard_map/ppermute | solution.py:106
  101.2 3.4 %collective-permute-done.43.refs_2_ = f32[256,256]{1,0:T(8,128)S(1)} collective-permute-done((f32[256,256]{1,0:T(8,128)S(1)}, f32[256,256]{1,0:T(8,128)S(1)}, u32[]{:S(2)}, u32[]{:S(2)}) %collective-permute-start.43) | collective-permute-done | bytes 262176 | tf_op jit(solution)/shard_map/ppermute | solution.py:106
  104.6 0.7 shard_map.53.refs_0_
  105.3 0.8 collective-permute-done.44.refs_3_
  106.1 0.7 shard_map.54.refs_1_
  106.9 9.1 %collective-permute-done.49 = f32[256,256]{1,0:T(8,128)S(1)} collective-permute-done((f32[256,256]{1,0:T(8,128)S(1)}, f32[256,256]{1,0:T(8,128)S(1)}, u32[]{:S(2)}, u32[]{:S(2)}) %collective-permute-start.49) | collective-permute-done | bytes 262176 | tf_op jit(solution)/shard_map/ppermute | solution.py:106
  116.2 1.2 collective-permute-start.52
  117.5 6.1 %collective-permute-done.50.refs_6_ = f32[256,256]{1,0:T(8,128)S(1)} collective-permute-done((f32[256,256]{1,0:T(8,128)S(1)}, f32[256,256]{1,0:T(8,128)S(1)}, u32[]{:S(2)}, u32[]{:S(2)}) %collective-permute-start.50) | collective-permute-done | bytes 262176 | tf_op jit(solution)/shard_map/ppermute | solution.py:106
  124.2 0.9 collective-permute-done.51.refs_7_
  125.1 0.6 shard_map.55.refs_0_
  125.9 1.3 %shard_map.56 = f32[256,256]{1,0:T(8,128)} custom-call(f32[256,256]{1,0:T(8,128)S(1)} %shard_map.55.refs_0_, f32[256,1024]{1,0:T(8,128)S(1)} %get-tuple-element.37.refs_1_.refs_5_.refs_4_.refs_2_, f32[256,256]{1,0:T(8,128)S(1)} %collective-permute-done.52.refs_2_, f32[256,256]{1,0:T(8,128)S(1)} %collective-permute-done.53.refs_3_, ...), custom_call_target="tpu_custom_call" | custom-call | flops 402653184 | tf_op jit(solution)/shard_map/pallas_call | solution.py:62
  (93 shorter events, 11.1 us)
Async XLA Ops:
  0.0 10.4 %collective-permute-start = (f32[256,256]{1,0:T(8,128)}, f32[256,256]{1,0:T(8,128)S(1)}, u32[]{:S(2)}, u32[]{:S(2)}) collective-permute-start(f32[256,256]{1,0:T(8,128)} %bitcast.6), channel_id=1, source_target_pairs={{0,4},{1,5},{2,6},{3,7},{4,0},{5,1},{6,2},{7,3},{8,12},{9,13},{10,... | collective-permute-start | bytes 786440 | tf_op jit(solution)/shard_map/ppermute | solution.py:106
  1.5 9.0 %collective-permute-start.6 = (f32[256,256]{1,0:T(8,128)}, f32[256,256]{1,0:T(8,128)S(1)}, u32[]{:S(2)}, u32[]{:S(2)}) collective-permute-start(f32[256,256]{1,0:T(8,128)} %bitcast.7), channel_id=1, source_target_pairs={{0,10},{1,11},{2,8},{3,9},{4,14},{5,15},{6,12},{7,13},{8,18},{9,19... | collective-permute-start | bytes 786440 | tf_op jit(solution)/shard_map/ppermute | solution.py:106
  10.5 7.6 %collective-permute-start.7 = (f32[256,256]{1,0:T(8,128)S(1)}, f32[256,256]{1,0:T(8,128)S(1)}, u32[]{:S(2)}, u32[]{:S(2)}) collective-permute-start(f32[256,256]{1,0:T(8,128)S(1)} %collective-permute-done.6), channel_id=1, source_target_pairs={{0,4},{1,5},{2,6},{3,7},{4,0},{5,1},{6,2},{7,3},{8,12},{9,13},{10,... | collective-permute-start | bytes 786440 | tf_op jit(solution)/shard_map/ppermute | solution.py:106
  11.1 7.4 %collective-permute-start.4 = (f32[256,256]{1,0:T(8,128)S(1)}, f32[256,256]{1,0:T(8,128)S(1)}, u32[]{:S(2)}, u32[]{:S(2)}) collective-permute-start(f32[256,256]{1,0:T(8,128)S(1)} %collective-permute-done.refs_2_), channel_id=1, source_target_pairs={{0,8},{1,9},{2,10},{3,11},{4,12},{5,13},{6,14},{7,15},{8,16},{9,17... | collective-permute-start | bytes 786440 | tf_op jit(solution)/shard_map/ppermute | solution.py:106
  12.6 6.9 %collective-permute-start.2 = (f32[256,256]{1,0:T(8,128)S(1)}, f32[256,256]{1,0:T(8,128)S(1)}, u32[]{:S(2)}, u32[]{:S(2)}) collective-permute-start(f32[256,256]{1,0:T(8,128)S(1)} %collective-permute-done.refs_2_), channel_id=1, source_target_pairs={{0,2},{1,3},{2,0},{3,1},{4,6},{5,7},{6,4},{7,5},{8,10},{9,11},{10,... | collective-permute-start | bytes 786440 | tf_op jit(solution)/shard_map/ppermute | solution.py:106
  14.0 5.6 %collective-permute-start.1 = (f32[256,256]{1,0:T(8,128)S(1)}, f32[256,256]{1,0:T(8,128)S(1)}, u32[]{:S(2)}, u32[]{:S(2)}) collective-permute-start(f32[256,256]{1,0:T(8,128)S(1)} %collective-permute-done.refs_2_), channel_id=1, source_target_pairs={{0,1},{1,0},{2,3},{3,2},{4,5},{5,4},{6,7},{7,6},{8,9},{9,8},{10,11... | collective-permute-start | bytes 786440 | tf_op jit(solution)/shard_map/ppermute | solution.py:106
  18.0 1.6 %collective-permute-start.8 = (f32[256,256]{1,0:T(8,128)S(1)}, f32[256,256]{1,0:T(8,128)S(1)}, u32[]{:S(2)}, u32[]{:S(2)}) collective-permute-start(f32[256,256]{1,0:T(8,128)S(1)} %collective-permute-done.7.refs_9_), channel_id=1, source_target_pairs={{0,1},{1,0},{2,3},{3,2},{4,5},{5,4},{6,7},{7,6},{8,9},{9,8},{10,11... | collective-permute-start | bytes 786440 | tf_op jit(solution)/shard_map/ppermute | solution.py:106
  22.2 13.4 %collective-permute-start.11 = (f32[256,256]{1,0:T(8,128)S(1)}, f32[256,256]{1,0:T(8,128)S(1)}, u32[]{:S(2)}, u32[]{:S(2)}) collective-permute-start(f32[256,256]{1,0:T(8,128)S(1)} %shard_map.38.refs_0_), channel_id=1, source_target_pairs={{0,1},{1,0},{2,3},{3,2},{4,5},{5,4},{6,7},{7,6},{8,18},{9,19},{10,... | collective-permute-start | bytes 786440 | tf_op jit(solution)/shard_map/ppermute | solution.py:125
  24.1 13.6 %collective-permute-start.9 = (f32[256,256]{1,0:T(8,128)S(1)}, f32[256,256]{1,0:T(8,128)S(1)}, u32[]{:S(2)}, u32[]{:S(2)}) collective-permute-start(f32[256,256]{1,0:T(8,128)S(1)} %shard_map.38.refs_0_), channel_id=1, source_target_pairs={{0,10},{1,11},{2,8},{3,9},{4,5},{5,4},{6,7},{7,6},{8,2},{9,3},{10,... | collective-permute-start | bytes 786440 | tf_op jit(solution)/shard_map/ppermute | solution.py:125
  25.7 13.3 %collective-permute-start.15 = (f32[256,256]{1,0:T(8,128)S(1)}, f32[256,256]{1,0:T(8,128)S(1)}, u32[]{:S(2)}, u32[]{:S(2)}) collective-permute-start(f32[256,256]{1,0:T(8,128)S(1)} %shard_map.38.refs_0_), channel_id=1, source_target_pairs={{0,1},{1,0},{2,3},{3,2},{4,5},{5,4},{6,7},{7,6},{8,16},{9,17},{10,... | collective-permute-start | bytes 786440 | tf_op jit(solution)/shard_map/ppermute | solution.py:125
  26.2 15.0 %collective-permute-start.13 = (f32[256,256]{1,0:T(8,128)S(1)}, f32[256,256]{1,0:T(8,128)S(1)}, u32[]{:S(2)}, u32[]{:S(2)}) collective-permute-start(f32[256,256]{1,0:T(8,128)S(1)} %shard_map.38.refs_0_), channel_id=1, source_target_pairs={{0,8},{1,9},{2,10},{3,11},{4,5},{5,4},{6,7},{7,6},{8,0},{9,1},{10,... | collective-permute-start | bytes 786440 | tf_op jit(solution)/shard_map/ppermute | solution.py:125
  35.6 5.7 %collective-permute-start.12 = (f32[256,256]{1,0:T(8,128)S(1)}, f32[256,256]{1,0:T(8,128)S(1)}, u32[]{:S(2)}, u32[]{:S(2)}) collective-permute-start(f32[256,256]{1,0:T(8,128)S(1)} %collective-permute-done.11.refs_5_), channel_id=1, source_target_pairs={{0,1},{1,0},{2,3},{3,2},{4,5},{5,4},{6,7},{7,6},{8,9},{9,8},{10,11... | collective-permute-start | bytes 786440 | tf_op jit(solution)/shard_map/ppermute | solution.py:106
  37.6 3.6 %collective-permute-start.10 = (f32[256,256]{1,0:T(8,128)S(1)}, f32[256,256]{1,0:T(8,128)S(1)}, u32[]{:S(2)}, u32[]{:S(2)}) collective-permute-start(f32[256,256]{1,0:T(8,128)S(1)} %collective-permute-done.9.refs_2_), channel_id=1, source_target_pairs={{0,1},{1,0},{2,3},{3,2},{4,5},{5,4},{6,7},{7,6},{8,9},{9,8},{10,11... | collective-permute-start | bytes 786440 | tf_op jit(solution)/shard_map/ppermute | solution.py:106
  39.0 2.9 %collective-permute-start.16 = (f32[256,256]{1,0:T(8,128)S(1)}, f32[256,256]{1,0:T(8,128)S(1)}, u32[]{:S(2)}, u32[]{:S(2)}) collective-permute-start(f32[256,256]{1,0:T(8,128)S(1)} %collective-permute-done.15.refs_5_), channel_id=1, source_target_pairs={{0,1},{1,0},{2,3},{3,2},{4,5},{5,4},{6,7},{7,6},{8,9},{9,8},{10,11... | collective-permute-start | bytes 786440 | tf_op jit(solution)/shard_map/ppermute | solution.py:106
  43.4 2.7 %collective-permute-start.17 = (f32[256,128]{1,0:T(8,128)S(1)}, f32[256,128]{1,0:T(8,128)S(1)}, u32[]{:S(2)}, u32[]{:S(2)}) collective-permute-start(f32[256,128]{1,0:T(8,128)S(1)} %get-tuple-element.39.refs_0_), channel_id=1, source_target_pairs={{16,2},{17,3},{18,0},{19,1}} | collective-permute-start | bytes 393224 | tf_op jit(solution)/shard_map/ppermute | solution.py:106
  44.1 2.2 %collective-permute-start.19 = (f32[256,128]{1,0:T(8,128)S(1)}, f32[256,128]{1,0:T(8,128)S(1)}, u32[]{:S(2)}, u32[]{:S(2)}) collective-permute-start(f32[256,128]{1,0:T(8,128)S(1)} %get-tuple-element.39.refs_0_), channel_id=1, source_target_pairs={{16,0},{17,1},{18,2},{19,3}} | collective-permute-start | bytes 393224 | tf_op jit(solution)/shard_map/ppermute | solution.py:106
  44.8 1.9 %collective-permute-start.24 = (f32[256,128]{1,0:T(8,128)S(1)}, f32[256,128]{1,0:T(8,128)S(1)}, u32[]{:S(2)}, u32[]{:S(2)}) collective-permute-start(f32[256,128]{1,0:T(8,128)S(1)} %get-tuple-element.40.refs_0_), channel_id=1, source_target_pairs={{16,2},{17,3},{18,0},{19,1}} | collective-permute-start | bytes 393224 | tf_op jit(solution)/shard_map/ppermute | solution.py:106
  46.3 1.6 %collective-permute-start.20 = (f32[256,128]{1,0:T(8,128)S(1)}, f32[256,128]{1,0:T(8,128)S(1)}, u32[]{:S(2)}, u32[]{:S(2)}) collective-permute-start(f32[256,128]{1,0:T(8,128)S(1)} %collective-permute-done.19.refs_2_), channel_id=1, source_target_pairs={{0,1},{1,0},{2,3},{3,2},{4,5},{5,4},{6,7},{7,6},{8,9},{9,8},{10,11... | collective-permute-start | bytes 393224 | tf_op jit(solution)/shard_map/ppermute | solution.py:106
  46.7 3.2 %collective-permute-start.25 = (f32[256,128]{1,0:T(8,128)S(1)}, f32[256,128]{1,0:T(8,128)S(1)}, u32[]{:S(2)}, u32[]{:S(2)}) collective-permute-start(f32[256,128]{1,0:T(8,128)S(1)} %collective-permute-done.24.refs_2_), channel_id=1, source_target_pairs={{0,1},{1,0},{2,3},{3,2},{4,5},{5,4},{6,7},{7,6},{8,9},{9,8},{10,11... | collective-permute-start | bytes 393224 | tf_op jit(solution)/shard_map/ppermute | solution.py:106
  46.8 3.4 %collective-permute-start.27 = (f32[256,128]{1,0:T(8,128)S(1)}, f32[256,128]{1,0:T(8,128)S(1)}, u32[]{:S(2)}, u32[]{:S(2)}) collective-permute-start(f32[256,128]{1,0:T(8,128)S(1)} %collective-permute-done.26.refs_2_), channel_id=1, source_target_pairs={{0,1},{1,0},{2,3},{3,2},{4,5},{5,4},{6,7},{7,6},{8,9},{9,8},{10,11... | collective-permute-start | bytes 393224 | tf_op jit(solution)/shard_map/ppermute | solution.py:106
  48.3 6.3 %collective-permute-start.22 = (f32[256,128]{1,0:T(8,128)S(1)}, f32[256,128]{1,0:T(8,128)S(1)}, u32[]{:S(2)}, u32[]{:S(2)}) collective-permute-start(f32[256,128]{1,0:T(8,128)S(1)} %shard_map.42.refs_1_), channel_id=1, source_target_pairs={{0,2},{1,3},{2,0},{3,1},{4,6},{5,7},{6,4},{7,5},{8,10},{9,11},{10,... | collective-permute-start | bytes 393224 | tf_op jit(solution)/shard_map/ppermute | solution.py:106
  50.6 6.1 %collective-permute-start.29 = (f32[256,128]{1,0:T(8,128)S(1)}, f32[256,128]{1,0:T(8,128)S(1)}, u32[]{:S(2)}, u32[]{:S(2)}) collective-permute-start(f32[256,128]{1,0:T(8,128)S(1)} %shard_map.46.refs_1_), channel_id=1, source_target_pairs={{0,2},{1,3},{2,0},{3,1},{4,6},{5,7},{6,4},{7,5},{8,10},{9,11},{10,... | collective-permute-start | bytes 393224 | tf_op jit(solution)/shard_map/ppermute | solution.py:106
  51.2 5.5 %collective-permute-start.21 = (f32[256,128]{1,0:T(8,128)S(1)}, f32[256,128]{1,0:T(8,128)S(1)}, u32[]{:S(2)}, u32[]{:S(2)}) collective-permute-start(f32[256,128]{1,0:T(8,128)S(1)} %shard_map.42.refs_1_), channel_id=1, source_target_pairs={{0,1},{1,0},{2,3},{3,2},{4,5},{5,4},{6,7},{7,6},{8,9},{9,8},{10,11... | collective-permute-start | bytes 393224 | tf_op jit(solution)/shard_map/ppermute | solution.py:106
  51.2 5.9 %collective-permute-start.28 = (f32[256,128]{1,0:T(8,128)S(1)}, f32[256,128]{1,0:T(8,128)S(1)}, u32[]{:S(2)}, u32[]{:S(2)}) collective-permute-start(f32[256,128]{1,0:T(8,128)S(1)} %shard_map.46.refs_1_), channel_id=1, source_target_pairs={{0,1},{1,0},{2,3},{3,2},{4,5},{5,4},{6,7},{7,6},{8,9},{9,8},{10,11... | collective-permute-start | bytes 393224 | tf_op jit(solution)/shard_map/ppermute | solution.py:106
  54.6 2.9 %collective-permute-start.23 = (f32[256,128]{1,0:T(8,128)S(1)}, f32[256,128]{1,0:T(8,128)S(1)}, u32[]{:S(2)}, u32[]{:S(2)}) collective-permute-start(f32[256,128]{1,0:T(8,128)S(1)} %collective-permute-done.22.refs_2_), channel_id=1, source_target_pairs={{0,1},{1,0},{2,3},{3,2},{4,5},{5,4},{6,7},{7,6},{8,9},{9,8},{10,11... | collective-permute-start | bytes 393224 | tf_op jit(solution)/shard_map/ppermute | solution.py:106
  56.7 1.8 %collective-permute-start.30 = (f32[256,128]{1,0:T(8,128)S(1)}, f32[256,128]{1,0:T(8,128)S(1)}, u32[]{:S(2)}, u32[]{:S(2)}) collective-permute-start(f32[256,128]{1,0:T(8,128)S(1)} %collective-permute-done.29.refs_2_), channel_id=1, source_target_pairs={{0,1},{1,0},{2,3},{3,2},{4,5},{5,4},{6,7},{7,6},{8,9},{9,8},{10,11... | collective-permute-start | bytes 393224 | tf_op jit(solution)/shard_map/ppermute | solution.py:106
  57.9 3.1 %collective-permute-start.31 = (f32[256,128]{1,0:T(8,128)S(1)}, f32[256,128]{1,0:T(8,128)S(1)}, u32[]{:S(2)}, u32[]{:S(2)}) collective-permute-start(f32[256,128]{1,0:T(8,128)S(1)} %shard_map.44.refs_0_), channel_id=1, source_target_pairs={{0,18},{1,19},{2,16},{3,17}} | collective-permute-start | bytes 393224 | tf_op jit(solution)/shard_map/ppermute | solution.py:106
  58.9 2.6 %collective-permute-start.35 = (f32[256,128]{1,0:T(8,128)S(1)}, f32[256,128]{1,0:T(8,128)S(1)}, u32[]{:S(2)}, u32[]{:S(2)}) collective-permute-start(f32[256,128]{1,0:T(8,128)S(1)} %shard_map.48.refs_0_), channel_id=1, source_target_pairs={{0,18},{1,19},{2,16},{3,17}} | collective-permute-start | bytes 393224 | tf_op jit(solution)/shard_map/ppermute | solution.py:106
  59.6 2.1 %collective-permute-start.33 = (f32[256,128]{1,0:T(8,128)S(1)}, f32[256,128]{1,0:T(8,128)S(1)}, u32[]{:S(2)}, u32[]{:S(2)}) collective-permute-start(f32[256,128]{1,0:T(8,128)S(1)} %shard_map.44.refs_0_), channel_id=1, source_target_pairs={{0,16},{1,17},{2,18},{3,19}} | collective-permute-start | bytes 393224 | tf_op jit(solution)/shard_map/ppermute | solution.py:106
  60.3 1.8 %collective-permute-start.37 = (f32[256,128]{1,0:T(8,128)S(1)}, f32[256,128]{1,0:T(8,128)S(1)}, u32[]{:S(2)}, u32[]{:S(2)}) collective-permute-start(f32[256,128]{1,0:T(8,128)S(1)} %shard_map.48.refs_0_), channel_id=1, source_target_pairs={{0,16},{1,17},{2,18},{3,19}} | collective-permute-start | bytes 393224 | tf_op jit(solution)/shard_map/ppermute | solution.py:106
  61.0 1.6 %collective-permute-start.32 = (f32[256,128]{1,0:T(8,128)S(1)}, f32[256,128]{1,0:T(8,128)S(1)}, u32[]{:S(2)}, u32[]{:S(2)}) collective-permute-start(f32[256,128]{1,0:T(8,128)S(1)} %collective-permute-done.31.refs_2_), channel_id=1, source_target_pairs={{0,1},{1,0},{2,3},{3,2},{4,5},{5,4},{6,7},{7,6},{8,9},{9,8},{10,11... | collective-permute-start | bytes 393224 | tf_op jit(solution)/shard_map/ppermute | solution.py:106
  61.6 1.7 %collective-permute-start.34 = (f32[256,128]{1,0:T(8,128)S(1)}, f32[256,128]{1,0:T(8,128)S(1)}, u32[]{:S(2)}, u32[]{:S(2)}) collective-permute-start(f32[256,128]{1,0:T(8,128)S(1)} %collective-permute-done.33.refs_2_), channel_id=1, source_target_pairs={{0,1},{1,0},{2,3},{3,2},{4,5},{5,4},{6,7},{7,6},{8,9},{9,8},{10,11... | collective-permute-start | bytes 393224 | tf_op jit(solution)/shard_map/ppermute | solution.py:106
  62.1 1.6 %collective-permute-start.38 = (f32[256,128]{1,0:T(8,128)S(1)}, f32[256,128]{1,0:T(8,128)S(1)}, u32[]{:S(2)}, u32[]{:S(2)}) collective-permute-start(f32[256,128]{1,0:T(8,128)S(1)} %collective-permute-done.37.refs_2_), channel_id=1, source_target_pairs={{0,1},{1,0},{2,3},{3,2},{4,5},{5,4},{6,7},{7,6},{8,9},{9,8},{10,11... | collective-permute-start | bytes 393224 | tf_op jit(solution)/shard_map/ppermute | solution.py:106
  64.1 31.5 %collective-permute-start.41 = (f32[256,256]{1,0:T(8,128)S(1)}, f32[256,256]{1,0:T(8,128)S(1)}, u32[]{:S(2)}, u32[]{:S(2)}) collective-permute-start(f32[256,256]{1,0:T(8,128)S(1)} %pad_maximum_fusion.1.refs_1_), channel_id=1, source_target_pairs={{0,10},{1,11},{2,8},{3,9},{4,5},{5,4},{6,7},{7,6},{8,2},{9,3},{10,... | collective-permute-start | bytes 786440 | tf_op jit(solution)/shard_map/ppermute | solution.py:125
  87.4 13.3 %collective-permute-start.39 = (f32[256,256]{1,0:T(8,128)S(1)}, f32[256,256]{1,0:T(8,128)S(1)}, u32[]{:S(2)}, u32[]{:S(2)}) collective-permute-start(f32[256,256]{1,0:T(8,128)S(1)} %pad_maximum_fusion.1.refs_1_), channel_id=1, source_target_pairs={{16,10},{17,11},{18,8},{19,9}} | collective-permute-start | bytes 786440 | tf_op jit(solution)/shard_map/ppermute | solution.py:106
  88.7 12.0 %collective-permute-start.45 = (f32[256,256]{1,0:T(8,128)S(1)}, f32[256,256]{1,0:T(8,128)S(1)}, u32[]{:S(2)}, u32[]{:S(2)}) collective-permute-start(f32[256,256]{1,0:T(8,128)S(1)} %pad_maximum_fusion.1.refs_1_), channel_id=1, source_target_pairs={{0,8},{1,9},{2,10},{3,11},{4,5},{5,4},{6,7},{7,6},{8,0},{9,1},{10,... | collective-permute-start | bytes 786440 | tf_op jit(solution)/shard_map/ppermute | solution.py:125
  88.7 15.9 %collective-permute-start.43 = (f32[256,256]{1,0:T(8,128)S(1)}, f32[256,256]{1,0:T(8,128)S(1)}, u32[]{:S(2)}, u32[]{:S(2)}) collective-permute-start(f32[256,256]{1,0:T(8,128)S(1)} %pad_maximum_fusion.1.refs_1_), channel_id=1, source_target_pairs={{16,8},{17,9},{18,10},{19,11}} | collective-permute-start | bytes 786440 | tf_op jit(solution)/shard_map/ppermute | solution.py:106
  95.6 9.1 %collective-permute-start.42 = (f32[256,256]{1,0:T(8,128)S(1)}, f32[256,256]{1,0:T(8,128)S(1)}, u32[]{:S(2)}, u32[]{:S(2)}) collective-permute-start(f32[256,256]{1,0:T(8,128)S(1)} %collective-permute-done.41.refs_6_), channel_id=1, source_target_pairs={{0,1},{1,0},{2,3},{3,2},{4,5},{5,4},{6,7},{7,6},{8,9},{9,8},{10,11... | collective-permute-start | bytes 786440 | tf_op jit(solution)/shard_map/ppermute | solution.py:106
  100.6 4.0 %collective-permute-start.40 = (f32[256,256]{1,0:T(8,128)S(1)}, f32[256,256]{1,0:T(8,128)S(1)}, u32[]{:S(2)}, u32[]{:S(2)}) collective-permute-start(f32[256,256]{1,0:T(8,128)S(1)} %collective-permute-done.39.refs_3_), channel_id=1, source_target_pairs={{0,1},{1,0},{2,3},{3,2},{4,5},{5,4},{6,7},{7,6},{8,9},{9,8},{10,11... | collective-permute-start | bytes 786440 | tf_op jit(solution)/shard_map/ppermute | solution.py:106
  100.6 4.7 %collective-permute-start.46 = (f32[256,256]{1,0:T(8,128)S(1)}, f32[256,256]{1,0:T(8,128)S(1)}, u32[]{:S(2)}, u32[]{:S(2)}) collective-permute-start(f32[256,256]{1,0:T(8,128)S(1)} %collective-permute-done.45.refs_5_), channel_id=1, source_target_pairs={{0,1},{1,0},{2,3},{3,2},{4,5},{5,4},{6,7},{7,6},{8,9},{9,8},{10,11... | collective-permute-start | bytes 786440 | tf_op jit(solution)/shard_map/ppermute | solution.py:106
  106.8 9.3 %collective-permute-start.49 = (f32[256,256]{1,0:T(8,128)S(1)}, f32[256,256]{1,0:T(8,128)S(1)}, u32[]{:S(2)}, u32[]{:S(2)}) collective-permute-start(f32[256,256]{1,0:T(8,128)S(1)} %shard_map.54.refs_1_), channel_id=1, source_target_pairs={{0,26},{1,27},{2,24},{3,25},{4,30},{5,31},{6,28},{7,29},{8,2},{9,3... | collective-permute-start | bytes 786440 | tf_op jit(solution)/shard_map/ppermute | solution.py:106
  106.8 9.2 %collective-permute-start.47 = (f32[256,256]{1,0:T(8,128)S(1)}, f32[256,256]{1,0:T(8,128)S(1)}, u32[]{:S(2)}, u32[]{:S(2)}) collective-permute-start(f32[256,256]{1,0:T(8,128)S(1)} %shard_map.54.refs_1_), channel_id=1, source_target_pairs={{0,4},{1,5},{2,6},{3,7},{4,0},{5,1},{6,2},{7,3},{8,12},{9,13},{10,... | collective-permute-start | bytes 786440 | tf_op jit(solution)/shard_map/ppermute | solution.py:106
  116.1 7.5 %collective-permute-start.50 = (f32[256,256]{1,0:T(8,128)S(1)}, f32[256,256]{1,0:T(8,128)S(1)}, u32[]{:S(2)}, u32[]{:S(2)}) collective-permute-start(f32[256,256]{1,0:T(8,128)S(1)} %collective-permute-done.49), channel_id=1, source_target_pairs={{0,4},{1,5},{2,6},{3,7},{4,0},{5,1},{6,2},{7,3},{8,12},{9,13},{10,... | collective-permute-start | bytes 786440 | tf_op jit(solution)/shard_map/ppermute | solution.py:106
  116.1 7.5 %collective-permute-start.54 = (f32[256,256]{1,0:T(8,128)S(1)}, f32[256,256]{1,0:T(8,128)S(1)}, u32[]{:S(2)}, u32[]{:S(2)}) collective-permute-start(f32[256,256]{1,0:T(8,128)S(1)} %collective-permute-done.47.refs_3_), channel_id=1, source_target_pairs={{0,24},{1,25},{2,26},{3,27},{4,28},{5,29},{6,30},{7,31},{8,0},{9,1... | collective-permute-start | bytes 786440 | tf_op jit(solution)/shard_map/ppermute | solution.py:106
  116.2 7.8 %collective-permute-start.52 = (f32[256,256]{1,0:T(8,128)S(1)}, f32[256,256]{1,0:T(8,128)S(1)}, u32[]{:S(2)}, u32[]{:S(2)}) collective-permute-start(f32[256,256]{1,0:T(8,128)S(1)} %collective-permute-done.47.refs_3_), channel_id=1, source_target_pairs={{0,2},{1,3},{2,0},{3,1},{4,6},{5,7},{6,4},{7,5},{8,10},{9,11},{10,... | collective-permute-start | bytes 786440 | tf_op jit(solution)/shard_map/ppermute | solution.py:106
  117.5 6.7 %collective-permute-start.48 = (f32[256,256]{1,0:T(8,128)S(1)}, f32[256,256]{1,0:T(8,128)S(1)}, u32[]{:S(2)}, u32[]{:S(2)}) collective-permute-start(f32[256,256]{1,0:T(8,128)S(1)} %collective-permute-done.47.refs_3_), channel_id=1, source_target_pairs={{0,1},{1,0},{2,3},{3,2},{4,5},{5,4},{6,7},{7,6},{8,9},{9,8},{10,11... | collective-permute-start | bytes 786440 | tf_op jit(solution)/shard_map/ppermute | solution.py:106
  123.6 2.2 %collective-permute-start.55 = (f32[256,256]{1,0:T(8,128)S(1)}, f32[256,256]{1,0:T(8,128)S(1)}, u32[]{:S(2)}, u32[]{:S(2)}) collective-permute-start(f32[256,256]{1,0:T(8,128)S(1)} %collective-permute-done.54.refs_5_), channel_id=1, source_target_pairs={{0,1},{1,0},{2,3},{3,2},{4,5},{5,4},{6,7},{7,6},{8,9},{9,8},{10,11... | collective-permute-start | bytes 786440 | tf_op jit(solution)/shard_map/ppermute | solution.py:106
  124.1 1.8 %collective-permute-start.53 = (f32[256,256]{1,0:T(8,128)S(1)}, f32[256,256]{1,0:T(8,128)S(1)}, u32[]{:S(2)}, u32[]{:S(2)}) collective-permute-start(f32[256,256]{1,0:T(8,128)S(1)} %collective-permute-done.52.refs_2_), channel_id=1, source_target_pairs={{0,1},{1,0},{2,3},{3,2},{4,5},{5,4},{6,7},{7,6},{8,9},{9,8},{10,11... | collective-permute-start | bytes 786440 | tf_op jit(solution)/shard_map/ppermute | solution.py:106
  (11 other events, 28.9 us)
